TPU v7x, 256 devices: a whole 4x4x8 slice. The times are simulated.
256 devices in a mesh: expert: 4 (over x_lo, core), hidden: 64 (over y, x_hi, z).
Axes of the slice: x: 4 (x_hi: 2, x_lo: 2; x = x_hi * 2 + x_lo), y: 4, z: 8, core: 2. Of those that a mesh axis runs over, the one named last changes fastest.
Arguments:
- tokens: bfloat16 [512, 6144], P(('expert', 'hidden')), may hold values from -6 to 6
- routing: int32 [512, 2], P(('expert', 'hidden')), may hold values from 0 to 3, all different within a row; in each aligned block of 2 rows (0 to 1, 2 to 3, ...) at most 2 rows name the same one
- mix_weights: float32 [512, 2], P(('expert', 'hidden')), may hold values from 0.2 to 1
- gate_weight: bfloat16 [4, 6144, 16384], P('expert', None, 'hidden'), may hold values from -0.078125 to 0.078125
- up_weight: bfloat16 [4, 6144, 16384], P('expert', None, 'hidden'), may hold values from -0.078125 to 0.078125
- down_weight: bfloat16 [4, 16384, 6144], P('expert', 'hidden'), may hold values from -0.125 to 0.125
Outputs:
- mixed: bfloat16 [512, 6144], P(('expert', 'hidden'))
Inputs may be any that keep to these rules, and one draw needn't show every extreme that they name: `routing`: each row names two different experts. Within each aligned block of 2 rows (the tokens of one device) no expert is named by more than 2 entries, and in every draw some expert is named by exactly 2 entries of some block.
All inputs are finite; a program needn't handle non-finite values.
Results may differ from a plain program's by a relative error of at most 0.0058.
Values may be sent and summed in bfloat16 or wider, within the bound.
No kernel may reach another device: no remote copies, remote signals or barrier semaphores. Data moves between devices by JAX's collectives and lax.ppermute only.
A program may use at most 128 MiB of HBM per device.

v0:
```python
import jax
import jax.numpy as jnp
from jax import lax
from jax.sharding import PartitionSpec as P

CAP = 2


def shards(tokens, routing, mix_weights, gate_weight, up_weight, down_weight):
    tok_rows = tokens.shape[0]
    model_width = tokens.shape[1]
    n_expert = lax.axis_size("expert")
    n_hidden = lax.axis_size("hidden")
    entries = routing.reshape(-1)
    one_hot = (entries[:, None] == jnp.arange(n_expert, dtype=jnp.int32)[None, :]).astype(jnp.int32)
    positions = jnp.arange(2 * tok_rows, dtype=jnp.int32)
    before = (positions[None, :] < positions[:, None]).astype(jnp.int32)
    earlier = jnp.sum(before[:, :, None] * one_hot[None, :, :], axis=1)
    slot_ids = jnp.sum(earlier * one_hot, axis=1)
    places = entries * CAP + slot_ids
    send_rows = n_expert * CAP
    row_ids = jnp.arange(send_rows, dtype=jnp.int32)
    place_pairs = places.reshape(tok_rows, 2)
    select = jnp.any(row_ids[:, None, None] == place_pairs[None, :, :], axis=2).astype(jnp.bfloat16)
    outgoing = jnp.dot(select, tokens, preferred_element_type=jnp.float32).astype(jnp.bfloat16)
    arrived = lax.all_to_all(outgoing, "expert", split_axis=0, concat_axis=0, tiled=True)
    w_gate = gate_weight[0]
    w_up = up_weight[0]
    w_down = down_weight[0]
    block_rows = lax.all_gather(arrived, "hidden", axis=0, tiled=True)
    gate_out = jnp.dot(block_rows, w_gate, preferred_element_type=jnp.float32)
    up_out = jnp.dot(block_rows, w_up, preferred_element_type=jnp.float32)
    hidden = (jax.nn.silu(gate_out) * up_out).astype(jnp.bfloat16)
    terms = jnp.dot(hidden, w_down, preferred_element_type=jnp.float32)
    by_row = terms.reshape(n_hidden, send_rows, model_width)
    received = lax.all_to_all(by_row, "hidden", split_axis=0, concat_axis=0, tiled=True)
    finished = jnp.sum(received, axis=0).astype(jnp.bfloat16)
    returned = lax.all_to_all(finished, "expert", split_axis=0, concat_axis=0, tiled=True)
    chooser = (places[:, None] == row_ids[None, :]).astype(jnp.bfloat16)
    picked = jnp.dot(chooser, returned, preferred_element_type=jnp.float32).reshape(
        tok_rows, 2, model_width
    )
    return jnp.sum(mix_weights[:, :, None] * picked, axis=1).astype(jnp.bfloat16)


def solution(mesh):
    in_specs = (
        P(("expert", "hidden"), None),
        P(("expert", "hidden"), None),
        P(("expert", "hidden"), None),
        P("expert", None, "hidden"),
        P("expert", None, "hidden"),
        P("expert", "hidden", None),
    )
    out_specs = P(("expert", "hidden"), None)
    return jax.shard_map(shards, mesh=mesh, in_specs=in_specs, out_specs=out_specs, check_vma=False)
```

profile of v0, /device:TPU:1, one launch (start us, length us, event | category | flops | bytes accessed | tf_op | source)
XLA Modules:
  0.0 481.6 jit_solution(17980004571483616409)
XLA Ops:
  6.5 0.0 copy-start
  6.5 0.0 all-gather.2.cloned.1.call-start
  6.5 0.9 eq.59
  7.4 0.1 fusion.27
  7.5 0.1 multiply_reduce_fusion
  7.6 0.2 select_reduce_fusion
  7.8 0.1 reduce_sum.40
  7.9 0.7 multiply_add_fusion
  8.6 0.1 compare_reduce_fusion
  8.7 1.0 convolution_convert_fusion
  9.6 0.1 all_to_all.17
  9.7 8.9 %all_to_all.26 = bf16[4,2,6144]{2,1,0:T(2,128)(2,1)S(1)} all-to-all(bf16[4,2,6144]{2,1,0:T(2,128)(2,1)S(1)} %all_to_all.17), channel_id=1, replica_groups=mesh['expert'=4,'hidden'=64] {'expert'}, dimensions={0} | all-to-all | bytes 196608 | tf_op jit(solution)/shard_map/all_to_all | solution.py:26
  18.6 0.7 all_to_all.19
  19.3 0.0 all-gather.2.cloned.1.call-update
  19.3 135.9 %all-gather.2.cloned.1.call-done = bf16[512,6144]{1,0:T(8,128)(2,1)} async-done(((bf16[8,6144]{1,0:T(8,128)(2,1)}), bf16[512,6144]{1,0:T(8,128)(2,1)}) %all-gather.2.cloned.1.call-update) | async-done | bytes 6291472 | tf_op jit(solution)/shard_map/all_gather | solution.py:30
  155.2 6.3 %fusion.4 = f32[512,256]{1,0:T(8,128)} fusion(bf16[512,6144]{1,0:T(8,128)(2,1)} %all-gather.2.cloned.1.call-done, bf16[1,6144,256]{2,1,0:T(8,128)(2,1)} %param.9), kind=kOutput, calls=%fused_computation.6 | convolution fusion | flops 1610612736 | bytes 9961472 | tf_op jit(solution)/shard_map/dot_general | solution.py:31
  161.5 0.0 copy-done
  161.5 15.0 %fusion = f32[64,8,6144]{2,1,0:T(8,128)} fusion(bf16[1,256,6144]{2,1,0:T(8,128)(2,1)S(1)} %copy-done, bf16[512,6144]{1,0:T(8,128)(2,1)} %all-gather.2.cloned.1.call-done, bf16[1,6144,256]{2,1,0:T(8,128)(2,1)} %param.10, f32[512,256]{1,0:T(8,128)} %fusion.4), kind=kOutput, calls=%fused_computation.2 | convolution fusion | flops 3222011904 | bytes 25690112 | tf_op jit(solution)/shard_map/dot_general | solution.py:34
  176.4 278.9 %all_to_all.27 = f32[64,8,6144]{2,1,0:T(8,128)} all-to-all(f32[64,8,6144]{2,1,0:T(8,128)} %fusion), channel_id=1, replica_groups=mesh['expert'=4,'hidden'=64] {'hidden'}, dimensions={0} | all-to-all | bytes 25165824 | tf_op jit(solution)/shard_map/all_to_all | solution.py:36
  455.3 0.0 copy-start.1
  455.3 5.2 %reduce_sum.41 = bf16[8,6144]{1,0:T(8,128)(2,1)S(1)} reduce(f32[64,8,6144]{2,1,0:T(8,128)} %all_to_all.27, f32[]{:T(128)} %constant.11.clone.1), dimensions={0}, to_apply=%region_3.4 | reduce | flops 3096576 | bytes 12681220 | tf_op jit(solution)/shard_map/reduce_sum | solution.py:37
  460.5 0.1 convert_element_type.37
  460.6 13.1 %all_to_all.28 = bf16[4,2,6144]{2,1,0:T(2,128)(2,1)S(1)} all-to-all(bf16[4,2,6144]{2,1,0:T(2,128)(2,1)S(1)} %convert_element_type.37), channel_id=1, replica_groups=mesh['expert'=4,'hidden'=64] {'expert'}, dimensions={0} | all-to-all | bytes 196608 | tf_op jit(solution)/shard_map/all_to_all | solution.py:38
  473.7 0.0 copy-done.1
  473.7 1.0 fusion.17
  (1 shorter events, 0.0 us)
Async XLA Ops:
  6.5 154.9 %copy-start = (bf16[1,256,6144]{2,1,0:T(8,128)(2,1)S(1)}, bf16[1,256,6144]{2,1,0:T(8,128)(2,1)}, u32[]{:S(2)}) copy-start(bf16[1,256,6144]{2,1,0:T(8,128)(2,1)} %param.11) | copy-start | bytes 9437188
  6.5 148.7 %all-gather.2.cloned.1.call-start = ((), (), s32[]{:S(2)}) async-start(), calls=%async_computation.3 | async-start | bytes 6389760 | tf_op jit(solution)/shard_map/all_gather | solution.py:30
  455.3 18.4 %copy-start.1 = (f32[2,2]{1,0:T(2,128)S(1)}, f32[2,2]{1,0:T(2,128)}, u32[]{:S(2)}) copy-start(f32[2,2]{1,0:T(2,128)} %param.8) | copy-start | bytes 52
Sparse Core Ops, SparseCore 0:
  19.4 135.7 all-gather.1
where the time goes:
time: 482 us
  blocking collectives  301 us (62%)
  waiting for transfers between devices  136 us (28%)
  matrix products  23.2 us (5%)
  between operations  13.4 us (3%)
  other arithmetic  6.29 us (1%)
    all_to_all x1, blocking collectives, shards(): lax.all_to_all(by_row, 'hidden', split_axis=0, concat_axis=0, tiled=True)  279 us
    all_gather x1, waiting for transfers between devices, shards(): block_rows = lax.all_gather(arrived, 'hidden', axis=0, tiled=True)  136 us
    dot_general x1, matrix products, shards(): terms = jnp.dot(hidden, w_down, preferred_element_type=jnp.float32)  15 us
    all_to_all x1, blocking collectives, shards(): lax.all_to_all(finished, 'expert', split_axis=0, concat_axis=0, tiled=True)  13.1 us
  transfers between devices with their start and end apart: 1, of which 1 were waited for; matrix products, arithmetic and copies ran while one was open for 0% of the time, Pallas kernels for 0%

commit v1 on v0

v1 whole, which is shorter than its diff:
```python
import jax
import jax.numpy as jnp
from jax import lax
from jax.sharding import Mesh
from jax.sharding import PartitionSpec as P

AXES = ("xl", "c", "y", "xh", "z")
SIZES = (2, 2, 4, 2, 8)
RING = 4
PAD = 128


def flat(xl, c, y, xh, z):
    return (((xl * 2 + c) * 4 + y) * 2 + xh) * 8 + z


def ring_perm(first, step):
    pairs = []
    for c in range(2):
        along_x = (c == 0) == first
        for x in range(4):
            for y in range(4):
                for z in range(8):
                    tx, ty = ((x + step) % 4, y) if along_x else (x, (y + step) % 4)
                    pairs.append((flat(x % 2, c, y, x // 2, z), flat(tx % 2, c, ty, tx // 2, z)))
    return pairs


def move(v, first, step):
    return lax.ppermute(v, AXES, ring_perm(first, step))


def swap(v):
    return lax.ppermute(v, "c", [(0, 1), (1, 0)])


def ring_gather(block, first):
    half = block.shape[0] // 2
    one, two = block[:half], block[half:]
    from_left_one = move(one, first, 1)
    from_right_two = move(two, first, -1)
    from_left_two = move(two, first, 1)
    from_right_one = move(one, first, -1)
    far_one = move(from_left_one, first, 1)
    far_two = move(from_right_two, first, -1)
    return [one, two, from_right_one, from_right_two, far_one, far_two, from_left_one, from_left_two]


def add(*terms):
    total = terms[0].astype(jnp.float32)
    for term in terms[1:]:
        total = total + term.astype(jnp.float32)
    return total


def ring_reduce(blocks, first):
    own, right, far, left = blocks
    half = own.shape[0] // 2
    to_right = move(far[:half], first, 1)
    to_left = move(far[half:], first, -1)
    right_two = move(right[half:], first, 1)
    left_one = move(left[:half], first, -1)
    right_one = move(add(right[:half], to_right).astype(jnp.bfloat16), first, 1)
    left_two = move(add(left[half:], to_left).astype(jnp.bfloat16), first, -1)
    one = add(own[:half], right_one, left_one)
    two = add(own[half:], right_two, left_two)
    return jnp.concatenate([one, two], axis=0)


def parts(w):
    high = lax.reduce_precision(w, 8, 7)
    mid = lax.reduce_precision(w - high, 8, 7)
    low = w - high - mid
    return jnp.concatenate([high, mid, low], axis=1).astype(jnp.bfloat16)


def shards(tokens, routing, mix_weights, gate_weight, up_weight, down_weight):
    tok_rows, width = tokens.shape
    half = width // 2
    core = lax.axis_index("c")
    expert = lax.axis_index("xl") * 2 + core
    experts = jnp.arange(4, dtype=jnp.int32)
    chosen = routing[:, :, None] == experts[None, None, :]
    share = jnp.sum(jnp.where(chosen, mix_weights[:, :, None], 0.0), axis=1)
    extra = jnp.pad(parts(share), ((0, 0), (0, PAD - 12)))
    sides = [jnp.concatenate([tokens[:, i * half:(i + 1) * half], extra], axis=1) for i in range(2)]
    outgoing = jnp.stack([sides[0]] * 8 + [sides[1]] * 8, axis=0)
    tile = lax.all_to_all(outgoing, ("c", "z"), split_axis=0, concat_axis=0, tiled=True)
    tile = tile.reshape(16 * tok_rows, half + PAD)
    rows = tile.shape[0]
    quarter = jnp.concatenate(ring_gather(tile, True), axis=0)
    quarter = quarter.reshape(RING, rows, half + PAD)
    pieces = ring_gather(quarter, False)
    mine = jnp.concatenate(pieces, axis=0)
    other = swap(mine)

    def halves(w, axis):
        own = lax.dynamic_slice_in_dim(w, core * half, half, axis)
        rest = lax.dynamic_slice_in_dim(w, (1 - core) * half, half, axis)
        return own, rest

    w_in = jnp.concatenate([gate_weight[0], up_weight[0]], axis=1)
    in_own, in_rest = [jnp.pad(w, ((0, PAD), (0, 0))) for w in halves(w_in, 0)]
    down_own, down_rest = halves(down_weight[0], 1)
    n = RING * RING * rows
    units = gate_weight.shape[2]

    def turned(v):
        return v.reshape(RING, RING, rows, v.shape[-1]).swapaxes(0, 1).reshape(n, v.shape[-1])

    mine = mine.reshape(n, half + PAD)
    other = other.reshape(n, half + PAD)
    act = jnp.dot(mine, in_own, preferred_element_type=jnp.float32)
    act = act + turned(jnp.dot(other, in_rest, preferred_element_type=jnp.float32))
    hidden = (jax.nn.silu(act[:, :units]) * act[:, units:]).astype(jnp.bfloat16)
    hidden_rest = turned(hidden)

    lane = jnp.arange(PAD, dtype=jnp.int32)
    mask = (lane % 4 == expert) & (lane < 12)

    def scale_of(v):
        return jnp.sum(jnp.where(mask[None, :], v[:, half:].astype(jnp.float32), 0.0), axis=1, keepdims=True)

    scale_own, scale_rest = scale_of(mine), scale_of(other)
    per = n // RING
    blocks = [None] * RING
    for d in (2, 1, 3, 0):
        span = slice(d * per, (d + 1) * per)
        rest = jnp.dot(hidden_rest[span], down_rest, preferred_element_type=jnp.float32) * scale_rest[span]
        came = swap(rest.astype(jnp.bfloat16))
        own = jnp.dot(hidden[span], down_own, preferred_element_type=jnp.float32) * scale_own[span]
        blocks[d] = add(own, came).astype(jnp.bfloat16).reshape(RING, rows, half)
    summed = ring_reduce(blocks, False).astype(jnp.bfloat16)
    last = ring_reduce([summed[d] for d in range(RING)], True)
    back = lax.all_to_all(last.reshape(16, tok_rows, half), ("c", "z"), split_axis=0, concat_axis=0, tiled=True)
    total = jnp.sum(back.reshape(2, 8, tok_rows, half), axis=1)
    return jnp.concatenate([total[0], total[1]], axis=1).astype(jnp.bfloat16)


def solution(mesh):
    fine = Mesh(mesh.devices.reshape(SIZES), AXES)
    expert, hidden = ("xl", "c"), ("y", "xh", "z")
    in_specs = (
        P(AXES, None),
        P(AXES, None),
        P(AXES, None),
        P(expert, None, hidden),
        P(expert, None, hidden),
        P(expert, hidden, None),
    )
    return jax.shard_map(shards, mesh=fine, in_specs=in_specs, out_specs=P(AXES, None), check_vma=False)
```

time: 482 us -> 132 us (0.27)
  blocking collectives: 301 us -> 39.6 us
  waiting for transfers between devices: 136 us -> 27.4 us
  starting transfers between devices: 0.01 us -> 37.3 us
  between operations: 13.4 us -> 0.4 us
  matrix products: 23.2 us -> 10.7 us
  local copies, waits for them, and re-layouts: 1.87 us -> 8.65 us
    all_to_all x3 -> x2, blocking collectives: 301 us -> 39.6 us  [the longest x1 21.4 us: shards(): lax.all_to_all(last.reshape(16, tok_rows, half), ('c', 'z'), split_axis=0...]
    all_gather x1 -> x0, waiting for transfers between devices: 136 us -> none  [shards(): block_rows = lax.all_gather(arrived, 'hidden', axis=0, tiled=True)]
    ppermute x0 -> x29, starting transfers between devices: none -> 37.3 us  [the longest x24 30.8 us: move(): return lax.ppermute(v, AXES, ring_perm(first, step))]
    ppermute x0 -> x29, waiting for transfers between devices: none -> 27.4 us  [the longest x24 23.3 us: move(): return lax.ppermute(v, AXES, ring_perm(first, step))]
    dot_general x4 -> x10, matrix products: 23.2 us -> 10.7 us  [the longest x1 3.76 us: shards(): act = jnp.dot(mine, in_own, preferred_element_type=jnp.float32)]
    unnamed x4 -> x9, local copies, waits for them, and re-layouts: 0.01 us -> 5.51 us
  transfers between devices with their start and end apart: 1 -> 29, of which waited for: 1 -> 12; matrix products, arithmetic and copies ran while one was open for 0% -> 9% of each run, Pallas kernels for 0% -> 0%
where the time goes in v1:
time: 132 us; the launch traced here: 131 us
  blocking collectives  39.6 us (30%)
  starting transfers between devices  37.3 us (28%)
  waiting for transfers between devices  27.4 us (21%)
  matrix products  10.7 us (8%)
  local copies, waits for them, and re-layouts  8.65 us (7%)
  other arithmetic  7.11 us (5%)
    ppermute x24, starting transfers between devices, move(): return lax.ppermute(v, AXES, ring_perm(first, step))  30.8 us
    ppermute x24, waiting for transfers between devices, move(): return lax.ppermute(v, AXES, ring_perm(first, step))  23.3 us
    all_to_all x1, blocking collectives, shards(): lax.all_to_all(last.reshape(16, tok_rows, half), ('c', 'z'), split_axis=0...  21.4 us
    all_to_all x1, blocking collectives, shards(): lax.all_to_all(outgoing, ('c', 'z'), split_axis=0, concat_axis=0, tiled=T...  18.2 us
    ppermute x5, starting transfers between devices, swap(): return lax.ppermute(v, 'c', [(0, 1), (1, 0)])  6.54 us
    unnamed x9, local copies, waits for them, and re-layouts  5.51 us
    ppermute x5, waiting for transfers between devices, swap(): return lax.ppermute(v, 'c', [(0, 1), (1, 0)])  4.14 us
    dot_general x1, matrix products, shards(): act = jnp.dot(mine, in_own, preferred_element_type=jnp.float32)  3.76 us
  transfers between devices with their start and end apart: 29, of which 12 were waited for; matrix products, arithmetic and copies ran while one was open for 9% of the time, Pallas kernels for 0%

profile of v1, /device:TPU:1, one launch (start us, length us, event | category | flops | bytes accessed | tf_op | source)
XLA Modules:
  0.0 131.2 jit_solution(15755099680701252958)
XLA Ops:
  0.0 0.9 fusion.58
  0.9 0.8 fusion.81
  2.2 18.2 %all_to_all.10 = bf16[16,2,3200]{2,1,0:T(2,128)(2,1)S(1)} all-to-all(bf16[16,2,3200]{2,1,0:T(2,128)(2,1)S(1)} %constant_dynamic-update-slice_fusion), channel_id=1, replica_groups=mesh['xl'=2,'c'=2,'y'=4,'xh'=2,'z'=8] {'c','z'}, dimensions={0} | all-to-all | bytes 409600 | tf_op jit(solution)/shard_map/all_to_all | solution.py:88
  20.6 2.8 %collective-permute-start.1 = (bf16[16,3200]{1,0:T(8,128)(2,1)S(1)}, bf16[16,3200]{1,0:T(8,128)(2,1)S(1)}, u32[]{:S(2)}, u32[]{:S(2)}) collective-permute-start(bf16[16,3200]{1,0:T(8,128)(2,1)S(1)} %slice.221), channel_id=1, source_target_pairs={{0,136},{1,137},{2,138},{3,139},{4,140},{5,141},{6,142},{7,143},{1... | collective-permute-start | bytes 307208 | tf_op jit(solution)/shard_map/ppermute | solution.py:30
  23.4 0.5 collective-permute-start
  24.0 1.0 collective-permute-start.5
  25.1 3.0 %collective-permute-start.4 = (bf16[16,3200]{1,0:T(8,128)(2,1)S(1)}, bf16[16,3200]{1,0:T(8,128)(2,1)S(1)}, u32[]{:S(2)}, u32[]{:S(2)}) collective-permute-start(bf16[16,3200]{1,0:T(8,128)(2,1)S(1)} %collective-permute-done.1), channel_id=1, source_target_pairs={{0,136},{1,137},{2,138},{3,139},{4,140},{5,141},{6,142},{7,143},{1... | collective-permute-start | bytes 307208 | tf_op jit(solution)/shard_map/ppermute | solution.py:30
  28.1 1.9 %collective-permute-done.2 = bf16[16,3200]{1,0:T(8,128)(2,1)S(1)} collective-permute-done((bf16[16,3200]{1,0:T(8,128)(2,1)S(1)}, bf16[16,3200]{1,0:T(8,128)(2,1)S(1)}, u32[]{:S(2)}, u32[]{:S(2)}) %collective-permute-start.2) | collective-permute-done | bytes 102432 | tf_op jit(solution)/shard_map/ppermute | solution.py:30
  30.1 0.8 constant_dynamic-update-slice_fusion.23
  30.9 2.2 %collective-permute-start.6 = (bf16[2,32,3200]{2,1,0:T(8,128)(2,1)S(1)}, bf16[2,32,3200]{2,1,0:T(8,128)(2,1)S(1)}, u32[]{:S(2)}, u32[]{:S(2)}) collective-permute-start(bf16[2,32,3200]{2,1,0:T(8,128)(2,1)S(1)} %bitcast.145), channel_id=1, source_target_pairs={{0,48},{1,49},{2,50},{3,51},{4,52},{5,53},{6,54},{7,55},{16,0},{17... | collective-permute-start | bytes 1228808 | tf_op jit(solution)/shard_map/ppermute | solution.py:30
  33.1 1.8 %collective-permute-done.3 = bf16[16,3200]{1,0:T(8,128)(2,1)S(1)} collective-permute-done((bf16[16,3200]{1,0:T(8,128)(2,1)S(1)}, bf16[16,3200]{1,0:T(8,128)(2,1)S(1)}, u32[]{:S(2)}, u32[]{:S(2)}) %collective-permute-start.3) | collective-permute-done | bytes 102432 | tf_op jit(solution)/shard_map/ppermute | solution.py:30
  34.8 2.3 %collective-permute-start.7 = (bf16[2,32,3200]{2,1,0:T(8,128)(2,1)S(1)}, bf16[2,32,3200]{2,1,0:T(8,128)(2,1)S(1)}, u32[]{:S(2)}, u32[]{:S(2)}) collective-permute-start(bf16[2,32,3200]{2,1,0:T(8,128)(2,1)S(1)} %bitcast.141), channel_id=1, source_target_pairs={{0,48},{1,49},{2,50},{3,51},{4,52},{5,53},{6,54},{7,55},{16,0},{17... | collective-permute-start | bytes 1228808 | tf_op jit(solution)/shard_map/ppermute | solution.py:30
  37.1 0.8 constant_dynamic-update-slice_fusion.22
  37.9 4.4 %collective-permute-done.8 = bf16[2,32,3200]{2,1,0:T(8,128)(2,1)S(1)} collective-permute-done((bf16[2,32,3200]{2,1,0:T(8,128)(2,1)S(1)}, bf16[2,32,3200]{2,1,0:T(8,128)(2,1)S(1)}, u32[]{:S(2)}, u32[]{:S(2)}) %collective-permute-start.8) | collective-permute-done | bytes 409632 | tf_op jit(solution)/shard_map/ppermute | solution.py:30
  42.3 0.8 constant_dynamic-update-slice_fusion.21
  43.1 2.7 %collective-permute-start.10 = (bf16[2,32,3200]{2,1,0:T(8,128)(2,1)S(1)}, bf16[2,32,3200]{2,1,0:T(8,128)(2,1)S(1)}, u32[]{:S(2)}, u32[]{:S(2)}) collective-permute-start(bf16[2,32,3200]{2,1,0:T(8,128)(2,1)S(1)} %collective-permute-done.7), channel_id=1, source_target_pairs={{0,48},{1,49},{2,50},{3,51},{4,52},{5,53},{6,54},{7,55},{16,0},{17... | collective-permute-start | bytes 1228808 | tf_op jit(solution)/shard_map/ppermute | solution.py:30
  45.8 0.8 constant_dynamic-update-slice_fusion.20
  46.5 4.5 %collective-permute-done.9 = bf16[2,32,3200]{2,1,0:T(8,128)(2,1)S(1)} collective-permute-done((bf16[2,32,3200]{2,1,0:T(8,128)(2,1)S(1)}, bf16[2,32,3200]{2,1,0:T(8,128)(2,1)S(1)}, u32[]{:S(2)}, u32[]{:S(2)}) %collective-permute-start.9) | collective-permute-done | bytes 409632 | tf_op jit(solution)/shard_map/ppermute | solution.py:30
  51.0 0.8 constant_dynamic-update-slice_fusion.19
  51.8 0.8 constant_dynamic-update-slice_fusion.18
  52.6 0.8 constant_dynamic-update-slice_fusion.17
  53.4 0.8 constant_dynamic-update-slice_fusion.16
  54.2 5.2 %collective-permute-start.12 = (bf16[16,32,3200]{2,1,0:T(8,128)(2,1)}, bf16[16,32,3200]{2,1,0:T(8,128)(2,1)}, u32[]{:S(2)}, u32[]{:S(2)}) collective-permute-start(bf16[16,32,3200]{2,1,0:T(8,128)(2,1)} %constant_dynamic-update-slice_fusion.16), channel_id=1, source_target_pairs={{0,64},{64,0},{1,65},{65,1},{2,66},{66,2},{3,67},{67,3},{4,68},{68... | collective-permute-start | bytes 9830408 | tf_op jit(solution)/shard_map/ppermute | solution.py:34
  59.4 3.0 %fusion.10 = (bf16[3072,512]{1,0:T(8,128)(2,1)S(1)}, bf16[3072,512]{1,0:T(8,128)(2,1)S(1)}) fusion(s32[]{:T(128)S(6)} %select_n.31, bf16[6144,256]{1,0:T(8,128)(2,1)} %bitcast.138, bf16[6144,256]{1,0:T(8,128)(2,1)} %bitcast.139, s32[]{:T(128)S(6)} %select_n.32), kind=kLoop, calls=%fused_computation.22 | loop fusion | flops 12582912 | bytes 12582920 | tf_op jit(solution)/shard_map/concatenate | solution.py:102
  62.4 2.8 %collective-permute-done.12 = bf16[16,32,3200]{2,1,0:T(8,128)(2,1)} collective-permute-done((bf16[16,32,3200]{2,1,0:T(8,128)(2,1)}, bf16[16,32,3200]{2,1,0:T(8,128)(2,1)}, u32[]{:S(2)}, u32[]{:S(2)}) %collective-permute-start.12) | collective-permute-done | bytes 3276832 | tf_op jit(solution)/shard_map/ppermute | solution.py:34
  65.2 3.8 %fusion.19 = f32[4,4,32,512]{3,2,0,1:T(8,128)S(1)} fusion(bf16[4,4,32,3200]{3,2,1,0:T(8,128)(2,1)} %bitcast.7, bf16[3072,512]{1,0:T(8,128)(2,1)S(1)} %get-tuple-element.8), kind=kOutput, calls=%fused_computation.35 | convolution fusion | flops 1677721600 | bytes 7471104 | tf_op jit(solution)/shard_map/dot_general | solution.py:114
  69.1 3.8 %fusion.22 = f32[512,512]{1,0:T(8,128)S(1)} fusion(f32[512,512]{1,0:T(8,128)S(1)} %bitcast.151, bf16[512,3200]{1,0:T(8,128)(2,1)} %bitcast.4, bf16[3072,512]{1,0:T(8,128)(2,1)S(1)} %get-tuple-element.7), kind=kOutput, calls=%fused_computation.36 | convolution fusion | flops 1677983744 | bytes 8519680 | tf_op jit(solution)/shard_map/dot_general | solution.py:113
  73.0 1.1 select_reduce_fusion.1
  74.6 0.5 collective-permute-start.15
  76.0 0.5 collective-permute-start.18
  77.1 0.4 add_convert_fusion.1
  77.6 1.3 %collective-permute-start.21 = (bf16[2,32,3072]{2,1,0:T(8,128)(2,1)S(1)}, bf16[2,32,3072]{2,1,0:T(8,128)(2,1)S(1)}, u32[]{:S(2)}, u32[]{:S(2)}) collective-permute-start(bf16[2,32,3072]{2,1,0:T(8,128)(2,1)S(1)} %bitcast.155), channel_id=1, source_target_pairs={{0,48},{1,49},{2,50},{3,51},{4,52},{5,53},{6,54},{7,55},{16,0},{17... | collective-permute-start | bytes 1179656 | tf_op jit(solution)/shard_map/ppermute | solution.py:30
  78.9 1.4 %collective-permute-done.14 = bf16[128,3072]{1,0:T(8,128)(2,1)S(1)} collective-permute-done((bf16[128,3072]{1,0:T(8,128)(2,1)S(1)}, bf16[128,3072]{1,0:T(8,128)(2,1)S(1)}, u32[]{:S(2)}, u32[]{:S(2)}) %collective-permute-start.14) | collective-permute-done | bytes 786464 | tf_op jit(solution)/shard_map/ppermute | solution.py:34
  80.3 0.4 add_convert_fusion.2
  80.9 0.4 add_convert_fusion
  81.4 2.7 %collective-permute-start.19 = (bf16[2,32,3072]{2,1,0:T(8,128)(2,1)S(1)}, bf16[2,32,3072]{2,1,0:T(8,128)(2,1)S(1)}, u32[]{:S(2)}, u32[]{:S(2)}) collective-permute-start(bf16[2,32,3072]{2,1,0:T(8,128)(2,1)S(1)} %bitcast.152), channel_id=1, source_target_pairs={{0,48},{1,49},{2,50},{3,51},{4,52},{5,53},{6,54},{7,55},{16,0},{17... | collective-permute-start | bytes 1179656 | tf_op jit(solution)/shard_map/ppermute | solution.py:30
  84.7 3.0 %collective-permute-start.22 = (bf16[2,32,3072]{2,1,0:T(8,128)(2,1)S(1)}, bf16[2,32,3072]{2,1,0:T(8,128)(2,1)S(1)}, u32[]{:S(2)}, u32[]{:S(2)}) collective-permute-start(bf16[2,32,3072]{2,1,0:T(8,128)(2,1)S(1)} %fusion.41), channel_id=1, source_target_pairs={{0,48},{1,49},{2,50},{3,51},{4,52},{5,53},{6,54},{7,55},{16,0},{17... | collective-permute-start | bytes 1179656 | tf_op jit(solution)/shard_map/ppermute | solution.py:30
  87.7 5.5 %collective-permute-done.16 = bf16[2,32,3072]{2,1,0:T(8,128)(2,1)S(1)} collective-permute-done((bf16[2,32,3072]{2,1,0:T(8,128)(2,1)S(1)}, bf16[2,32,3072]{2,1,0:T(8,128)(2,1)S(1)}, u32[]{:S(2)}, u32[]{:S(2)}) %collective-permute-start.16) | collective-permute-done | bytes 393248 | tf_op jit(solution)/shard_map/ppermute | solution.py:30
  93.6 3.5 %collective-permute-start.25 = (bf16[16,3072]{1,0:T(8,128)(2,1)S(1)}, bf16[16,3072]{1,0:T(8,128)(2,1)S(1)}, u32[]{:S(2)}, u32[]{:S(2)}) collective-permute-start(bf16[16,3072]{1,0:T(8,128)(2,1)S(1)} %get-tuple-element.21), channel_id=1, source_target_pairs={{0,136},{1,137},{2,138},{3,139},{4,140},{5,141},{6,142},{7,143},{1... | collective-permute-start | bytes 294920 | tf_op jit(solution)/shard_map/ppermute | solution.py:30
  97.1 2.7 %collective-permute-start.27 = (bf16[16,3072]{1,0:T(8,128)(2,1)S(1)}, bf16[16,3072]{1,0:T(8,128)(2,1)S(1)}, u32[]{:S(2)}, u32[]{:S(2)}) collective-permute-start(bf16[16,3072]{1,0:T(8,128)(2,1)S(1)} %get-tuple-element.20), channel_id=1, source_target_pairs={{0,136},{1,137},{2,138},{3,139},{4,140},{5,141},{6,142},{7,143},{1... | collective-permute-start | bytes 294920 | tf_op jit(solution)/shard_map/ppermute | solution.py:30
  99.8 1.8 %collective-permute-done.17 = bf16[2,32,3072]{2,1,0:T(8,128)(2,1)S(1)} collective-permute-done((bf16[2,32,3072]{2,1,0:T(8,128)(2,1)S(1)}, bf16[2,32,3072]{2,1,0:T(8,128)(2,1)S(1)}, u32[]{:S(2)}, u32[]{:S(2)}) %collective-permute-start.17) | collective-permute-done | bytes 393248 | tf_op jit(solution)/shard_map/ppermute | solution.py:30
  101.8 1.3 %collective-permute-done.23 = bf16[16,3072]{1,0:T(8,128)(2,1)S(1)} collective-permute-done((bf16[16,3072]{1,0:T(8,128)(2,1)S(1)}, bf16[16,3072]{1,0:T(8,128)(2,1)S(1)}, u32[]{:S(2)}, u32[]{:S(2)}) %collective-permute-start.23) | collective-permute-done | bytes 98336 | tf_op jit(solution)/shard_map/ppermute | solution.py:30
  103.3 2.7 %collective-permute-start.28 = (bf16[16,3072]{1,0:T(8,128)(2,1)S(1)}, bf16[16,3072]{1,0:T(8,128)(2,1)S(1)}, u32[]{:S(2)}, u32[]{:S(2)}) collective-permute-start(bf16[16,3072]{1,0:T(8,128)(2,1)S(1)} %fusion.48), channel_id=1, source_target_pairs={{0,136},{1,137},{2,138},{3,139},{4,140},{5,141},{6,142},{7,143},{1... | collective-permute-start | bytes 294920 | tf_op jit(solution)/shard_map/ppermute | solution.py:30
  106.0 0.9 collective-permute-done.26
  106.9 1.1 collective-permute-done.24
  108.1 1.0 reshape.105
  109.1 21.4 %all_to_all.11 = f32[16,2,3072]{2,1,0:T(2,128)S(1)} all-to-all(f32[16,2,3072]{2,1,0:T(2,128)} %reshape.105), channel_id=1, replica_groups=mesh['xl'=2,'c'=2,'y'=4,'xh'=2,'z'=8] {'c','z'}, dimensions={0} | all-to-all | bytes 786432 | tf_op jit(solution)/shard_map/all_to_all | solution.py:135
  130.6 0.6 pad_maximum_fusion.3
  (83 shorter events, 4.9 us)
Async XLA Ops:
  0.0 74.2 %copy-start = (bf16[1,256,6144]{2,1,0:T(8,128)(2,1)S(1)}, bf16[1,256,6144]{2,1,0:T(8,128)(2,1)}, u32[]{:S(2)}) copy-start(bf16[1,256,6144]{2,1,0:T(8,128)(2,1)} %param.11) | copy-start | bytes 9437188
  20.6 4.5 %collective-permute-start.1 = (bf16[16,3200]{1,0:T(8,128)(2,1)S(1)}, bf16[16,3200]{1,0:T(8,128)(2,1)S(1)}, u32[]{:S(2)}, u32[]{:S(2)}) collective-permute-start(bf16[16,3200]{1,0:T(8,128)(2,1)S(1)} %slice.221), channel_id=1, source_target_pairs={{0,136},{1,137},{2,138},{3,139},{4,140},{5,141},{6,142},{7,143},{1... | collective-permute-start | bytes 307208 | tf_op jit(solution)/shard_map/ppermute | solution.py:30
  23.4 4.7 %collective-permute-start = (bf16[16,3200]{1,0:T(8,128)(2,1)S(1)}, bf16[16,3200]{1,0:T(8,128)(2,1)S(1)}, u32[]{:S(2)}, u32[]{:S(2)}) collective-permute-start(bf16[16,3200]{1,0:T(8,128)(2,1)S(1)} %slice.219), channel_id=1, source_target_pairs={{0,136},{1,137},{2,138},{3,139},{4,140},{5,141},{6,142},{7,143},{1... | collective-permute-start | bytes 307208 | tf_op jit(solution)/shard_map/ppermute | solution.py:30
  24.0 9.1 %collective-permute-start.5 = (bf16[16,3200]{1,0:T(8,128)(2,1)S(1)}, bf16[16,3200]{1,0:T(8,128)(2,1)S(1)}, u32[]{:S(2)}, u32[]{:S(2)}) collective-permute-start(bf16[16,3200]{1,0:T(8,128)(2,1)S(1)} %slice.221), channel_id=1, source_target_pairs={{0,128},{1,129},{2,130},{3,131},{4,132},{5,133},{6,134},{7,135},{1... | collective-permute-start | bytes 307208 | tf_op jit(solution)/shard_map/ppermute | solution.py:30
  25.0 5.1 %collective-permute-start.2 = (bf16[16,3200]{1,0:T(8,128)(2,1)S(1)}, bf16[16,3200]{1,0:T(8,128)(2,1)S(1)}, u32[]{:S(2)}, u32[]{:S(2)}) collective-permute-start(bf16[16,3200]{1,0:T(8,128)(2,1)S(1)} %slice.219), channel_id=1, source_target_pairs={{0,128},{1,129},{2,130},{3,131},{4,132},{5,133},{6,134},{7,135},{1... | collective-permute-start | bytes 307208 | tf_op jit(solution)/shard_map/ppermute | solution.py:30
  25.1 8.0 %collective-permute-start.4 = (bf16[16,3200]{1,0:T(8,128)(2,1)S(1)}, bf16[16,3200]{1,0:T(8,128)(2,1)S(1)}, u32[]{:S(2)}, u32[]{:S(2)}) collective-permute-start(bf16[16,3200]{1,0:T(8,128)(2,1)S(1)} %collective-permute-done.1), channel_id=1, source_target_pairs={{0,136},{1,137},{2,138},{3,139},{4,140},{5,141},{6,142},{7,143},{1... | collective-permute-start | bytes 307208 | tf_op jit(solution)/shard_map/ppermute | solution.py:30
  30.1 4.7 %collective-permute-start.3 = (bf16[16,3200]{1,0:T(8,128)(2,1)S(1)}, bf16[16,3200]{1,0:T(8,128)(2,1)S(1)}, u32[]{:S(2)}, u32[]{:S(2)}) collective-permute-start(bf16[16,3200]{1,0:T(8,128)(2,1)S(1)} %collective-permute-done.2), channel_id=1, source_target_pairs={{0,128},{1,129},{2,130},{3,131},{4,132},{5,133},{6,134},{7,135},{1... | collective-permute-start | bytes 307208 | tf_op jit(solution)/shard_map/ppermute | solution.py:30
  30.9 11.4 %collective-permute-start.6 = (bf16[2,32,3200]{2,1,0:T(8,128)(2,1)S(1)}, bf16[2,32,3200]{2,1,0:T(8,128)(2,1)S(1)}, u32[]{:S(2)}, u32[]{:S(2)}) collective-permute-start(bf16[2,32,3200]{2,1,0:T(8,128)(2,1)S(1)} %bitcast.145), channel_id=1, source_target_pairs={{0,48},{1,49},{2,50},{3,51},{4,52},{5,53},{6,54},{7,55},{16,0},{17... | collective-permute-start | bytes 1228808 | tf_op jit(solution)/shard_map/ppermute | solution.py:30
  33.0 9.2 %collective-permute-start.8 = (bf16[2,32,3200]{2,1,0:T(8,128)(2,1)S(1)}, bf16[2,32,3200]{2,1,0:T(8,128)(2,1)S(1)}, u32[]{:S(2)}, u32[]{:S(2)}) collective-permute-start(bf16[2,32,3200]{2,1,0:T(8,128)(2,1)S(1)} %bitcast.146), channel_id=1, source_target_pairs={{0,16},{1,17},{2,18},{3,19},{4,20},{5,21},{6,22},{7,23},{16,32},{1... | collective-permute-start | bytes 1228808 | tf_op jit(solution)/shard_map/ppermute | solution.py:30
  34.8 8.2 %collective-permute-start.7 = (bf16[2,32,3200]{2,1,0:T(8,128)(2,1)S(1)}, bf16[2,32,3200]{2,1,0:T(8,128)(2,1)S(1)}, u32[]{:S(2)}, u32[]{:S(2)}) collective-permute-start(bf16[2,32,3200]{2,1,0:T(8,128)(2,1)S(1)} %bitcast.141), channel_id=1, source_target_pairs={{0,48},{1,49},{2,50},{3,51},{4,52},{5,53},{6,54},{7,55},{16,0},{17... | collective-permute-start | bytes 1228808 | tf_op jit(solution)/shard_map/ppermute | solution.py:30
  37.1 16.3 %collective-permute-start.11 = (bf16[2,32,3200]{2,1,0:T(8,128)(2,1)S(1)}, bf16[2,32,3200]{2,1,0:T(8,128)(2,1)S(1)}, u32[]{:S(2)}, u32[]{:S(2)}) collective-permute-start(bf16[2,32,3200]{2,1,0:T(8,128)(2,1)S(1)} %bitcast.142), channel_id=1, source_target_pairs={{0,16},{1,17},{2,18},{3,19},{4,20},{5,21},{6,22},{7,23},{16,32},{1... | collective-permute-start | bytes 1228808 | tf_op jit(solution)/shard_map/ppermute | solution.py:30
  42.3 8.8 %collective-permute-start.9 = (bf16[2,32,3200]{2,1,0:T(8,128)(2,1)S(1)}, bf16[2,32,3200]{2,1,0:T(8,128)(2,1)S(1)}, u32[]{:S(2)}, u32[]{:S(2)}) collective-permute-start(bf16[2,32,3200]{2,1,0:T(8,128)(2,1)S(1)} %collective-permute-done.8), channel_id=1, source_target_pairs={{0,16},{1,17},{2,18},{3,19},{4,20},{5,21},{6,22},{7,23},{16,32},{1... | collective-permute-start | bytes 1228808 | tf_op jit(solution)/shard_map/ppermute | solution.py:30
  43.1 8.8 %collective-permute-start.10 = (bf16[2,32,3200]{2,1,0:T(8,128)(2,1)S(1)}, bf16[2,32,3200]{2,1,0:T(8,128)(2,1)S(1)}, u32[]{:S(2)}, u32[]{:S(2)}) collective-permute-start(bf16[2,32,3200]{2,1,0:T(8,128)(2,1)S(1)} %collective-permute-done.7), channel_id=1, source_target_pairs={{0,48},{1,49},{2,50},{3,51},{4,52},{5,53},{6,54},{7,55},{16,0},{17... | collective-permute-start | bytes 1228808 | tf_op jit(solution)/shard_map/ppermute | solution.py:30
  54.2 11.0 %collective-permute-start.12 = (bf16[16,32,3200]{2,1,0:T(8,128)(2,1)}, bf16[16,32,3200]{2,1,0:T(8,128)(2,1)}, u32[]{:S(2)}, u32[]{:S(2)}) collective-permute-start(bf16[16,32,3200]{2,1,0:T(8,128)(2,1)} %constant_dynamic-update-slice_fusion.16), channel_id=1, source_target_pairs={{0,64},{64,0},{1,65},{65,1},{2,66},{66,2},{3,67},{67,3},{4,68},{68... | collective-permute-start | bytes 9830408 | tf_op jit(solution)/shard_map/ppermute | solution.py:34
  74.6 2.5 %collective-permute-start.15 = (bf16[128,3072]{1,0:T(8,128)(2,1)S(1)}, bf16[128,3072]{1,0:T(8,128)(2,1)S(1)}, u32[]{:S(2)}, u32[]{:S(2)}) collective-permute-start(bf16[128,3072]{1,0:T(8,128)(2,1)S(1)} %fusion.2), channel_id=1, source_target_pairs={{0,64},{64,0},{1,65},{65,1},{2,66},{66,2},{3,67},{67,3},{4,68},{68... | collective-permute-start | bytes 2359304 | tf_op jit(solution)/shard_map/ppermute | solution.py:34
  75.4 8.7 %collective-permute-start.13 = (bf16[128,3072]{1,0:T(8,128)(2,1)S(1)}, bf16[128,3072]{1,0:T(8,128)(2,1)S(1)}, u32[]{:S(2)}, u32[]{:S(2)}) collective-permute-start(bf16[128,3072]{1,0:T(8,128)(2,1)S(1)} %fusion), channel_id=1, source_target_pairs={{0,64},{64,0},{1,65},{65,1},{2,66},{66,2},{3,67},{67,3},{4,68},{68... | collective-permute-start | bytes 2359304 | tf_op jit(solution)/shard_map/ppermute | solution.py:34
  76.0 4.9 %collective-permute-start.18 = (bf16[128,3072]{1,0:T(8,128)(2,1)S(1)}, bf16[128,3072]{1,0:T(8,128)(2,1)S(1)}, u32[]{:S(2)}, u32[]{:S(2)}) collective-permute-start(bf16[128,3072]{1,0:T(8,128)(2,1)S(1)} %fusion.3), channel_id=1, source_target_pairs={{0,64},{64,0},{1,65},{65,1},{2,66},{66,2},{3,67},{67,3},{4,68},{68... | collective-permute-start | bytes 2359304 | tf_op jit(solution)/shard_map/ppermute | solution.py:34
  76.9 3.4 %collective-permute-start.14 = (bf16[128,3072]{1,0:T(8,128)(2,1)S(1)}, bf16[128,3072]{1,0:T(8,128)(2,1)S(1)}, u32[]{:S(2)}, u32[]{:S(2)}) collective-permute-start(bf16[128,3072]{1,0:T(8,128)(2,1)S(1)} %fusion.1), channel_id=1, source_target_pairs={{0,64},{64,0},{1,65},{65,1},{2,66},{66,2},{3,67},{67,3},{4,68},{68... | collective-permute-start | bytes 2359304 | tf_op jit(solution)/shard_map/ppermute | solution.py:34
  77.6 7.0 %collective-permute-start.21 = (bf16[2,32,3072]{2,1,0:T(8,128)(2,1)S(1)}, bf16[2,32,3072]{2,1,0:T(8,128)(2,1)S(1)}, u32[]{:S(2)}, u32[]{:S(2)}) collective-permute-start(bf16[2,32,3072]{2,1,0:T(8,128)(2,1)S(1)} %bitcast.155), channel_id=1, source_target_pairs={{0,48},{1,49},{2,50},{3,51},{4,52},{5,53},{6,54},{7,55},{16,0},{17... | collective-permute-start | bytes 1179656 | tf_op jit(solution)/shard_map/ppermute | solution.py:30
  80.8 12.6 %collective-permute-start.20 = (bf16[2,32,3072]{2,1,0:T(8,128)(2,1)S(1)}, bf16[2,32,3072]{2,1,0:T(8,128)(2,1)S(1)}, u32[]{:S(2)}, u32[]{:S(2)}) collective-permute-start(bf16[2,32,3072]{2,1,0:T(8,128)(2,1)S(1)} %bitcast.154), channel_id=1, source_target_pairs={{0,16},{1,17},{2,18},{3,19},{4,20},{5,21},{6,22},{7,23},{16,32},{1... | collective-permute-start | bytes 1179656 | tf_op jit(solution)/shard_map/ppermute | solution.py:30
  81.4 18.4 %collective-permute-start.19 = (bf16[2,32,3072]{2,1,0:T(8,128)(2,1)S(1)}, bf16[2,32,3072]{2,1,0:T(8,128)(2,1)S(1)}, u32[]{:S(2)}, u32[]{:S(2)}) collective-permute-start(bf16[2,32,3072]{2,1,0:T(8,128)(2,1)S(1)} %bitcast.152), channel_id=1, source_target_pairs={{0,48},{1,49},{2,50},{3,51},{4,52},{5,53},{6,54},{7,55},{16,0},{17... | collective-permute-start | bytes 1179656 | tf_op jit(solution)/shard_map/ppermute | solution.py:30
  84.1 9.1 %collective-permute-start.16 = (bf16[2,32,3072]{2,1,0:T(8,128)(2,1)S(1)}, bf16[2,32,3072]{2,1,0:T(8,128)(2,1)S(1)}, u32[]{:S(2)}, u32[]{:S(2)}) collective-permute-start(bf16[2,32,3072]{2,1,0:T(8,128)(2,1)S(1)} %bitcast.153), channel_id=1, source_target_pairs={{0,16},{1,17},{2,18},{3,19},{4,20},{5,21},{6,22},{7,23},{16,32},{1... | collective-permute-start | bytes 1179656 | tf_op jit(solution)/shard_map/ppermute | solution.py:30
  84.7 8.7 %collective-permute-start.22 = (bf16[2,32,3072]{2,1,0:T(8,128)(2,1)S(1)}, bf16[2,32,3072]{2,1,0:T(8,128)(2,1)S(1)}, u32[]{:S(2)}, u32[]{:S(2)}) collective-permute-start(bf16[2,32,3072]{2,1,0:T(8,128)(2,1)S(1)} %fusion.41), channel_id=1, source_target_pairs={{0,48},{1,49},{2,50},{3,51},{4,52},{5,53},{6,54},{7,55},{16,0},{17... | collective-permute-start | bytes 1179656 | tf_op jit(solution)/shard_map/ppermute | solution.py:30
  93.3 8.2 %collective-permute-start.17 = (bf16[2,32,3072]{2,1,0:T(8,128)(2,1)S(1)}, bf16[2,32,3072]{2,1,0:T(8,128)(2,1)S(1)}, u32[]{:S(2)}, u32[]{:S(2)}) collective-permute-start(bf16[2,32,3072]{2,1,0:T(8,128)(2,1)S(1)} %fusion.44), channel_id=1, source_target_pairs={{0,16},{1,17},{2,18},{3,19},{4,20},{5,21},{6,22},{7,23},{16,32},{1... | collective-permute-start | bytes 1179656 | tf_op jit(solution)/shard_map/ppermute | solution.py:30
  93.6 12.4 %collective-permute-start.25 = (bf16[16,3072]{1,0:T(8,128)(2,1)S(1)}, bf16[16,3072]{1,0:T(8,128)(2,1)S(1)}, u32[]{:S(2)}, u32[]{:S(2)}) collective-permute-start(bf16[16,3072]{1,0:T(8,128)(2,1)S(1)} %get-tuple-element.21), channel_id=1, source_target_pairs={{0,136},{1,137},{2,138},{3,139},{4,140},{5,141},{6,142},{7,143},{1... | collective-permute-start | bytes 294920 | tf_op jit(solution)/shard_map/ppermute | solution.py:30
  97.1 6.0 %collective-permute-start.23 = (bf16[16,3072]{1,0:T(8,128)(2,1)S(1)}, bf16[16,3072]{1,0:T(8,128)(2,1)S(1)}, u32[]{:S(2)}, u32[]{:S(2)}) collective-permute-start(bf16[16,3072]{1,0:T(8,128)(2,1)S(1)} %get-tuple-element.19), channel_id=1, source_target_pairs={{0,128},{1,129},{2,130},{3,131},{4,132},{5,133},{6,134},{7,135},{1... | collective-permute-start | bytes 294920 | tf_op jit(solution)/shard_map/ppermute | solution.py:30
  97.1 6.1 %collective-permute-start.27 = (bf16[16,3072]{1,0:T(8,128)(2,1)S(1)}, bf16[16,3072]{1,0:T(8,128)(2,1)S(1)}, u32[]{:S(2)}, u32[]{:S(2)}) collective-permute-start(bf16[16,3072]{1,0:T(8,128)(2,1)S(1)} %get-tuple-element.20), channel_id=1, source_target_pairs={{0,136},{1,137},{2,138},{3,139},{4,140},{5,141},{6,142},{7,143},{1... | collective-permute-start | bytes 294920 | tf_op jit(solution)/shard_map/ppermute | solution.py:30
  101.7 5.2 %collective-permute-start.26 = (bf16[16,3072]{1,0:T(8,128)(2,1)S(1)}, bf16[16,3072]{1,0:T(8,128)(2,1)S(1)}, u32[]{:S(2)}, u32[]{:S(2)}) collective-permute-start(bf16[16,3072]{1,0:T(8,128)(2,1)S(1)} %slice_bitcast_fusion.2), channel_id=1, source_target_pairs={{0,128},{1,129},{2,130},{3,131},{4,132},{5,133},{6,134},{7,135},{1... | collective-permute-start | bytes 294920 | tf_op jit(solution)/shard_map/ppermute | solution.py:30
  103.2 4.8 %collective-permute-start.24 = (bf16[16,3072]{1,0:T(8,128)(2,1)S(1)}, bf16[16,3072]{1,0:T(8,128)(2,1)S(1)}, u32[]{:S(2)}, u32[]{:S(2)}) collective-permute-start(bf16[16,3072]{1,0:T(8,128)(2,1)S(1)} %fusion.50), channel_id=1, source_target_pairs={{0,128},{1,129},{2,130},{3,131},{4,132},{5,133},{6,134},{7,135},{1... | collective-permute-start | bytes 294920 | tf_op jit(solution)/shard_map/ppermute | solution.py:30
  103.3 4.7 %collective-permute-start.28 = (bf16[16,3072]{1,0:T(8,128)(2,1)S(1)}, bf16[16,3072]{1,0:T(8,128)(2,1)S(1)}, u32[]{:S(2)}, u32[]{:S(2)}) collective-permute-start(bf16[16,3072]{1,0:T(8,128)(2,1)S(1)} %fusion.48), channel_id=1, source_target_pairs={{0,136},{1,137},{2,138},{3,139},{4,140},{5,141},{6,142},{7,143},{1... | collective-permute-start | bytes 294920 | tf_op jit(solution)/shard_map/ppermute | solution.py:30

commit v2 on v1

--- a/solution.py
+++ b/solution.py
@@ -34,9 +34,7 @@
     return lax.ppermute(v, "c", [(0, 1), (1, 0)])
 
 
-def ring_gather(block, first):
-    half = block.shape[0] // 2
-    one, two = block[:half], block[half:]
+def ring_gather(one, two, first):
     from_left_one = move(one, first, 1)
     from_right_two = move(two, first, -1)
     from_left_two = move(two, first, 1)
@@ -64,7 +62,7 @@
     left_two = move(add(left[half:], to_left).astype(jnp.bfloat16), first, -1)
     one = add(own[:half], right_one, left_one)
     two = add(own[half:], right_two, left_two)
-    return jnp.concatenate([one, two], axis=0)
+    return one, two
 
 
 def parts(w):
@@ -88,11 +86,11 @@
     tile = lax.all_to_all(outgoing, ("c", "z"), split_axis=0, concat_axis=0, tiled=True)
     tile = tile.reshape(16 * tok_rows, half + PAD)
     rows = tile.shape[0]
-    quarter = jnp.concatenate(ring_gather(tile, True), axis=0)
-    quarter = quarter.reshape(RING, rows, half + PAD)
-    pieces = ring_gather(quarter, False)
-    mine = jnp.concatenate(pieces, axis=0)
-    other = swap(mine)
+    tiles = [tile] + [move(tile, True, step) for step in (-1, 2, 1)]
+    one = jnp.stack(tiles[:2], axis=0)
+    two = jnp.stack(tiles[2:], axis=0)
+    mine = [v.reshape(2 * rows, half + PAD) for v in ring_gather(one, two, False)]
+    other = [swap(v) for v in mine]
 
     def halves(w, axis):
         own = lax.dynamic_slice_in_dim(w, core * half, half, axis)
@@ -108,18 +106,19 @@
     def turned(v):
         return v.reshape(RING, RING, rows, v.shape[-1]).swapaxes(0, 1).reshape(n, v.shape[-1])
 
-    mine = mine.reshape(n, half + PAD)
-    other = other.reshape(n, half + PAD)
-    act = jnp.dot(mine, in_own, preferred_element_type=jnp.float32)
-    act = act + turned(jnp.dot(other, in_rest, preferred_element_type=jnp.float32))
+    def product(pieces, w):
+        return jnp.concatenate([jnp.dot(v, w, preferred_element_type=jnp.float32) for v in pieces], axis=0)
+
+    act = product(mine, in_own) + turned(product(other, in_rest))
     hidden = (jax.nn.silu(act[:, :units]) * act[:, units:]).astype(jnp.bfloat16)
     hidden_rest = turned(hidden)
 
     lane = jnp.arange(PAD, dtype=jnp.int32)
     mask = (lane % 4 == expert) & (lane < 12)
 
-    def scale_of(v):
-        return jnp.sum(jnp.where(mask[None, :], v[:, half:].astype(jnp.float32), 0.0), axis=1, keepdims=True)
+    def scale_of(pieces):
+        v = jnp.concatenate([p[:, half:] for p in pieces], axis=0)
+        return jnp.sum(jnp.where(mask[None, :], v.astype(jnp.float32), 0.0), axis=1, keepdims=True)
 
     scale_own, scale_rest = scale_of(mine), scale_of(other)
     per = n // RING
@@ -130,10 +129,13 @@
         came = swap(rest.astype(jnp.bfloat16))
         own = jnp.dot(hidden[span], down_own, preferred_element_type=jnp.float32) * scale_own[span]
         blocks[d] = add(own, came).astype(jnp.bfloat16).reshape(RING, rows, half)
-    summed = ring_reduce(blocks, False).astype(jnp.bfloat16)
-    last = ring_reduce([summed[d] for d in range(RING)], True)
+    one, two = ring_reduce(blocks, False)
+    from_left = move(one[1].astype(jnp.bfloat16), True, 1)
+    from_far = move(two[0].astype(jnp.bfloat16), True, 2)
+    from_right = move(two[1].astype(jnp.bfloat16), True, -1)
+    last = add(one[0], from_left, from_far, from_right).astype(jnp.bfloat16)
     back = lax.all_to_all(last.reshape(16, tok_rows, half), ("c", "z"), split_axis=0, concat_axis=0, tiled=True)
-    total = jnp.sum(back.reshape(2, 8, tok_rows, half), axis=1)
+    total = jnp.sum(back.reshape(2, 8, tok_rows, half).astype(jnp.float32), axis=1)
     return jnp.concatenate([total[0], total[1]], axis=1).astype(jnp.bfloat16)
 
 

time: 132 us -> 135 us (1.023)
  blocking collectives: 39.6 us -> 17.2 us
  other arithmetic: 7.11 us -> 20.2 us
  waiting for transfers between devices: 27.4 us -> 35.5 us
  local copies, waits for them, and re-layouts: 8.65 us -> 2.34 us
  starting transfers between devices: 37.3 us -> 42.9 us
  matrix products: 10.7 us -> 16 us
    all_to_all x1 -> x0, blocking collectives: 18.2 us -> none  [shards(): lax.all_to_all(outgoing, ('c', 'z'), split_axis=0, concat_axis=0, tiled=T...]
    ppermute x24 -> x18, starting transfers between devices: 30.8 us -> 19.9 us  [move(): return lax.ppermute(v, AXES, ring_perm(first, step))]
    all_to_all x0 -> x1, starting transfers between devices: none -> 9.97 us  [shards(): lax.all_to_all(outgoing, ('c', 'z'), split_axis=0, concat_axis=0, tiled=T...]
    unnamed x15, other arithmetic: 0.33 us -> 9.14 us
    all_to_all x0 -> x1, waiting for transfers between devices: none -> 8.41 us  [shards(): lax.all_to_all(outgoing, ('c', 'z'), split_axis=0, concat_axis=0, tiled=T...]
    ppermute x5 -> x12, starting transfers between devices: 6.54 us -> 12.9 us  [swap(): return lax.ppermute(v, 'c', [(0, 1), (1, 0)])]
    unnamed x9 -> x22, local copies, waits for them, and re-layouts: 5.51 us -> 0.21 us
    dot_general x2 -> x16, matrix products: 7.52 us -> 12.7 us  [product(): jnp.dot(v, w, preferred_element_type=jnp.float32)]
  transfers between devices with their start and end apart: 29 -> 31, of which waited for: 12 -> 11; matrix products, arithmetic and copies ran while one was open for 9% -> 17% of each run, Pallas kernels for 0% -> 0%
where the time goes in v2:
time: 135 us
  starting transfers between devices  42.9 us (32%)
  waiting for transfers between devices  35.5 us (26%)
  other arithmetic  20.2 us (15%)
  blocking collectives  17.2 us (13%)
  matrix products  16 us (12%)
  local copies, waits for them, and re-layouts  2.34 us (2%)
    ppermute x18, waiting for transfers between devices, move(): return lax.ppermute(v, AXES, ring_perm(first, step))  26.6 us
    ppermute x18, starting transfers between devices, move(): return lax.ppermute(v, AXES, ring_perm(first, step))  19.9 us
    all_to_all x1, blocking collectives, shards(): lax.all_to_all(last.reshape(16, tok_rows, half), ('c', 'z'), split_axis=0...  17.2 us
    ppermute x12, starting transfers between devices, swap(): return lax.ppermute(v, 'c', [(0, 1), (1, 0)])  12.9 us
    dot_general x16, matrix products, product(): jnp.dot(v, w, preferred_element_type=jnp.float32)  12.7 us
    all_to_all x1, starting transfers between devices, shards(): lax.all_to_all(outgoing, ('c', 'z'), split_axis=0, concat_axis=0, tiled=T...  9.97 us
    unnamed x15, other arithmetic  9.14 us
    all_to_all x1, waiting for transfers between devices, shards(): lax.all_to_all(outgoing, ('c', 'z'), split_axis=0, concat_axis=0, tiled=T...  8.41 us
  transfers between devices with their start and end apart: 31, of which 11 were waited for; matrix products, arithmetic and copies ran while one was open for 17% of the time, Pallas kernels for 0%

profile of v2, /device:TPU:1, one launch (start us, length us, event | category | flops | bytes accessed | tf_op | source)
XLA Modules:
  0.0 134.6 jit_solution(503781218517433558)
XLA Ops:
  0.0 0.9 fusion.63
  0.9 0.8 fusion.99
  5.5 0.6 constant_dynamic-update-slice_fusion.9
  11.6 10.0 %all-to-all-start = ((bf16[16,2,3200]{2,1,0:T(2,128)(2,1)}), bf16[16,2,3200]{2,1,0:T(2,128)(2,1)S(1)}, u32[]{:S(2)}, u32[]{:S(2)}) async-start(bf16[16,2,3200]{2,1,0:T(2,128)(2,1)} %constant_dynamic-update-slice_fusion), calls=%async_computation | async-start | bytes 409600 | tf_op jit(solution)/shard_map/all_to_all | solution.py:86
  21.5 8.4 %all-to-all-done = bf16[16,2,3200]{2,1,0:T(2,128)(2,1)S(1)} async-done(((bf16[16,2,3200]{2,1,0:T(2,128)(2,1)}), bf16[16,2,3200]{2,1,0:T(2,128)(2,1)S(1)}, u32[]{:S(2)}, u32[]{:S(2)}) %all-to-all-start) | async-done | bytes 204832 | tf_op jit(solution)/shard_map/all_to_all | solution.py:86
  30.0 0.8 reshape.103
  30.7 2.7 %collective-permute-start = (bf16[32,3200]{1,0:T(8,128)(2,1)}, bf16[32,3200]{1,0:T(8,128)(2,1)}, u32[]{:S(2)}, u32[]{:S(2)}) collective-permute-start(bf16[32,3200]{1,0:T(8,128)(2,1)} %reshape.103), channel_id=1, source_target_pairs={{0,136},{1,137},{2,138},{3,139},{4,140},{5,141},{6,142},{7,143},{1... | collective-permute-start | bytes 614408 | tf_op jit(solution)/shard_map/ppermute | solution.py:30
  33.5 4.8 %fusion.4 = (bf16[3072,512]{1,0:T(8,128)(2,1)}, bf16[3072,512]{1,0:T(8,128)(2,1)}) fusion(s32[]{:T(128)S(6)} %select_n.32, bf16[6144,256]{1,0:T(8,128)(2,1)} %bitcast.141, bf16[6144,256]{1,0:T(8,128)(2,1)} %bitcast.142, s32[]{:T(128)S(6)} %select_n.31), kind=kLoop, calls=%fused_computation.16 | loop fusion | flops 12582912 | bytes 12582920 | tf_op jit(solution)/shard_map/concatenate | solution.py:100
  38.8 1.6 %collective-permute-start.1 = (bf16[32,3200]{1,0:T(8,128)(2,1)}, bf16[32,3200]{1,0:T(8,128)(2,1)}, u32[]{:S(2)}, u32[]{:S(2)}) collective-permute-start(bf16[32,3200]{1,0:T(8,128)(2,1)} %reshape.103), channel_id=1, source_target_pairs={{0,8},{1,9},{2,10},{3,11},{4,12},{5,13},{6,14},{7,15},{16,24},{17,... | collective-permute-start | bytes 614408 | tf_op jit(solution)/shard_map/ppermute | solution.py:30
  40.5 1.1 pad_maximum_fusion
  41.6 2.6 %collective-permute-start.3 = (bf16[2,32,3200]{2,1,0:T(8,128)(2,1)S(1)}, bf16[2,32,3200]{2,1,0:T(8,128)(2,1)S(1)}, u32[]{:S(2)}, u32[]{:S(2)}) collective-permute-start(bf16[2,32,3200]{2,1,0:T(8,128)(2,1)S(1)} %pad_maximum_fusion), channel_id=1, source_target_pairs={{0,48},{1,49},{2,50},{3,51},{4,52},{5,53},{6,54},{7,55},{16,0},{17... | collective-permute-start | bytes 1228808 | tf_op jit(solution)/shard_map/ppermute | solution.py:30
  44.2 3.2 %collective-permute-done.2 = bf16[32,3200]{1,0:T(8,128)(2,1)} collective-permute-done((bf16[32,3200]{1,0:T(8,128)(2,1)}, bf16[32,3200]{1,0:T(8,128)(2,1)}, u32[]{:S(2)}, u32[]{:S(2)}) %collective-permute-start.2) | collective-permute-done | bytes 204832 | tf_op jit(solution)/shard_map/ppermute | solution.py:30
  47.4 1.1 pad_maximum_fusion.1
  48.5 2.6 %collective-permute-start.4 = (bf16[2,32,3200]{2,1,0:T(8,128)(2,1)S(1)}, bf16[2,32,3200]{2,1,0:T(8,128)(2,1)S(1)}, u32[]{:S(2)}, u32[]{:S(2)}) collective-permute-start(bf16[2,32,3200]{2,1,0:T(8,128)(2,1)S(1)} %pad_maximum_fusion.1), channel_id=1, source_target_pairs={{0,48},{1,49},{2,50},{3,51},{4,52},{5,53},{6,54},{7,55},{16,0},{17... | collective-permute-start | bytes 1228808 | tf_op jit(solution)/shard_map/ppermute | solution.py:30
  51.0 3.8 %collective-permute-start.9 = (bf16[64,3200]{1,0:T(8,128)(2,1)S(1)}, bf16[64,3200]{1,0:T(8,128)(2,1)S(1)}, u32[]{:S(2)}, u32[]{:S(2)}) collective-permute-start(bf16[64,3200]{1,0:T(8,128)(2,1)S(1)} %bitcast.147), channel_id=1, source_target_pairs={{0,64},{64,0},{1,65},{65,1},{2,66},{66,2},{3,67},{67,3},{4,68},{68... | collective-permute-start | bytes 1228808 | tf_op jit(solution)/shard_map/ppermute | solution.py:34
  54.8 2.6 %convolution_dynamic-update-slice_fusion.15 = f32[512,512]{1,0:T(8,128)S(1)} fusion(bf16[64,3200]{1,0:T(8,128)(2,1)S(1)} %bitcast.148, bf16[3072,512]{1,0:T(8,128)(2,1)} %get-tuple-element.8), kind=kOutput, calls=%fused_computation.45 | convolution fusion | flops 209715200 | bytes 3686400 | tf_op jit(solution)/shard_map/dot_general | solution.py:110
  57.4 0.7 convolution_dynamic-update-slice_fusion.14
  58.2 0.7 convolution_dynamic-update-slice_fusion.13
  58.9 1.4 %collective-permute-start.11 = (bf16[64,3200]{1,0:T(8,128)(2,1)S(1)}, bf16[64,3200]{1,0:T(8,128)(2,1)S(1)}, u32[]{:S(2)}, u32[]{:S(2)}) collective-permute-start(bf16[64,3200]{1,0:T(8,128)(2,1)S(1)} %bitcast.162), channel_id=1, source_target_pairs={{0,64},{64,0},{1,65},{65,1},{2,66},{66,2},{3,67},{67,3},{4,68},{68... | collective-permute-start | bytes 1228808 | tf_op jit(solution)/shard_map/ppermute | solution.py:34
  60.3 0.7 convolution_dynamic-update-slice_fusion.12
  61.1 0.7 convolution_dynamic-update-slice_fusion.7
  61.8 1.9 %collective-permute-start.7 = (bf16[2,32,3200]{2,1,0:T(8,128)(2,1)S(1)}, bf16[2,32,3200]{2,1,0:T(8,128)(2,1)S(1)}, u32[]{:S(2)}, u32[]{:S(2)}) collective-permute-start(bf16[2,32,3200]{2,1,0:T(8,128)(2,1)S(1)} %collective-permute-done.4), channel_id=1, source_target_pairs={{0,48},{1,49},{2,50},{3,51},{4,52},{5,53},{6,54},{7,55},{16,0},{17... | collective-permute-start | bytes 1228808 | tf_op jit(solution)/shard_map/ppermute | solution.py:30
  63.7 0.7 convolution_dynamic-update-slice_fusion.6
  64.4 2.4 %collective-permute-start.15 = (bf16[64,3200]{1,0:T(8,128)(2,1)S(1)}, bf16[64,3200]{1,0:T(8,128)(2,1)S(1)}, u32[]{:S(2)}, u32[]{:S(2)}) collective-permute-start(bf16[64,3200]{1,0:T(8,128)(2,1)S(1)} %bitcast.155), channel_id=1, source_target_pairs={{0,64},{64,0},{1,65},{65,1},{2,66},{66,2},{3,67},{67,3},{4,68},{68... | collective-permute-start | bytes 1228808 | tf_op jit(solution)/shard_map/ppermute | solution.py:34
  66.8 5.2 %collective-permute-done.6 = bf16[2,32,3200]{2,1,0:T(8,128)(2,1)S(1)} collective-permute-done((bf16[2,32,3200]{2,1,0:T(8,128)(2,1)S(1)}, bf16[2,32,3200]{2,1,0:T(8,128)(2,1)S(1)}, u32[]{:S(2)}, u32[]{:S(2)}) %collective-permute-start.6) | collective-permute-done | bytes 409632 | tf_op jit(solution)/shard_map/ppermute | solution.py:30
  72.0 3.2 %collective-permute-start.16 = (bf16[64,3200]{1,0:T(8,128)(2,1)S(1)}, bf16[64,3200]{1,0:T(8,128)(2,1)S(1)}, u32[]{:S(2)}, u32[]{:S(2)}) collective-permute-start(bf16[64,3200]{1,0:T(8,128)(2,1)S(1)} %bitcast.158), channel_id=1, source_target_pairs={{0,64},{64,0},{1,65},{65,1},{2,66},{66,2},{3,67},{67,3},{4,68},{68... | collective-permute-start | bytes 1228808 | tf_op jit(solution)/shard_map/ppermute | solution.py:34
  75.2 0.7 convolution_dynamic-update-slice_fusion.11
  76.0 0.7 convolution_dynamic-update-slice_fusion.10
  76.6 0.7 convolution_dynamic-update-slice_fusion.9
  77.3 0.7 convolution_dynamic-update-slice_fusion.8
  78.7 0.7 convolution_dynamic-update-slice_fusion.5
  79.3 0.7 convolution_dynamic-update-slice_fusion.4
  80.0 0.7 convolution_dynamic-update-slice_fusion.3
  80.7 0.7 convolution_dynamic-update-slice_fusion.2
  81.4 0.7 convolution_dynamic-update-slice_fusion.1
  82.1 0.7 convolution_dynamic-update-slice_fusion
  87.1 2.2 %collective-permute-start.23 = (bf16[2,32,3072]{2,1,0:T(8,128)(2,1)S(1)}, bf16[2,32,3072]{2,1,0:T(8,128)(2,1)S(1)}, u32[]{:S(2)}, u32[]{:S(2)}) collective-permute-start(bf16[2,32,3072]{2,1,0:T(8,128)(2,1)S(1)} %bitcast.173), channel_id=1, source_target_pairs={{0,48},{1,49},{2,50},{3,51},{4,52},{5,53},{6,54},{7,55},{16,0},{17... | collective-permute-start | bytes 1179656 | tf_op jit(solution)/shard_map/ppermute | solution.py:30
  90.3 2.7 %collective-permute-start.26 = (bf16[2,32,3072]{2,1,0:T(8,128)(2,1)S(1)}, bf16[2,32,3072]{2,1,0:T(8,128)(2,1)S(1)}, u32[]{:S(2)}, u32[]{:S(2)}) collective-permute-start(bf16[2,32,3072]{2,1,0:T(8,128)(2,1)S(1)} %bitcast.176), channel_id=1, source_target_pairs={{0,48},{1,49},{2,50},{3,51},{4,52},{5,53},{6,54},{7,55},{16,0},{17... | collective-permute-start | bytes 1179656 | tf_op jit(solution)/shard_map/ppermute | solution.py:30
  94.1 4.4 %collective-permute-done.26 = bf16[2,32,3072]{2,1,0:T(8,128)(2,1)S(1)} collective-permute-done((bf16[2,32,3072]{2,1,0:T(8,128)(2,1)S(1)}, bf16[2,32,3072]{2,1,0:T(8,128)(2,1)S(1)}, u32[]{:S(2)}, u32[]{:S(2)}) %collective-permute-start.26) | collective-permute-done | bytes 393248 | tf_op jit(solution)/shard_map/ppermute | solution.py:30
  98.6 3.2 %collective-permute-start.27 = (bf16[2,32,3072]{2,1,0:T(8,128)(2,1)S(1)}, bf16[2,32,3072]{2,1,0:T(8,128)(2,1)S(1)}, u32[]{:S(2)}, u32[]{:S(2)}) collective-permute-start(bf16[2,32,3072]{2,1,0:T(8,128)(2,1)S(1)} %fusion.46), channel_id=1, source_target_pairs={{0,48},{1,49},{2,50},{3,51},{4,52},{5,53},{6,54},{7,55},{16,0},{17... | collective-permute-start | bytes 1179656 | tf_op jit(solution)/shard_map/ppermute | solution.py:30
  102.0 0.7 collective-permute-done.25
  102.7 3.8 %collective-permute-done.27 = bf16[2,32,3072]{2,1,0:T(8,128)(2,1)S(1)} collective-permute-done((bf16[2,32,3072]{2,1,0:T(8,128)(2,1)S(1)}, bf16[2,32,3072]{2,1,0:T(8,128)(2,1)S(1)}, u32[]{:S(2)}, u32[]{:S(2)}) %collective-permute-start.27) | collective-permute-done | bytes 393248 | tf_op jit(solution)/shard_map/ppermute | solution.py:30
  106.9 3.2 %collective-permute-done.21 = bf16[2,32,3072]{2,1,0:T(8,128)(2,1)S(1)} collective-permute-done((bf16[2,32,3072]{2,1,0:T(8,128)(2,1)S(1)}, bf16[2,32,3072]{2,1,0:T(8,128)(2,1)S(1)}, u32[]{:S(2)}, u32[]{:S(2)}) %collective-permute-start.21) | collective-permute-done | bytes 393248 | tf_op jit(solution)/shard_map/ppermute | solution.py:30
  110.3 1.2 collective-permute-done.29
  111.6 1.4 %collective-permute-done.28 = bf16[32,3072]{1,0:T(8,128)(2,1)S(1)} collective-permute-done((bf16[32,3072]{1,0:T(8,128)(2,1)S(1)}, bf16[32,3072]{1,0:T(8,128)(2,1)S(1)}, u32[]{:S(2)}, u32[]{:S(2)}) %collective-permute-start.28) | collective-permute-done | bytes 196640 | tf_op jit(solution)/shard_map/ppermute | solution.py:30
  113.0 3.4 %collective-permute-done.24 = bf16[32,3072]{1,0:T(8,128)(2,1)S(1)} collective-permute-done((bf16[32,3072]{1,0:T(8,128)(2,1)S(1)}, bf16[32,3072]{1,0:T(8,128)(2,1)S(1)}, u32[]{:S(2)}, u32[]{:S(2)}) %collective-permute-start.24) | collective-permute-done | bytes 196640 | tf_op jit(solution)/shard_map/ppermute | solution.py:30
  116.5 17.2 %all_to_all.10 = bf16[16,2,3072]{2,1,0:T(2,128)(2,1)S(1)} all-to-all(bf16[16,2,3072]{2,1,0:T(2,128)(2,1)S(1)} %reshape.115), channel_id=1, replica_groups=mesh['xl'=2,'c'=2,'y'=4,'xh'=2,'z'=8] {'c','z'}, dimensions={0} | all-to-all | bytes 393216 | tf_op jit(solution)/shard_map/all_to_all | solution.py:137
  134.0 0.6 pad_maximum_fusion.2
  (111 shorter events, 18.4 us)
Async XLA Ops:
  0.0 83.6 %copy-start = (bf16[1,256,6144]{2,1,0:T(8,128)(2,1)S(1)}, bf16[1,256,6144]{2,1,0:T(8,128)(2,1)}, u32[]{:S(2)}) copy-start(bf16[1,256,6144]{2,1,0:T(8,128)(2,1)} %param.11) | copy-start | bytes 9437188
  11.6 18.4 %all-to-all-start = ((bf16[16,2,3200]{2,1,0:T(2,128)(2,1)}), bf16[16,2,3200]{2,1,0:T(2,128)(2,1)S(1)}, u32[]{:S(2)}, u32[]{:S(2)}) async-start(bf16[16,2,3200]{2,1,0:T(2,128)(2,1)} %constant_dynamic-update-slice_fusion), calls=%async_computation | async-start | bytes 409600 | tf_op jit(solution)/shard_map/all_to_all | solution.py:86
  30.7 9.8 %collective-permute-start = (bf16[32,3200]{1,0:T(8,128)(2,1)}, bf16[32,3200]{1,0:T(8,128)(2,1)}, u32[]{:S(2)}, u32[]{:S(2)}) collective-permute-start(bf16[32,3200]{1,0:T(8,128)(2,1)} %reshape.103), channel_id=1, source_target_pairs={{0,136},{1,137},{2,138},{3,139},{4,140},{5,141},{6,142},{7,143},{1... | collective-permute-start | bytes 614408 | tf_op jit(solution)/shard_map/ppermute | solution.py:30
  38.8 8.6 %collective-permute-start.2 = (bf16[32,3200]{1,0:T(8,128)(2,1)}, bf16[32,3200]{1,0:T(8,128)(2,1)}, u32[]{:S(2)}, u32[]{:S(2)}) collective-permute-start(bf16[32,3200]{1,0:T(8,128)(2,1)} %reshape.103), channel_id=1, source_target_pairs={{0,128},{1,129},{2,130},{3,131},{4,132},{5,133},{6,134},{7,135},{1... | collective-permute-start | bytes 614408 | tf_op jit(solution)/shard_map/ppermute | solution.py:30
  38.8 8.6 %collective-permute-start.1 = (bf16[32,3200]{1,0:T(8,128)(2,1)}, bf16[32,3200]{1,0:T(8,128)(2,1)}, u32[]{:S(2)}, u32[]{:S(2)}) collective-permute-start(bf16[32,3200]{1,0:T(8,128)(2,1)} %reshape.103), channel_id=1, source_target_pairs={{0,8},{1,9},{2,10},{3,11},{4,12},{5,13},{6,14},{7,15},{16,24},{17,... | collective-permute-start | bytes 614408 | tf_op jit(solution)/shard_map/ppermute | solution.py:30
  40.5 16.9 %copy-start.2 = (bf16[3072,512]{1,0:T(8,128)(2,1)S(1)}, bf16[3072,512]{1,0:T(8,128)(2,1)}, u32[]{:S(2)}) copy-start(bf16[3072,512]{1,0:T(8,128)(2,1)} %get-tuple-element.8) | copy-start | bytes 9437188
  41.6 16.4 %collective-permute-start.3 = (bf16[2,32,3200]{2,1,0:T(8,128)(2,1)S(1)}, bf16[2,32,3200]{2,1,0:T(8,128)(2,1)S(1)}, u32[]{:S(2)}, u32[]{:S(2)}) collective-permute-start(bf16[2,32,3200]{2,1,0:T(8,128)(2,1)S(1)} %pad_maximum_fusion), channel_id=1, source_target_pairs={{0,48},{1,49},{2,50},{3,51},{4,52},{5,53},{6,54},{7,55},{16,0},{17... | collective-permute-start | bytes 1228808 | tf_op jit(solution)/shard_map/ppermute | solution.py:30
  44.2 17.6 %collective-permute-start.5 = (bf16[2,32,3200]{2,1,0:T(8,128)(2,1)S(1)}, bf16[2,32,3200]{2,1,0:T(8,128)(2,1)S(1)}, u32[]{:S(2)}, u32[]{:S(2)}) collective-permute-start(bf16[2,32,3200]{2,1,0:T(8,128)(2,1)S(1)} %pad_maximum_fusion), channel_id=1, source_target_pairs={{0,16},{1,17},{2,18},{3,19},{4,20},{5,21},{6,22},{7,23},{16,32},{1... | collective-permute-start | bytes 1228808 | tf_op jit(solution)/shard_map/ppermute | solution.py:30
  48.5 10.4 %collective-permute-start.4 = (bf16[2,32,3200]{2,1,0:T(8,128)(2,1)S(1)}, bf16[2,32,3200]{2,1,0:T(8,128)(2,1)S(1)}, u32[]{:S(2)}, u32[]{:S(2)}) collective-permute-start(bf16[2,32,3200]{2,1,0:T(8,128)(2,1)S(1)} %pad_maximum_fusion.1), channel_id=1, source_target_pairs={{0,48},{1,49},{2,50},{3,51},{4,52},{5,53},{6,54},{7,55},{16,0},{17... | collective-permute-start | bytes 1228808 | tf_op jit(solution)/shard_map/ppermute | solution.py:30
  51.0 13.4 %collective-permute-start.8 = (bf16[2,32,3200]{2,1,0:T(8,128)(2,1)S(1)}, bf16[2,32,3200]{2,1,0:T(8,128)(2,1)S(1)}, u32[]{:S(2)}, u32[]{:S(2)}) collective-permute-start(bf16[2,32,3200]{2,1,0:T(8,128)(2,1)S(1)} %pad_maximum_fusion.1), channel_id=1, source_target_pairs={{0,16},{1,17},{2,18},{3,19},{4,20},{5,21},{6,22},{7,23},{16,32},{1... | collective-permute-start | bytes 1228808 | tf_op jit(solution)/shard_map/ppermute | solution.py:30
  51.0 9.9 %collective-permute-start.9 = (bf16[64,3200]{1,0:T(8,128)(2,1)S(1)}, bf16[64,3200]{1,0:T(8,128)(2,1)S(1)}, u32[]{:S(2)}, u32[]{:S(2)}) collective-permute-start(bf16[64,3200]{1,0:T(8,128)(2,1)S(1)} %bitcast.147), channel_id=1, source_target_pairs={{0,64},{64,0},{1,65},{65,1},{2,66},{66,2},{3,67},{67,3},{4,68},{68... | collective-permute-start | bytes 1228808 | tf_op jit(solution)/shard_map/ppermute | solution.py:34
  58.1 5.6 %collective-permute-start.10 = (bf16[64,3200]{1,0:T(8,128)(2,1)S(1)}, bf16[64,3200]{1,0:T(8,128)(2,1)S(1)}, u32[]{:S(2)}, u32[]{:S(2)}) collective-permute-start(bf16[64,3200]{1,0:T(8,128)(2,1)S(1)} %bitcast.146), channel_id=1, source_target_pairs={{0,64},{64,0},{1,65},{65,1},{2,66},{66,2},{3,67},{67,3},{4,68},{68... | collective-permute-start | bytes 1228808 | tf_op jit(solution)/shard_map/ppermute | solution.py:34
  58.2 2.9 %copy-start.1 = (bf16[3072,512]{1,0:T(8,128)(2,1)S(1)}, bf16[3072,512]{1,0:T(8,128)(2,1)}, u32[]{:S(2)}) copy-start(bf16[3072,512]{1,0:T(8,128)(2,1)} %get-tuple-element.7) | copy-start | bytes 9437188
  58.9 19.2 %collective-permute-start.11 = (bf16[64,3200]{1,0:T(8,128)(2,1)S(1)}, bf16[64,3200]{1,0:T(8,128)(2,1)S(1)}, u32[]{:S(2)}, u32[]{:S(2)}) collective-permute-start(bf16[64,3200]{1,0:T(8,128)(2,1)S(1)} %bitcast.162), channel_id=1, source_target_pairs={{0,64},{64,0},{1,65},{65,1},{2,66},{66,2},{3,67},{67,3},{4,68},{68... | collective-permute-start | bytes 1228808 | tf_op jit(solution)/shard_map/ppermute | solution.py:34
  61.0 18.4 %collective-permute-start.12 = (bf16[64,3200]{1,0:T(8,128)(2,1)S(1)}, bf16[64,3200]{1,0:T(8,128)(2,1)S(1)}, u32[]{:S(2)}, u32[]{:S(2)}) collective-permute-start(bf16[64,3200]{1,0:T(8,128)(2,1)S(1)} %bitcast.166), channel_id=1, source_target_pairs={{0,64},{64,0},{1,65},{65,1},{2,66},{66,2},{3,67},{67,3},{4,68},{68... | collective-permute-start | bytes 1228808 | tf_op jit(solution)/shard_map/ppermute | solution.py:34
  61.8 14.1 %collective-permute-start.7 = (bf16[2,32,3200]{2,1,0:T(8,128)(2,1)S(1)}, bf16[2,32,3200]{2,1,0:T(8,128)(2,1)S(1)}, u32[]{:S(2)}, u32[]{:S(2)}) collective-permute-start(bf16[2,32,3200]{2,1,0:T(8,128)(2,1)S(1)} %collective-permute-done.4), channel_id=1, source_target_pairs={{0,48},{1,49},{2,50},{3,51},{4,52},{5,53},{6,54},{7,55},{16,0},{17... | collective-permute-start | bytes 1228808 | tf_op jit(solution)/shard_map/ppermute | solution.py:30
  63.7 8.3 %collective-permute-start.6 = (bf16[2,32,3200]{2,1,0:T(8,128)(2,1)S(1)}, bf16[2,32,3200]{2,1,0:T(8,128)(2,1)S(1)}, u32[]{:S(2)}, u32[]{:S(2)}) collective-permute-start(bf16[2,32,3200]{2,1,0:T(8,128)(2,1)S(1)} %collective-permute-done.5), channel_id=1, source_target_pairs={{0,16},{1,17},{2,18},{3,19},{4,20},{5,21},{6,22},{7,23},{16,32},{1... | collective-permute-start | bytes 1228808 | tf_op jit(solution)/shard_map/ppermute | solution.py:30
  64.4 17.0 %collective-permute-start.15 = (bf16[64,3200]{1,0:T(8,128)(2,1)S(1)}, bf16[64,3200]{1,0:T(8,128)(2,1)S(1)}, u32[]{:S(2)}, u32[]{:S(2)}) collective-permute-start(bf16[64,3200]{1,0:T(8,128)(2,1)S(1)} %bitcast.155), channel_id=1, source_target_pairs={{0,64},{64,0},{1,65},{65,1},{2,66},{66,2},{3,67},{67,3},{4,68},{68... | collective-permute-start | bytes 1228808 | tf_op jit(solution)/shard_map/ppermute | solution.py:34
  72.0 10.1 %collective-permute-start.16 = (bf16[64,3200]{1,0:T(8,128)(2,1)S(1)}, bf16[64,3200]{1,0:T(8,128)(2,1)S(1)}, u32[]{:S(2)}, u32[]{:S(2)}) collective-permute-start(bf16[64,3200]{1,0:T(8,128)(2,1)S(1)} %bitcast.158), channel_id=1, source_target_pairs={{0,64},{64,0},{1,65},{65,1},{2,66},{66,2},{3,67},{67,3},{4,68},{68... | collective-permute-start | bytes 1228808 | tf_op jit(solution)/shard_map/ppermute | solution.py:34
  75.9 4.2 %collective-permute-start.13 = (bf16[64,3200]{1,0:T(8,128)(2,1)S(1)}, bf16[64,3200]{1,0:T(8,128)(2,1)S(1)}, u32[]{:S(2)}, u32[]{:S(2)}) collective-permute-start(bf16[64,3200]{1,0:T(8,128)(2,1)S(1)} %bitcast.171), channel_id=1, source_target_pairs={{0,64},{64,0},{1,65},{65,1},{2,66},{66,2},{3,67},{67,3},{4,68},{68... | collective-permute-start | bytes 1228808 | tf_op jit(solution)/shard_map/ppermute | solution.py:34
  78.1 2.7 %collective-permute-start.14 = (bf16[64,3200]{1,0:T(8,128)(2,1)S(1)}, bf16[64,3200]{1,0:T(8,128)(2,1)S(1)}, u32[]{:S(2)}, u32[]{:S(2)}) collective-permute-start(bf16[64,3200]{1,0:T(8,128)(2,1)S(1)} %bitcast.169), channel_id=1, source_target_pairs={{0,64},{64,0},{1,65},{65,1},{2,66},{66,2},{3,67},{67,3},{4,68},{68... | collective-permute-start | bytes 1228808 | tf_op jit(solution)/shard_map/ppermute | solution.py:34
  82.8 0.7 copy-start.3
  84.0 2.6 %collective-permute-start.22 = (bf16[128,3072]{1,0:T(8,128)(2,1)S(1)}, bf16[128,3072]{1,0:T(8,128)(2,1)S(1)}, u32[]{:S(2)}, u32[]{:S(2)}) collective-permute-start(bf16[128,3072]{1,0:T(8,128)(2,1)S(1)} %fusion.3), channel_id=1, source_target_pairs={{0,64},{64,0},{1,65},{65,1},{2,66},{66,2},{3,67},{67,3},{4,68},{68... | collective-permute-start | bytes 2359304 | tf_op jit(solution)/shard_map/ppermute | solution.py:34
  84.5 9.1 %collective-permute-start.17 = (bf16[128,3072]{1,0:T(8,128)(2,1)S(1)}, bf16[128,3072]{1,0:T(8,128)(2,1)S(1)}, u32[]{:S(2)}, u32[]{:S(2)}) collective-permute-start(bf16[128,3072]{1,0:T(8,128)(2,1)S(1)} %fusion), channel_id=1, source_target_pairs={{0,64},{64,0},{1,65},{65,1},{2,66},{66,2},{3,67},{67,3},{4,68},{68... | collective-permute-start | bytes 2359304 | tf_op jit(solution)/shard_map/ppermute | solution.py:34
  85.5 7.5 %collective-permute-start.18 = (bf16[128,3072]{1,0:T(8,128)(2,1)S(1)}, bf16[128,3072]{1,0:T(8,128)(2,1)S(1)}, u32[]{:S(2)}, u32[]{:S(2)}) collective-permute-start(bf16[128,3072]{1,0:T(8,128)(2,1)S(1)} %fusion.1), channel_id=1, source_target_pairs={{0,64},{64,0},{1,65},{65,1},{2,66},{66,2},{3,67},{67,3},{4,68},{68... | collective-permute-start | bytes 2359304 | tf_op jit(solution)/shard_map/ppermute | solution.py:34
  86.0 3.8 %collective-permute-start.19 = (bf16[128,3072]{1,0:T(8,128)(2,1)S(1)}, bf16[128,3072]{1,0:T(8,128)(2,1)S(1)}, u32[]{:S(2)}, u32[]{:S(2)}) collective-permute-start(bf16[128,3072]{1,0:T(8,128)(2,1)S(1)} %fusion.2), channel_id=1, source_target_pairs={{0,64},{64,0},{1,65},{65,1},{2,66},{66,2},{3,67},{67,3},{4,68},{68... | collective-permute-start | bytes 2359304 | tf_op jit(solution)/shard_map/ppermute | solution.py:34
  87.1 19.8 %collective-permute-start.23 = (bf16[2,32,3072]{2,1,0:T(8,128)(2,1)S(1)}, bf16[2,32,3072]{2,1,0:T(8,128)(2,1)S(1)}, u32[]{:S(2)}, u32[]{:S(2)}) collective-permute-start(bf16[2,32,3072]{2,1,0:T(8,128)(2,1)S(1)} %bitcast.173), channel_id=1, source_target_pairs={{0,48},{1,49},{2,50},{3,51},{4,52},{5,53},{6,54},{7,55},{16,0},{17... | collective-permute-start | bytes 1179656 | tf_op jit(solution)/shard_map/ppermute | solution.py:30
  90.3 11.5 %collective-permute-start.20 = (bf16[2,32,3072]{2,1,0:T(8,128)(2,1)S(1)}, bf16[2,32,3072]{2,1,0:T(8,128)(2,1)S(1)}, u32[]{:S(2)}, u32[]{:S(2)}) collective-permute-start(bf16[2,32,3072]{2,1,0:T(8,128)(2,1)S(1)} %bitcast.174), channel_id=1, source_target_pairs={{0,16},{1,17},{2,18},{3,19},{4,20},{5,21},{6,22},{7,23},{16,32},{1... | collective-permute-start | bytes 1179656 | tf_op jit(solution)/shard_map/ppermute | solution.py:30
  90.3 8.2 %collective-permute-start.26 = (bf16[2,32,3072]{2,1,0:T(8,128)(2,1)S(1)}, bf16[2,32,3072]{2,1,0:T(8,128)(2,1)S(1)}, u32[]{:S(2)}, u32[]{:S(2)}) collective-permute-start(bf16[2,32,3072]{2,1,0:T(8,128)(2,1)S(1)} %bitcast.176), channel_id=1, source_target_pairs={{0,48},{1,49},{2,50},{3,51},{4,52},{5,53},{6,54},{7,55},{16,0},{17... | collective-permute-start | bytes 1179656 | tf_op jit(solution)/shard_map/ppermute | solution.py:30
  93.5 9.2 %collective-permute-start.25 = (bf16[2,32,3072]{2,1,0:T(8,128)(2,1)S(1)}, bf16[2,32,3072]{2,1,0:T(8,128)(2,1)S(1)}, u32[]{:S(2)}, u32[]{:S(2)}) collective-permute-start(bf16[2,32,3072]{2,1,0:T(8,128)(2,1)S(1)} %bitcast.175), channel_id=1, source_target_pairs={{0,16},{1,17},{2,18},{3,19},{4,20},{5,21},{6,22},{7,23},{16,32},{1... | collective-permute-start | bytes 1179656 | tf_op jit(solution)/shard_map/ppermute | solution.py:30
  98.6 7.9 %collective-permute-start.27 = (bf16[2,32,3072]{2,1,0:T(8,128)(2,1)S(1)}, bf16[2,32,3072]{2,1,0:T(8,128)(2,1)S(1)}, u32[]{:S(2)}, u32[]{:S(2)}) collective-permute-start(bf16[2,32,3072]{2,1,0:T(8,128)(2,1)S(1)} %fusion.46), channel_id=1, source_target_pairs={{0,48},{1,49},{2,50},{3,51},{4,52},{5,53},{6,54},{7,55},{16,0},{17... | collective-permute-start | bytes 1179656 | tf_op jit(solution)/shard_map/ppermute | solution.py:30
  101.9 8.2 %collective-permute-start.21 = (bf16[2,32,3072]{2,1,0:T(8,128)(2,1)S(1)}, bf16[2,32,3072]{2,1,0:T(8,128)(2,1)S(1)}, u32[]{:S(2)}, u32[]{:S(2)}) collective-permute-start(bf16[2,32,3072]{2,1,0:T(8,128)(2,1)S(1)} %fusion.49), channel_id=1, source_target_pairs={{0,16},{1,17},{2,18},{3,19},{4,20},{5,21},{6,22},{7,23},{16,32},{1... | collective-permute-start | bytes 1179656 | tf_op jit(solution)/shard_map/ppermute | solution.py:30
  106.7 4.9 %collective-permute-start.29 = (bf16[32,3072]{1,0:T(8,128)(2,1)S(1)}, bf16[32,3072]{1,0:T(8,128)(2,1)S(1)}, u32[]{:S(2)}, u32[]{:S(2)}) collective-permute-start(bf16[32,3072]{1,0:T(8,128)(2,1)S(1)} %get-tuple-element.18), channel_id=1, source_target_pairs={{0,136},{1,137},{2,138},{3,139},{4,140},{5,141},{6,142},{7,143},{1... | collective-permute-start | bytes 589832 | tf_op jit(solution)/shard_map/ppermute | solution.py:30
  106.8 6.2 %collective-permute-start.28 = (bf16[32,3072]{1,0:T(8,128)(2,1)S(1)}, bf16[32,3072]{1,0:T(8,128)(2,1)S(1)}, u32[]{:S(2)}, u32[]{:S(2)}) collective-permute-start(bf16[32,3072]{1,0:T(8,128)(2,1)S(1)} %get-tuple-element.17), channel_id=1, source_target_pairs={{0,8},{1,9},{2,10},{3,11},{4,12},{5,13},{6,14},{7,15},{16,24},{17,... | collective-permute-start | bytes 589832 | tf_op jit(solution)/shard_map/ppermute | solution.py:30
  110.2 6.1 %collective-permute-start.24 = (bf16[32,3072]{1,0:T(8,128)(2,1)S(1)}, bf16[32,3072]{1,0:T(8,128)(2,1)S(1)}, u32[]{:S(2)}, u32[]{:S(2)}) collective-permute-start(bf16[32,3072]{1,0:T(8,128)(2,1)S(1)} %fusion.56), channel_id=1, source_target_pairs={{0,128},{1,129},{2,130},{3,131},{4,132},{5,133},{6,134},{7,135},{1... | collective-permute-start | bytes 589832 | tf_op jit(solution)/shard_map/ppermute | solution.py:30

commit v3 on v2

--- a/solution.py
+++ b/solution.py
@@ -3,6 +3,7 @@
 from jax import lax
 from jax.sharding import Mesh
 from jax.sharding import PartitionSpec as P
+
 
 AXES = ("xl", "c", "y", "xh", "z")
 SIZES = (2, 2, 4, 2, 8)
@@ -41,7 +42,7 @@
     from_right_one = move(one, first, -1)
     far_one = move(from_left_one, first, 1)
     far_two = move(from_right_two, first, -1)
-    return [one, two, from_right_one, from_right_two, far_one, far_two, from_left_one, from_left_two]
+    return [one, two, from_right_one, from_right_two, from_left_one, from_left_two, far_one, far_two]
 
 
 def add(*terms):
@@ -52,7 +53,7 @@
 
 
 def ring_reduce(blocks, first):
-    own, right, far, left = blocks
+    own, right, left, far = blocks
     half = own.shape[0] // 2
     to_right = move(far[:half], first, 1)
     to_left = move(far[half:], first, -1)
@@ -82,15 +83,10 @@
     share = jnp.sum(jnp.where(chosen, mix_weights[:, :, None], 0.0), axis=1)
     extra = jnp.pad(parts(share), ((0, 0), (0, PAD - 12)))
     sides = [jnp.concatenate([tokens[:, i * half:(i + 1) * half], extra], axis=1) for i in range(2)]
-    outgoing = jnp.stack([sides[0]] * 8 + [sides[1]] * 8, axis=0)
+    outgoing = jnp.broadcast_to(jnp.stack(sides)[:, None], (2, 8) + sides[0].shape).reshape((16,) + sides[0].shape)
     tile = lax.all_to_all(outgoing, ("c", "z"), split_axis=0, concat_axis=0, tiled=True)
     tile = tile.reshape(16 * tok_rows, half + PAD)
     rows = tile.shape[0]
-    tiles = [tile] + [move(tile, True, step) for step in (-1, 2, 1)]
-    one = jnp.stack(tiles[:2], axis=0)
-    two = jnp.stack(tiles[2:], axis=0)
-    mine = [v.reshape(2 * rows, half + PAD) for v in ring_gather(one, two, False)]
-    other = [swap(v) for v in mine]
 
     def halves(w, axis):
         own = lax.dynamic_slice_in_dim(w, core * half, half, axis)
@@ -100,6 +96,17 @@
     w_in = jnp.concatenate([gate_weight[0], up_weight[0]], axis=1)
     in_own, in_rest = [jnp.pad(w, ((0, PAD), (0, 0))) for w in halves(w_in, 0)]
     down_own, down_rest = halves(down_weight[0], 1)
+    tile, in_own, in_rest = lax.optimization_barrier((tile, in_own, in_rest))
+    tiles = [tile]
+    for step in (-1, 1, 2):
+        tiles.append(move(tile, True, step))
+    one = jnp.stack(tiles[:2], axis=0)
+    two = jnp.stack(tiles[2:], axis=0)
+    mine = [v.reshape(2 * rows, half + PAD) for v in ring_gather(one, two, False)]
+    other = []
+    for v in mine:
+        other.append(swap(v))
+
     n = RING * RING * rows
     units = gate_weight.shape[2]
 
@@ -107,9 +114,14 @@
         return v.reshape(RING, RING, rows, v.shape[-1]).swapaxes(0, 1).reshape(n, v.shape[-1])
 
     def product(pieces, w):
-        return jnp.concatenate([jnp.dot(v, w, preferred_element_type=jnp.float32) for v in pieces], axis=0)
+        parts = []
+        for v in pieces:
+            parts.append(jnp.dot(v, w, preferred_element_type=jnp.float32))
+        return jnp.concatenate(parts, axis=0)
 
-    act = product(mine, in_own) + turned(product(other, in_rest))
+    act_own = product(mine, in_own)
+    act_rest = product(other, in_rest)
+    act = act_own + turned(act_rest)
     hidden = (jax.nn.silu(act[:, :units]) * act[:, units:]).astype(jnp.bfloat16)
     hidden_rest = turned(hidden)
 
@@ -123,16 +135,16 @@
     scale_own, scale_rest = scale_of(mine), scale_of(other)
     per = n // RING
     blocks = [None] * RING
-    for d in (2, 1, 3, 0):
+    for d in (3, 1, 2, 0):
         span = slice(d * per, (d + 1) * per)
         rest = jnp.dot(hidden_rest[span], down_rest, preferred_element_type=jnp.float32) * scale_rest[span]
         came = swap(rest.astype(jnp.bfloat16))
         own = jnp.dot(hidden[span], down_own, preferred_element_type=jnp.float32) * scale_own[span]
         blocks[d] = add(own, came).astype(jnp.bfloat16).reshape(RING, rows, half)
     one, two = ring_reduce(blocks, False)
+    from_far = move(two[1].astype(jnp.bfloat16), True, 2)
     from_left = move(one[1].astype(jnp.bfloat16), True, 1)
-    from_far = move(two[0].astype(jnp.bfloat16), True, 2)
-    from_right = move(two[1].astype(jnp.bfloat16), True, -1)
+    from_right = move(two[0].astype(jnp.bfloat16), True, -1)
     last = add(one[0], from_left, from_far, from_right).astype(jnp.bfloat16)
     back = lax.all_to_all(last.reshape(16, tok_rows, half), ("c", "z"), split_axis=0, concat_axis=0, tiled=True)
     total = jnp.sum(back.reshape(2, 8, tok_rows, half).astype(jnp.float32), axis=1)

time: 135 us -> 118 us (0.87)
  other arithmetic: 20.2 us -> 6.16 us
  waiting for transfers between devices: 35.5 us -> 27.5 us
  local copies, waits for them, and re-layouts: 2.34 us -> 6.12 us
  starting transfers between devices: 42.9 us -> 44.3 us
    unnamed x15 -> x0, other arithmetic: 9.14 us -> none
    all_to_all x1, waiting for transfers between devices: 8.41 us -> 1.53 us  [shards(): lax.all_to_all(outgoing, ('c', 'z'), split_axis=0, concat_axis=0, tiled=T...]
    ppermute x18, starting transfers between devices: 19.9 us -> 25.2 us  [move(): return lax.ppermute(v, AXES, ring_perm(first, step))]
    pad x0 -> x2, local copies, waits for them, and re-layouts: none -> 3.83 us  [shards(): in_own, in_rest = [jnp.pad(w, ((0, PAD), (0, 0))) for w in halves(w_in, 0)]]
    ppermute x12, starting transfers between devices: 12.9 us -> 9.18 us  [swap(): return lax.ppermute(v, 'c', [(0, 1), (1, 0)])]
    concatenate x1, other arithmetic: 4.77 us -> 3.04 us  [shards(): w_in = jnp.concatenate([gate_weight[0], up_weight[0]], axis=1)]
  transfers between devices with their start and end apart: 31 -> 31, of which waited for: 11 -> 11; matrix products, arithmetic and copies ran while one was open for 17% -> 19% of each run, Pallas kernels for 0% -> 0%
where the time goes in v3:
time: 118 us; the launch traced here: 117 us
  starting transfers between devices  44.3 us (38%)
  waiting for transfers between devices  27.5 us (23%)
  blocking collectives  16.1 us (14%)
  matrix products  15.9 us (13%)
  other arithmetic  6.16 us (5%)
  local copies, waits for them, and re-layouts  6.12 us (5%)
    ppermute x18, waiting for transfers between devices, move(): return lax.ppermute(v, AXES, ring_perm(first, step))  25.9 us
    ppermute x18, starting transfers between devices, move(): return lax.ppermute(v, AXES, ring_perm(first, step))  25.2 us
    all_to_all x1, blocking collectives, shards(): lax.all_to_all(last.reshape(16, tok_rows, half), ('c', 'z'), split_axis=0...  16.1 us
    dot_general x16, matrix products, product(): parts.append(jnp.dot(v, w, preferred_element_type=jnp.float32))  12.7 us
    all_to_all x1, starting transfers between devices, shards(): lax.all_to_all(outgoing, ('c', 'z'), split_axis=0, concat_axis=0, tiled=T...  9.97 us
    ppermute x12, starting transfers between devices, swap(): return lax.ppermute(v, 'c', [(0, 1), (1, 0)])  9.18 us
    pad x2, local copies, waits for them, and re-layouts, shards(): in_own, in_rest = [jnp.pad(w, ((0, PAD), (0, 0))) for w in halves(w_in, 0)]  3.83 us
    concatenate x1, other arithmetic, shards(): w_in = jnp.concatenate([gate_weight[0], up_weight[0]], axis=1)  3.04 us
  transfers between devices with their start and end apart: 31, of which 11 were waited for; matrix products, arithmetic and copies ran while one was open for 19% of the time, Pallas kernels for 0%

profile of v3, /device:TPU:1, one launch (start us, length us, event | category | flops | bytes accessed | tf_op | source)
XLA Modules:
  0.0 116.8 jit_solution(2852484126553944655)
XLA Ops:
  0.0 0.9 fusion.47
  0.9 0.8 fusion.67
  1.9 0.8 broadcast_in_dim.43
  2.7 10.0 %all-to-all-start = ((bf16[16,2,3200]{2,1,0:T(2,128)(2,1)}), bf16[16,2,3200]{2,1,0:T(2,128)(2,1)S(1)}, u32[]{:S(2)}, u32[]{:S(2)}) async-start(bf16[16,2,3200]{2,1,0:T(2,128)(2,1)} %bitcast.2), calls=%async_computation | async-start | bytes 409600 | tf_op jit(solution)/shard_map/all_to_all | solution.py:87
  12.7 3.0 %fusion.4 = (bf16[3072,512]{1,0:T(8,128)(2,1)S(1)}, bf16[3072,512]{1,0:T(8,128)(2,1)S(1)}) fusion(s32[]{:T(128)S(6)} %select_n.32, bf16[6144,256]{1,0:T(8,128)(2,1)} %bitcast.127, bf16[6144,256]{1,0:T(8,128)(2,1)} %bitcast.128, s32[]{:T(128)S(6)} %select_n.31), kind=kLoop, calls=%fused_computation.16 | loop fusion | flops 12582912 | bytes 12582920 | tf_op jit(solution)/shard_map/concatenate | solution.py:96
  15.7 1.9 %pad.12 = bf16[3200,512]{1,0:T(8,128)(2,1)} pad(bf16[3072,512]{1,0:T(8,128)(2,1)S(1)} %get-tuple-element.14, bf16[]{:T(256)} %constant.33.clone.1), padding=0_128x0_0 | pad | bytes 6422530 | tf_op jit(solution)/shard_map/jit(_pad)/pad | solution.py:97
  17.6 1.9 %pad.13 = bf16[3200,512]{1,0:T(8,128)(2,1)} pad(bf16[3072,512]{1,0:T(8,128)(2,1)S(1)} %get-tuple-element.13, bf16[]{:T(256)} %constant.33.clone.1), padding=0_128x0_0 | pad | bytes 6422530 | tf_op jit(solution)/shard_map/jit(_pad)/pad | solution.py:97
  19.5 1.5 %all-to-all-done = bf16[16,2,3200]{2,1,0:T(2,128)(2,1)S(1)} async-done(((bf16[16,2,3200]{2,1,0:T(2,128)(2,1)}), bf16[16,2,3200]{2,1,0:T(2,128)(2,1)S(1)}, u32[]{:S(2)}, u32[]{:S(2)}) %all-to-all-start) | async-done | bytes 204832 | tf_op jit(solution)/shard_map/all_to_all | solution.py:87
  21.1 2.8 %collective-permute-start = (bf16[32,3200]{1,0:T(8,128)(2,1)S(1)}, bf16[32,3200]{1,0:T(8,128)(2,1)S(1)}, u32[]{:S(2)}, u32[]{:S(2)}) collective-permute-start(bf16[32,3200]{1,0:T(8,128)(2,1)S(1)} %reshape.108), channel_id=1, source_target_pairs={{0,136},{1,137},{2,138},{3,139},{4,140},{5,141},{6,142},{7,143},{1... | collective-permute-start | bytes 614408 | tf_op jit(solution)/shard_map/ppermute | solution.py:31
  24.4 0.7 collective-permute-start.1
  25.1 3.8 %collective-permute-done = bf16[32,3200]{1,0:T(8,128)(2,1)S(1)} collective-permute-done((bf16[32,3200]{1,0:T(8,128)(2,1)S(1)}, bf16[32,3200]{1,0:T(8,128)(2,1)S(1)}, u32[]{:S(2)}, u32[]{:S(2)}) %collective-permute-start) | collective-permute-done | bytes 204832 | tf_op jit(solution)/shard_map/ppermute | solution.py:31
  28.9 2.6 %collective-permute-start.3 = (bf16[2,32,3200]{2,1,0:T(8,128)(2,1)S(1)}, bf16[2,32,3200]{2,1,0:T(8,128)(2,1)S(1)}, u32[]{:S(2)}, u32[]{:S(2)}) collective-permute-start(bf16[2,32,3200]{2,1,0:T(8,128)(2,1)S(1)} %pad_maximum_fusion), channel_id=1, source_target_pairs={{0,48},{1,49},{2,50},{3,51},{4,52},{5,53},{6,54},{7,55},{16,0},{17... | collective-permute-start | bytes 1228808 | tf_op jit(solution)/shard_map/ppermute | solution.py:31
  31.5 1.2 %collective-permute-done.1 = bf16[32,3200]{1,0:T(8,128)(2,1)S(1)} collective-permute-done((bf16[32,3200]{1,0:T(8,128)(2,1)S(1)}, bf16[32,3200]{1,0:T(8,128)(2,1)S(1)}, u32[]{:S(2)}, u32[]{:S(2)}) %collective-permute-start.1) | collective-permute-done | bytes 204832 | tf_op jit(solution)/shard_map/ppermute | solution.py:31
  32.7 2.3 %collective-permute-start.4 = (bf16[2,32,3200]{2,1,0:T(8,128)(2,1)S(1)}, bf16[2,32,3200]{2,1,0:T(8,128)(2,1)S(1)}, u32[]{:S(2)}, u32[]{:S(2)}) collective-permute-start(bf16[2,32,3200]{2,1,0:T(8,128)(2,1)S(1)} %pad_maximum_fusion.1), channel_id=1, source_target_pairs={{0,48},{1,49},{2,50},{3,51},{4,52},{5,53},{6,54},{7,55},{16,0},{17... | collective-permute-start | bytes 1228808 | tf_op jit(solution)/shard_map/ppermute | solution.py:31
  35.0 3.1 %collective-permute-start.9 = (bf16[64,3200]{1,0:T(8,128)(2,1)S(1)}, bf16[64,3200]{1,0:T(8,128)(2,1)S(1)}, u32[]{:S(2)}, u32[]{:S(2)}) collective-permute-start(bf16[64,3200]{1,0:T(8,128)(2,1)S(1)} %bitcast.130), channel_id=1, source_target_pairs={{0,64},{64,0},{1,65},{65,1},{2,66},{66,2},{3,67},{67,3},{4,68},{68... | collective-permute-start | bytes 1228808 | tf_op jit(solution)/shard_map/ppermute | solution.py:35
  38.1 2.6 %convolution_dynamic-update-slice_fusion.15 = f32[512,512]{1,0:T(8,128)S(1)} fusion(bf16[64,3200]{1,0:T(8,128)(2,1)S(1)} %bitcast.131, bf16[3200,512]{1,0:T(8,128)(2,1)} %pad.12), kind=kOutput, calls=%fused_computation.45 | convolution fusion | flops 209715200 | bytes 3817472 | tf_op jit(solution)/shard_map/dot_general | solution.py:119
  40.7 0.7 convolution_dynamic-update-slice_fusion.14
  41.5 0.7 convolution_dynamic-update-slice_fusion.13
  42.2 1.7 %collective-permute-start.11 = (bf16[64,3200]{1,0:T(8,128)(2,1)S(1)}, bf16[64,3200]{1,0:T(8,128)(2,1)S(1)}, u32[]{:S(2)}, u32[]{:S(2)}) collective-permute-start(bf16[64,3200]{1,0:T(8,128)(2,1)S(1)} %bitcast.149), channel_id=1, source_target_pairs={{0,64},{64,0},{1,65},{65,1},{2,66},{66,2},{3,67},{67,3},{4,68},{68... | collective-permute-start | bytes 1228808 | tf_op jit(solution)/shard_map/ppermute | solution.py:35
  43.9 0.7 convolution_dynamic-update-slice_fusion.12
  44.7 0.7 convolution_dynamic-update-slice_fusion.11
  45.4 1.7 %collective-permute-start.13 = (bf16[64,3200]{1,0:T(8,128)(2,1)S(1)}, bf16[64,3200]{1,0:T(8,128)(2,1)S(1)}, u32[]{:S(2)}, u32[]{:S(2)}) collective-permute-start(bf16[64,3200]{1,0:T(8,128)(2,1)S(1)} %bitcast.143), channel_id=1, source_target_pairs={{0,64},{64,0},{1,65},{65,1},{2,66},{66,2},{3,67},{67,3},{4,68},{68... | collective-permute-start | bytes 1228808 | tf_op jit(solution)/shard_map/ppermute | solution.py:35
  47.2 0.7 convolution_dynamic-update-slice_fusion.10
  48.2 0.7 convolution_dynamic-update-slice_fusion.7
  48.9 3.5 %collective-permute-start.8 = (bf16[2,32,3200]{2,1,0:T(8,128)(2,1)S(1)}, bf16[2,32,3200]{2,1,0:T(8,128)(2,1)S(1)}, u32[]{:S(2)}, u32[]{:S(2)}) collective-permute-start(bf16[2,32,3200]{2,1,0:T(8,128)(2,1)S(1)} %collective-permute-done.4), channel_id=1, source_target_pairs={{0,48},{1,49},{2,50},{3,51},{4,52},{5,53},{6,54},{7,55},{16,0},{17... | collective-permute-start | bytes 1228808 | tf_op jit(solution)/shard_map/ppermute | solution.py:31
  52.3 0.7 convolution_dynamic-update-slice_fusion.6
  53.0 3.9 %collective-permute-done.7 = bf16[2,32,3200]{2,1,0:T(8,128)(2,1)S(1)} collective-permute-done((bf16[2,32,3200]{2,1,0:T(8,128)(2,1)S(1)}, bf16[2,32,3200]{2,1,0:T(8,128)(2,1)S(1)}, u32[]{:S(2)}, u32[]{:S(2)}) %collective-permute-start.7) | collective-permute-done | bytes 409632 | tf_op jit(solution)/shard_map/ppermute | solution.py:31
  57.3 0.7 convolution_dynamic-update-slice_fusion.9
  58.2 0.7 convolution_dynamic-update-slice_fusion.8
  59.4 0.7 convolution_dynamic-update-slice_fusion.5
  60.1 0.7 convolution_dynamic-update-slice_fusion.4
  60.8 0.7 convolution_dynamic-update-slice_fusion.3
  61.5 0.7 convolution_dynamic-update-slice_fusion.2
  62.2 0.7 convolution_dynamic-update-slice_fusion.1
  62.9 0.7 convolution_dynamic-update-slice_fusion
  66.8 0.5 collective-permute-start.19
  67.8 3.5 %collective-permute-start.23 = (bf16[2,32,3072]{2,1,0:T(8,128)(2,1)S(1)}, bf16[2,32,3072]{2,1,0:T(8,128)(2,1)S(1)}, u32[]{:S(2)}, u32[]{:S(2)}) collective-permute-start(bf16[2,32,3072]{2,1,0:T(8,128)(2,1)S(1)} %bitcast.160), channel_id=1, source_target_pairs={{0,48},{1,49},{2,50},{3,51},{4,52},{5,53},{6,54},{7,55},{16,0},{17... | collective-permute-start | bytes 1179656 | tf_op jit(solution)/shard_map/ppermute | solution.py:31
  72.0 2.7 %collective-permute-start.26 = (bf16[2,32,3072]{2,1,0:T(8,128)(2,1)S(1)}, bf16[2,32,3072]{2,1,0:T(8,128)(2,1)S(1)}, u32[]{:S(2)}, u32[]{:S(2)}) collective-permute-start(bf16[2,32,3072]{2,1,0:T(8,128)(2,1)S(1)} %bitcast.163), channel_id=1, source_target_pairs={{0,48},{1,49},{2,50},{3,51},{4,52},{5,53},{6,54},{7,55},{16,0},{17... | collective-permute-start | bytes 1179656 | tf_op jit(solution)/shard_map/ppermute | solution.py:31
  75.8 4.4 %collective-permute-done.26 = bf16[2,32,3072]{2,1,0:T(8,128)(2,1)S(1)} collective-permute-done((bf16[2,32,3072]{2,1,0:T(8,128)(2,1)S(1)}, bf16[2,32,3072]{2,1,0:T(8,128)(2,1)S(1)}, u32[]{:S(2)}, u32[]{:S(2)}) %collective-permute-start.26) | collective-permute-done | bytes 393248 | tf_op jit(solution)/shard_map/ppermute | solution.py:31
  80.2 3.5 %collective-permute-start.27 = (bf16[2,32,3072]{2,1,0:T(8,128)(2,1)S(1)}, bf16[2,32,3072]{2,1,0:T(8,128)(2,1)S(1)}, u32[]{:S(2)}, u32[]{:S(2)}) collective-permute-start(bf16[2,32,3072]{2,1,0:T(8,128)(2,1)S(1)} %fusion.30), channel_id=1, source_target_pairs={{0,48},{1,49},{2,50},{3,51},{4,52},{5,53},{6,54},{7,55},{16,0},{17... | collective-permute-start | bytes 1179656 | tf_op jit(solution)/shard_map/ppermute | solution.py:31
  84.4 4.1 %collective-permute-done.27 = bf16[2,32,3072]{2,1,0:T(8,128)(2,1)S(1)} collective-permute-done((bf16[2,32,3072]{2,1,0:T(8,128)(2,1)S(1)}, bf16[2,32,3072]{2,1,0:T(8,128)(2,1)S(1)}, u32[]{:S(2)}, u32[]{:S(2)}) %collective-permute-start.27) | collective-permute-done | bytes 393248 | tf_op jit(solution)/shard_map/ppermute | solution.py:31
  88.6 2.5 %collective-permute-start.29 = (bf16[32,3072]{1,0:T(8,128)(2,1)S(1)}, bf16[32,3072]{1,0:T(8,128)(2,1)S(1)}, u32[]{:S(2)}, u32[]{:S(2)}) collective-permute-start(bf16[32,3072]{1,0:T(8,128)(2,1)S(1)} %get-tuple-element.24), channel_id=1, source_target_pairs={{0,136},{1,137},{2,138},{3,139},{4,140},{5,141},{6,142},{7,143},{1... | collective-permute-start | bytes 589832 | tf_op jit(solution)/shard_map/ppermute | solution.py:31
  91.2 0.9 collective-permute-done.21
  92.3 3.6 %collective-permute-done.29 = bf16[32,3072]{1,0:T(8,128)(2,1)S(1)} collective-permute-done((bf16[32,3072]{1,0:T(8,128)(2,1)S(1)}, bf16[32,3072]{1,0:T(8,128)(2,1)S(1)}, u32[]{:S(2)}, u32[]{:S(2)}) %collective-permute-start.29) | collective-permute-done | bytes 196640 | tf_op jit(solution)/shard_map/ppermute | solution.py:31
  95.9 1.4 %collective-permute-done.28 = bf16[32,3072]{1,0:T(8,128)(2,1)S(1)} collective-permute-done((bf16[32,3072]{1,0:T(8,128)(2,1)S(1)}, bf16[32,3072]{1,0:T(8,128)(2,1)S(1)}, u32[]{:S(2)}, u32[]{:S(2)}) %collective-permute-start.28) | collective-permute-done | bytes 196640 | tf_op jit(solution)/shard_map/ppermute | solution.py:31
  97.3 2.3 %collective-permute-done.24 = bf16[32,3072]{1,0:T(8,128)(2,1)S(1)} collective-permute-done((bf16[32,3072]{1,0:T(8,128)(2,1)S(1)}, bf16[32,3072]{1,0:T(8,128)(2,1)S(1)}, u32[]{:S(2)}, u32[]{:S(2)}) %collective-permute-start.24) | collective-permute-done | bytes 196640 | tf_op jit(solution)/shard_map/ppermute | solution.py:31
  99.8 16.1 %all_to_all.10 = bf16[16,2,3072]{2,1,0:T(2,128)(2,1)S(1)} all-to-all(bf16[16,2,3072]{2,1,0:T(2,128)(2,1)S(1)} %reshape.120), channel_id=1, replica_groups=mesh['xl'=2,'c'=2,'y'=4,'xh'=2,'z'=8] {'c','z'}, dimensions={0} | all-to-all | bytes 393216 | tf_op jit(solution)/shard_map/all_to_all | solution.py:149
  116.1 0.6 pad_maximum_fusion.3
  (97 shorter events, 9.4 us)
Async XLA Ops:
  0.0 64.3 %copy-start = (bf16[1,256,6144]{2,1,0:T(8,128)(2,1)S(1)}, bf16[1,256,6144]{2,1,0:T(8,128)(2,1)}, u32[]{:S(2)}) copy-start(bf16[1,256,6144]{2,1,0:T(8,128)(2,1)} %param.11) | copy-start | bytes 9437188
  2.7 18.4 %all-to-all-start = ((bf16[16,2,3200]{2,1,0:T(2,128)(2,1)}), bf16[16,2,3200]{2,1,0:T(2,128)(2,1)S(1)}, u32[]{:S(2)}, u32[]{:S(2)}) async-start(bf16[16,2,3200]{2,1,0:T(2,128)(2,1)} %bitcast.2), calls=%async_computation | async-start | bytes 409600 | tf_op jit(solution)/shard_map/all_to_all | solution.py:87
  21.1 7.7 %collective-permute-start = (bf16[32,3200]{1,0:T(8,128)(2,1)S(1)}, bf16[32,3200]{1,0:T(8,128)(2,1)S(1)}, u32[]{:S(2)}, u32[]{:S(2)}) collective-permute-start(bf16[32,3200]{1,0:T(8,128)(2,1)S(1)} %reshape.108), channel_id=1, source_target_pairs={{0,136},{1,137},{2,138},{3,139},{4,140},{5,141},{6,142},{7,143},{1... | collective-permute-start | bytes 614408 | tf_op jit(solution)/shard_map/ppermute | solution.py:31
  24.0 16.7 %copy-start.2 = (bf16[3200,512]{1,0:T(8,128)(2,1)S(1)}, bf16[3200,512]{1,0:T(8,128)(2,1)}, u32[]{:S(2)}) copy-start(bf16[3200,512]{1,0:T(8,128)(2,1)} %pad.12) | copy-start | bytes 9830404
  24.0 7.5 %collective-permute-start.2 = (bf16[32,3200]{1,0:T(8,128)(2,1)S(1)}, bf16[32,3200]{1,0:T(8,128)(2,1)S(1)}, u32[]{:S(2)}, u32[]{:S(2)}) collective-permute-start(bf16[32,3200]{1,0:T(8,128)(2,1)S(1)} %reshape.108), channel_id=1, source_target_pairs={{0,8},{1,9},{2,10},{3,11},{4,12},{5,13},{6,14},{7,15},{16,24},{17,... | collective-permute-start | bytes 614408 | tf_op jit(solution)/shard_map/ppermute | solution.py:31
  24.4 8.3 %collective-permute-start.1 = (bf16[32,3200]{1,0:T(8,128)(2,1)S(1)}, bf16[32,3200]{1,0:T(8,128)(2,1)S(1)}, u32[]{:S(2)}, u32[]{:S(2)}) collective-permute-start(bf16[32,3200]{1,0:T(8,128)(2,1)S(1)} %reshape.108), channel_id=1, source_target_pairs={{0,128},{1,129},{2,130},{3,131},{4,132},{5,133},{6,134},{7,135},{1... | collective-permute-start | bytes 614408 | tf_op jit(solution)/shard_map/ppermute | solution.py:31
  28.9 12.5 %collective-permute-start.3 = (bf16[2,32,3200]{2,1,0:T(8,128)(2,1)S(1)}, bf16[2,32,3200]{2,1,0:T(8,128)(2,1)S(1)}, u32[]{:S(2)}, u32[]{:S(2)}) collective-permute-start(bf16[2,32,3200]{2,1,0:T(8,128)(2,1)S(1)} %pad_maximum_fusion), channel_id=1, source_target_pairs={{0,48},{1,49},{2,50},{3,51},{4,52},{5,53},{6,54},{7,55},{16,0},{17... | collective-permute-start | bytes 1228808 | tf_op jit(solution)/shard_map/ppermute | solution.py:31
  31.5 13.1 %collective-permute-start.5 = (bf16[2,32,3200]{2,1,0:T(8,128)(2,1)S(1)}, bf16[2,32,3200]{2,1,0:T(8,128)(2,1)S(1)}, u32[]{:S(2)}, u32[]{:S(2)}) collective-permute-start(bf16[2,32,3200]{2,1,0:T(8,128)(2,1)S(1)} %pad_maximum_fusion), channel_id=1, source_target_pairs={{0,16},{1,17},{2,18},{3,19},{4,20},{5,21},{6,22},{7,23},{16,32},{1... | collective-permute-start | bytes 1228808 | tf_op jit(solution)/shard_map/ppermute | solution.py:31
  32.7 9.5 %collective-permute-start.4 = (bf16[2,32,3200]{2,1,0:T(8,128)(2,1)S(1)}, bf16[2,32,3200]{2,1,0:T(8,128)(2,1)S(1)}, u32[]{:S(2)}, u32[]{:S(2)}) collective-permute-start(bf16[2,32,3200]{2,1,0:T(8,128)(2,1)S(1)} %pad_maximum_fusion.1), channel_id=1, source_target_pairs={{0,48},{1,49},{2,50},{3,51},{4,52},{5,53},{6,54},{7,55},{16,0},{17... | collective-permute-start | bytes 1228808 | tf_op jit(solution)/shard_map/ppermute | solution.py:31
  35.0 10.4 %collective-permute-start.6 = (bf16[2,32,3200]{2,1,0:T(8,128)(2,1)S(1)}, bf16[2,32,3200]{2,1,0:T(8,128)(2,1)S(1)}, u32[]{:S(2)}, u32[]{:S(2)}) collective-permute-start(bf16[2,32,3200]{2,1,0:T(8,128)(2,1)S(1)} %pad_maximum_fusion.1), channel_id=1, source_target_pairs={{0,16},{1,17},{2,18},{3,19},{4,20},{5,21},{6,22},{7,23},{16,32},{1... | collective-permute-start | bytes 1228808 | tf_op jit(solution)/shard_map/ppermute | solution.py:31
  35.0 12.9 %collective-permute-start.9 = (bf16[64,3200]{1,0:T(8,128)(2,1)S(1)}, bf16[64,3200]{1,0:T(8,128)(2,1)S(1)}, u32[]{:S(2)}, u32[]{:S(2)}) collective-permute-start(bf16[64,3200]{1,0:T(8,128)(2,1)S(1)} %bitcast.130), channel_id=1, source_target_pairs={{0,64},{64,0},{1,65},{65,1},{2,66},{66,2},{3,67},{67,3},{4,68},{68... | collective-permute-start | bytes 1228808 | tf_op jit(solution)/shard_map/ppermute | solution.py:35
  41.4 7.5 %collective-permute-start.10 = (bf16[64,3200]{1,0:T(8,128)(2,1)S(1)}, bf16[64,3200]{1,0:T(8,128)(2,1)S(1)}, u32[]{:S(2)}, u32[]{:S(2)}) collective-permute-start(bf16[64,3200]{1,0:T(8,128)(2,1)S(1)} %bitcast.135), channel_id=1, source_target_pairs={{0,64},{64,0},{1,65},{65,1},{2,66},{66,2},{3,67},{67,3},{4,68},{68... | collective-permute-start | bytes 1228808 | tf_op jit(solution)/shard_map/ppermute | solution.py:35
  42.2 16.7 %collective-permute-start.11 = (bf16[64,3200]{1,0:T(8,128)(2,1)S(1)}, bf16[64,3200]{1,0:T(8,128)(2,1)S(1)}, u32[]{:S(2)}, u32[]{:S(2)}) collective-permute-start(bf16[64,3200]{1,0:T(8,128)(2,1)S(1)} %bitcast.149), channel_id=1, source_target_pairs={{0,64},{64,0},{1,65},{65,1},{2,66},{66,2},{3,67},{67,3},{4,68},{68... | collective-permute-start | bytes 1228808 | tf_op jit(solution)/shard_map/ppermute | solution.py:35
  44.6 15.5 %collective-permute-start.12 = (bf16[64,3200]{1,0:T(8,128)(2,1)S(1)}, bf16[64,3200]{1,0:T(8,128)(2,1)S(1)}, u32[]{:S(2)}, u32[]{:S(2)}) collective-permute-start(bf16[64,3200]{1,0:T(8,128)(2,1)S(1)} %bitcast.153), channel_id=1, source_target_pairs={{0,64},{64,0},{1,65},{65,1},{2,66},{66,2},{3,67},{67,3},{4,68},{68... | collective-permute-start | bytes 1228808 | tf_op jit(solution)/shard_map/ppermute | solution.py:35
  44.7 3.4 %copy-start.1 = (bf16[3200,512]{1,0:T(8,128)(2,1)S(1)}, bf16[3200,512]{1,0:T(8,128)(2,1)}, u32[]{:S(2)}) copy-start(bf16[3200,512]{1,0:T(8,128)(2,1)} %pad.13) | copy-start | bytes 9830404
  45.4 15.4 %collective-permute-start.13 = (bf16[64,3200]{1,0:T(8,128)(2,1)S(1)}, bf16[64,3200]{1,0:T(8,128)(2,1)S(1)}, u32[]{:S(2)}, u32[]{:S(2)}) collective-permute-start(bf16[64,3200]{1,0:T(8,128)(2,1)S(1)} %bitcast.143), channel_id=1, source_target_pairs={{0,64},{64,0},{1,65},{65,1},{2,66},{66,2},{3,67},{67,3},{4,68},{68... | collective-permute-start | bytes 1228808 | tf_op jit(solution)/shard_map/ppermute | solution.py:35
  47.9 9.0 %collective-permute-start.7 = (bf16[2,32,3200]{2,1,0:T(8,128)(2,1)S(1)}, bf16[2,32,3200]{2,1,0:T(8,128)(2,1)S(1)}, u32[]{:S(2)}, u32[]{:S(2)}) collective-permute-start(bf16[2,32,3200]{2,1,0:T(8,128)(2,1)S(1)} %collective-permute-done.5), channel_id=1, source_target_pairs={{0,16},{1,17},{2,18},{3,19},{4,20},{5,21},{6,22},{7,23},{16,32},{1... | collective-permute-start | bytes 1228808 | tf_op jit(solution)/shard_map/ppermute | solution.py:31
  48.9 9.1 %collective-permute-start.8 = (bf16[2,32,3200]{2,1,0:T(8,128)(2,1)S(1)}, bf16[2,32,3200]{2,1,0:T(8,128)(2,1)S(1)}, u32[]{:S(2)}, u32[]{:S(2)}) collective-permute-start(bf16[2,32,3200]{2,1,0:T(8,128)(2,1)S(1)} %collective-permute-done.4), channel_id=1, source_target_pairs={{0,48},{1,49},{2,50},{3,51},{4,52},{5,53},{6,54},{7,55},{16,0},{17... | collective-permute-start | bytes 1228808 | tf_op jit(solution)/shard_map/ppermute | solution.py:31
  56.9 4.6 %collective-permute-start.14 = (bf16[64,3200]{1,0:T(8,128)(2,1)S(1)}, bf16[64,3200]{1,0:T(8,128)(2,1)S(1)}, u32[]{:S(2)}, u32[]{:S(2)}) collective-permute-start(bf16[64,3200]{1,0:T(8,128)(2,1)S(1)} %bitcast.147), channel_id=1, source_target_pairs={{0,64},{64,0},{1,65},{65,1},{2,66},{66,2},{3,67},{67,3},{4,68},{68... | collective-permute-start | bytes 1228808 | tf_op jit(solution)/shard_map/ppermute | solution.py:35
  58.0 4.2 %collective-permute-start.15 = (bf16[64,3200]{1,0:T(8,128)(2,1)S(1)}, bf16[64,3200]{1,0:T(8,128)(2,1)S(1)}, u32[]{:S(2)}, u32[]{:S(2)}) collective-permute-start(bf16[64,3200]{1,0:T(8,128)(2,1)S(1)} %bitcast.155), channel_id=1, source_target_pairs={{0,64},{64,0},{1,65},{65,1},{2,66},{66,2},{3,67},{67,3},{4,68},{68... | collective-permute-start | bytes 1228808 | tf_op jit(solution)/shard_map/ppermute | solution.py:35
  58.9 4.0 %collective-permute-start.16 = (bf16[64,3200]{1,0:T(8,128)(2,1)S(1)}, bf16[64,3200]{1,0:T(8,128)(2,1)S(1)}, u32[]{:S(2)}, u32[]{:S(2)}) collective-permute-start(bf16[64,3200]{1,0:T(8,128)(2,1)S(1)} %bitcast.159), channel_id=1, source_target_pairs={{0,64},{64,0},{1,65},{65,1},{2,66},{66,2},{3,67},{67,3},{4,68},{68... | collective-permute-start | bytes 1228808 | tf_op jit(solution)/shard_map/ppermute | solution.py:35
  64.7 2.6 %collective-permute-start.22 = (bf16[128,3072]{1,0:T(8,128)(2,1)S(1)}, bf16[128,3072]{1,0:T(8,128)(2,1)S(1)}, u32[]{:S(2)}, u32[]{:S(2)}) collective-permute-start(bf16[128,3072]{1,0:T(8,128)(2,1)S(1)} %fusion.3), channel_id=1, source_target_pairs={{0,64},{64,0},{1,65},{65,1},{2,66},{66,2},{3,67},{67,3},{4,68},{68... | collective-permute-start | bytes 2359304 | tf_op jit(solution)/shard_map/ppermute | solution.py:35
  65.3 10.0 %collective-permute-start.17 = (bf16[128,3072]{1,0:T(8,128)(2,1)S(1)}, bf16[128,3072]{1,0:T(8,128)(2,1)S(1)}, u32[]{:S(2)}, u32[]{:S(2)}) collective-permute-start(bf16[128,3072]{1,0:T(8,128)(2,1)S(1)} %fusion), channel_id=1, source_target_pairs={{0,64},{64,0},{1,65},{65,1},{2,66},{66,2},{3,67},{67,3},{4,68},{68... | collective-permute-start | bytes 2359304 | tf_op jit(solution)/shard_map/ppermute | solution.py:35
  66.2 8.5 %collective-permute-start.18 = (bf16[128,3072]{1,0:T(8,128)(2,1)S(1)}, bf16[128,3072]{1,0:T(8,128)(2,1)S(1)}, u32[]{:S(2)}, u32[]{:S(2)}) collective-permute-start(bf16[128,3072]{1,0:T(8,128)(2,1)S(1)} %fusion.1), channel_id=1, source_target_pairs={{0,64},{64,0},{1,65},{65,1},{2,66},{66,2},{3,67},{67,3},{4,68},{68... | collective-permute-start | bytes 2359304 | tf_op jit(solution)/shard_map/ppermute | solution.py:35
  66.8 4.5 %collective-permute-start.19 = (bf16[128,3072]{1,0:T(8,128)(2,1)S(1)}, bf16[128,3072]{1,0:T(8,128)(2,1)S(1)}, u32[]{:S(2)}, u32[]{:S(2)}) collective-permute-start(bf16[128,3072]{1,0:T(8,128)(2,1)S(1)} %fusion.2), channel_id=1, source_target_pairs={{0,64},{64,0},{1,65},{65,1},{2,66},{66,2},{3,67},{67,3},{4,68},{68... | collective-permute-start | bytes 2359304 | tf_op jit(solution)/shard_map/ppermute | solution.py:35
  67.8 23.4 %collective-permute-start.23 = (bf16[2,32,3072]{2,1,0:T(8,128)(2,1)S(1)}, bf16[2,32,3072]{2,1,0:T(8,128)(2,1)S(1)}, u32[]{:S(2)}, u32[]{:S(2)}) collective-permute-start(bf16[2,32,3072]{2,1,0:T(8,128)(2,1)S(1)} %bitcast.160), channel_id=1, source_target_pairs={{0,48},{1,49},{2,50},{3,51},{4,52},{5,53},{6,54},{7,55},{16,0},{17... | collective-permute-start | bytes 1179656 | tf_op jit(solution)/shard_map/ppermute | solution.py:31
  71.7 12.0 %collective-permute-start.20 = (bf16[2,32,3072]{2,1,0:T(8,128)(2,1)S(1)}, bf16[2,32,3072]{2,1,0:T(8,128)(2,1)S(1)}, u32[]{:S(2)}, u32[]{:S(2)}) collective-permute-start(bf16[2,32,3072]{2,1,0:T(8,128)(2,1)S(1)} %bitcast.161), channel_id=1, source_target_pairs={{0,16},{1,17},{2,18},{3,19},{4,20},{5,21},{6,22},{7,23},{16,32},{1... | collective-permute-start | bytes 1179656 | tf_op jit(solution)/shard_map/ppermute | solution.py:31
  72.0 8.1 %collective-permute-start.26 = (bf16[2,32,3072]{2,1,0:T(8,128)(2,1)S(1)}, bf16[2,32,3072]{2,1,0:T(8,128)(2,1)S(1)}, u32[]{:S(2)}, u32[]{:S(2)}) collective-permute-start(bf16[2,32,3072]{2,1,0:T(8,128)(2,1)S(1)} %bitcast.163), channel_id=1, source_target_pairs={{0,48},{1,49},{2,50},{3,51},{4,52},{5,53},{6,54},{7,55},{16,0},{17... | collective-permute-start | bytes 1179656 | tf_op jit(solution)/shard_map/ppermute | solution.py:31
  75.2 9.2 %collective-permute-start.25 = (bf16[2,32,3072]{2,1,0:T(8,128)(2,1)S(1)}, bf16[2,32,3072]{2,1,0:T(8,128)(2,1)S(1)}, u32[]{:S(2)}, u32[]{:S(2)}) collective-permute-start(bf16[2,32,3072]{2,1,0:T(8,128)(2,1)S(1)} %bitcast.162), channel_id=1, source_target_pairs={{0,16},{1,17},{2,18},{3,19},{4,20},{5,21},{6,22},{7,23},{16,32},{1... | collective-permute-start | bytes 1179656 | tf_op jit(solution)/shard_map/ppermute | solution.py:31
  80.2 8.2 %collective-permute-start.27 = (bf16[2,32,3072]{2,1,0:T(8,128)(2,1)S(1)}, bf16[2,32,3072]{2,1,0:T(8,128)(2,1)S(1)}, u32[]{:S(2)}, u32[]{:S(2)}) collective-permute-start(bf16[2,32,3072]{2,1,0:T(8,128)(2,1)S(1)} %fusion.30), channel_id=1, source_target_pairs={{0,48},{1,49},{2,50},{3,51},{4,52},{5,53},{6,54},{7,55},{16,0},{17... | collective-permute-start | bytes 1179656 | tf_op jit(solution)/shard_map/ppermute | solution.py:31
  83.8 8.2 %collective-permute-start.21 = (bf16[2,32,3072]{2,1,0:T(8,128)(2,1)S(1)}, bf16[2,32,3072]{2,1,0:T(8,128)(2,1)S(1)}, u32[]{:S(2)}, u32[]{:S(2)}) collective-permute-start(bf16[2,32,3072]{2,1,0:T(8,128)(2,1)S(1)} %fusion.33), channel_id=1, source_target_pairs={{0,16},{1,17},{2,18},{3,19},{4,20},{5,21},{6,22},{7,23},{16,32},{1... | collective-permute-start | bytes 1179656 | tf_op jit(solution)/shard_map/ppermute | solution.py:31
  88.6 7.2 %collective-permute-start.29 = (bf16[32,3072]{1,0:T(8,128)(2,1)S(1)}, bf16[32,3072]{1,0:T(8,128)(2,1)S(1)}, u32[]{:S(2)}, u32[]{:S(2)}) collective-permute-start(bf16[32,3072]{1,0:T(8,128)(2,1)S(1)} %get-tuple-element.24), channel_id=1, source_target_pairs={{0,136},{1,137},{2,138},{3,139},{4,140},{5,141},{6,142},{7,143},{1... | collective-permute-start | bytes 589832 | tf_op jit(solution)/shard_map/ppermute | solution.py:31
  91.2 6.1 %collective-permute-start.28 = (bf16[32,3072]{1,0:T(8,128)(2,1)S(1)}, bf16[32,3072]{1,0:T(8,128)(2,1)S(1)}, u32[]{:S(2)}, u32[]{:S(2)}) collective-permute-start(bf16[32,3072]{1,0:T(8,128)(2,1)S(1)} %get-tuple-element.23), channel_id=1, source_target_pairs={{0,8},{1,9},{2,10},{3,11},{4,12},{5,13},{6,14},{7,15},{16,24},{17,... | collective-permute-start | bytes 589832 | tf_op jit(solution)/shard_map/ppermute | solution.py:31
  92.2 7.4 %collective-permute-start.24 = (bf16[32,3072]{1,0:T(8,128)(2,1)S(1)}, bf16[32,3072]{1,0:T(8,128)(2,1)S(1)}, u32[]{:S(2)}, u32[]{:S(2)}) collective-permute-start(bf16[32,3072]{1,0:T(8,128)(2,1)S(1)} %fusion.40), channel_id=1, source_target_pairs={{0,128},{1,129},{2,130},{3,131},{4,132},{5,133},{6,134},{7,135},{1... | collective-permute-start | bytes 589832 | tf_op jit(solution)/shard_map/ppermute | solution.py:31

commit v4 on v3

--- a/solution.py
+++ b/solution.py
@@ -1,6 +1,8 @@
 import jax
 import jax.numpy as jnp
 from jax import lax
+from jax.experimental import pallas as pl
+from jax.experimental.pallas import tpu as pltpu
 from jax.sharding import Mesh
 from jax.sharding import PartitionSpec as P
 
@@ -66,11 +68,41 @@
     return one, two
 
 
-def parts(w):
-    high = lax.reduce_precision(w, 8, 7)
-    mid = lax.reduce_precision(w - high, 8, 7)
-    low = w - high - mid
-    return jnp.concatenate([high, mid, low], axis=1).astype(jnp.bfloat16)
+def prepare_kernel(routing, weights, tokens, out):
+    rows, width = tokens.shape
+    half = width // 2
+    lane = lax.broadcasted_iota(jnp.int32, (rows, PAD), 1)
+    row = lax.broadcasted_iota(jnp.int32, (rows, PAD), 0)
+    share = jnp.zeros((rows, PAD), jnp.float32)
+    for t in range(rows):
+        for k in range(2):
+            here = (row == t) & (lane % 4 == routing[t, k])
+            share = jnp.where(here, weights[t, k], share)
+    high = share.astype(jnp.bfloat16).astype(jnp.float32)
+    mid = (share - high).astype(jnp.bfloat16).astype(jnp.float32)
+    low = share - high - mid
+    extra = jnp.where(lane < 4, high, jnp.where(lane < 8, mid, jnp.where(lane < 12, low, 0.0)))
+    extra = extra.astype(jnp.bfloat16)
+    for core in range(2):
+        side = tokens[:, core * half:(core + 1) * half]
+        for copy in range(8):
+            out[core * 8 + copy, :, :half] = side
+            out[core * 8 + copy, :, half:] = extra
+
+
+def prepare(tokens, routing, mix_weights):
+    rows, width = tokens.shape
+    return pl.pallas_call(
+        prepare_kernel,
+        out_shape=jax.ShapeDtypeStruct((16, rows, width // 2 + PAD), jnp.bfloat16),
+        in_specs=[
+            pl.BlockSpec(memory_space=pltpu.SMEM),
+            pl.BlockSpec(memory_space=pltpu.SMEM),
+            pl.BlockSpec(memory_space=pltpu.VMEM),
+        ],
+        out_specs=pl.BlockSpec(memory_space=pltpu.VMEM),
+        name="prepare",
+    )(routing, mix_weights, tokens)
 
 
 def shards(tokens, routing, mix_weights, gate_weight, up_weight, down_weight):
@@ -78,12 +110,7 @@
     half = width // 2
     core = lax.axis_index("c")
     expert = lax.axis_index("xl") * 2 + core
-    experts = jnp.arange(4, dtype=jnp.int32)
-    chosen = routing[:, :, None] == experts[None, None, :]
-    share = jnp.sum(jnp.where(chosen, mix_weights[:, :, None], 0.0), axis=1)
-    extra = jnp.pad(parts(share), ((0, 0), (0, PAD - 12)))
-    sides = [jnp.concatenate([tokens[:, i * half:(i + 1) * half], extra], axis=1) for i in range(2)]
-    outgoing = jnp.broadcast_to(jnp.stack(sides)[:, None], (2, 8) + sides[0].shape).reshape((16,) + sides[0].shape)
+    outgoing = prepare(tokens, routing, mix_weights)
     tile = lax.all_to_all(outgoing, ("c", "z"), split_axis=0, concat_axis=0, tiled=True)
     tile = tile.reshape(16 * tok_rows, half + PAD)
     rows = tile.shape[0]
@@ -94,7 +121,7 @@
         return own, rest
 
     w_in = jnp.concatenate([gate_weight[0], up_weight[0]], axis=1)
-    in_own, in_rest = [jnp.pad(w, ((0, PAD), (0, 0))) for w in halves(w_in, 0)]
+    in_own, in_rest = halves(w_in, 0)
     down_own, down_rest = halves(down_weight[0], 1)
     tile, in_own, in_rest = lax.optimization_barrier((tile, in_own, in_rest))
     tiles = [tile]
@@ -116,7 +143,7 @@
     def product(pieces, w):
         parts = []
         for v in pieces:
-            parts.append(jnp.dot(v, w, preferred_element_type=jnp.float32))
+            parts.append(jnp.dot(v[:, :half], w, preferred_element_type=jnp.float32))
         return jnp.concatenate(parts, axis=0)
 
     act_own = product(mine, in_own)

time: 118 us -> 116 us (0.983)
  local copies, waits for them, and re-layouts: 6.12 us -> 0.71 us
  waiting for transfers between devices: 27.5 us -> 29.4 us
  Pallas kernels: 0 us -> 1.62 us
    pad x2 -> x0, local copies, waits for them, and re-layouts: 3.83 us -> none  [shards(): in_own, in_rest = [jnp.pad(w, ((0, PAD), (0, 0))) for w in halves(w_in, 0)]]
    all_to_all x1, waiting for transfers between devices: 1.53 us -> 3.64 us  [shards(): lax.all_to_all(outgoing, ('c', 'z'), split_axis=0, concat_axis=0, tiled=T...]
    concatenate x1, other arithmetic: 3.04 us -> 4.77 us  [shards(): w_in = jnp.concatenate([gate_weight[0], up_weight[0]], axis=1)]
    pallas_call x0 -> x1, Pallas kernels: none -> 1.62 us  [prepare(): pl.pallas_call(prepare_kernel, out_shape=jax.ShapeDtypeStruct((16, rows,...]
  transfers between devices with their start and end apart: 31 -> 31, of which waited for: 11 -> 11; matrix products, arithmetic and copies ran while one was open for 19% -> 18% of each run, Pallas kernels for 0% -> 0%
where the time goes in v4:
time: 116 us; the launch traced here: 115 us
  starting transfers between devices  44.7 us (39%)
  waiting for transfers between devices  29.4 us (25%)
  matrix products  15.5 us (13%)
  blocking collectives  15.3 us (13%)
  other arithmetic  6.83 us (6%)
  Pallas kernels  1.62 us (1%)
    ppermute x18, waiting for transfers between devices, move(): return lax.ppermute(v, AXES, ring_perm(first, step))  25.8 us
    ppermute x18, starting transfers between devices, move(): return lax.ppermute(v, AXES, ring_perm(first, step))  25.4 us
    all_to_all x1, blocking collectives, shards(): lax.all_to_all(last.reshape(16, tok_rows, half), ('c', 'z'), split_axis=0...  15.3 us
    dot_general x16, matrix products, product(): parts.append(jnp.dot(v[:, :half], w, preferred_element_type=jnp.float32))  12.2 us
    all_to_all x1, starting transfers between devices, shards(): lax.all_to_all(outgoing, ('c', 'z'), split_axis=0, concat_axis=0, tiled=T...  9.97 us
    ppermute x12, starting transfers between devices, swap(): return lax.ppermute(v, 'c', [(0, 1), (1, 0)])  9.35 us
    concatenate x1, other arithmetic, shards(): w_in = jnp.concatenate([gate_weight[0], up_weight[0]], axis=1)  4.77 us
    all_to_all x1, waiting for transfers between devices, shards(): lax.all_to_all(outgoing, ('c', 'z'), split_axis=0, concat_axis=0, tiled=T...  3.64 us
  transfers between devices with their start and end apart: 31, of which 11 were waited for; matrix products, arithmetic and copies ran while one was open for 18% of the time, Pallas kernels for 0%

profile of v4, /device:TPU:1, one launch (start us, length us, event | category | flops | bytes accessed | tf_op | source)
XLA Modules:
  0.0 114.7 jit_solution(12255180672706606584)
XLA Ops:
  0.0 1.6 %prepare.1 = bf16[16,2,3200]{2,1,0:T(2,128)(2,1)} custom-call(s32[2,2]{1,0:T(2,128)} %routing.1, f32[2,2]{1,0:T(2,128)} %weights.1, bf16[2,6144]{1,0:T(2,128)(2,1)} %tokens.1), custom_call_target="tpu_custom_call" | custom-call | tf_op jit(solution)/shard_map/prepare/pallas_call | solution.py:95
  1.6 10.0 %all-to-all-start = ((bf16[16,2,3200]{2,1,0:T(2,128)(2,1)}), bf16[16,2,3200]{2,1,0:T(2,128)(2,1)S(1)}, u32[]{:S(2)}, u32[]{:S(2)}) async-start(bf16[16,2,3200]{2,1,0:T(2,128)(2,1)} %prepare.1), calls=%async_computation | async-start | bytes 409600 | tf_op jit(solution)/shard_map/all_to_all | solution.py:114
  11.6 4.8 %fusion.4 = (bf16[3072,512]{1,0:T(8,128)(2,1)}, bf16[3072,512]{1,0:T(8,128)(2,1)}) fusion(s32[]{:T(128)S(6)} %select_n.27, bf16[6144,256]{1,0:T(8,128)(2,1)} %bitcast.106, bf16[6144,256]{1,0:T(8,128)(2,1)} %bitcast.107, s32[]{:T(128)S(6)} %select_n.26), kind=kLoop, calls=%fused_computation.16 | loop fusion | flops 12582912 | bytes 12582920 | tf_op jit(solution)/shard_map/concatenate | solution.py:123
  16.4 3.6 %all-to-all-done = bf16[16,2,3200]{2,1,0:T(2,128)(2,1)S(1)} async-done(((bf16[16,2,3200]{2,1,0:T(2,128)(2,1)}), bf16[16,2,3200]{2,1,0:T(2,128)(2,1)S(1)}, u32[]{:S(2)}, u32[]{:S(2)}) %all-to-all-start) | async-done | bytes 204832 | tf_op jit(solution)/shard_map/all_to_all | solution.py:114
  20.1 2.8 %collective-permute-start = (bf16[32,3200]{1,0:T(8,128)(2,1)S(1)}, bf16[32,3200]{1,0:T(8,128)(2,1)S(1)}, u32[]{:S(2)}, u32[]{:S(2)}) collective-permute-start(bf16[32,3200]{1,0:T(8,128)(2,1)S(1)} %reshape.101), channel_id=1, source_target_pairs={{0,136},{1,137},{2,138},{3,139},{4,140},{5,141},{6,142},{7,143},{1... | collective-permute-start | bytes 614408 | tf_op jit(solution)/shard_map/ppermute | solution.py:33
  22.9 0.4 collective-permute-start.2
  23.3 0.7 collective-permute-start.1
  24.0 3.8 %collective-permute-done = bf16[32,3200]{1,0:T(8,128)(2,1)S(1)} collective-permute-done((bf16[32,3200]{1,0:T(8,128)(2,1)S(1)}, bf16[32,3200]{1,0:T(8,128)(2,1)S(1)}, u32[]{:S(2)}, u32[]{:S(2)}) %collective-permute-start) | collective-permute-done | bytes 204832 | tf_op jit(solution)/shard_map/ppermute | solution.py:33
  27.9 2.6 %collective-permute-start.3 = (bf16[2,32,3200]{2,1,0:T(8,128)(2,1)S(1)}, bf16[2,32,3200]{2,1,0:T(8,128)(2,1)S(1)}, u32[]{:S(2)}, u32[]{:S(2)}) collective-permute-start(bf16[2,32,3200]{2,1,0:T(8,128)(2,1)S(1)} %pad_maximum_fusion), channel_id=1, source_target_pairs={{0,48},{1,49},{2,50},{3,51},{4,52},{5,53},{6,54},{7,55},{16,0},{17... | collective-permute-start | bytes 1228808 | tf_op jit(solution)/shard_map/ppermute | solution.py:33
  30.4 1.2 %collective-permute-done.1 = bf16[32,3200]{1,0:T(8,128)(2,1)S(1)} collective-permute-done((bf16[32,3200]{1,0:T(8,128)(2,1)S(1)}, bf16[32,3200]{1,0:T(8,128)(2,1)S(1)}, u32[]{:S(2)}, u32[]{:S(2)}) %collective-permute-start.1) | collective-permute-done | bytes 204832 | tf_op jit(solution)/shard_map/ppermute | solution.py:33
  31.7 2.3 %collective-permute-start.4 = (bf16[2,32,3200]{2,1,0:T(8,128)(2,1)S(1)}, bf16[2,32,3200]{2,1,0:T(8,128)(2,1)S(1)}, u32[]{:S(2)}, u32[]{:S(2)}) collective-permute-start(bf16[2,32,3200]{2,1,0:T(8,128)(2,1)S(1)} %pad_maximum_fusion.1), channel_id=1, source_target_pairs={{0,48},{1,49},{2,50},{3,51},{4,52},{5,53},{6,54},{7,55},{16,0},{17... | collective-permute-start | bytes 1228808 | tf_op jit(solution)/shard_map/ppermute | solution.py:33
  33.9 3.1 %collective-permute-start.9 = (bf16[64,3200]{1,0:T(8,128)(2,1)S(1)}, bf16[64,3200]{1,0:T(8,128)(2,1)S(1)}, u32[]{:S(2)}, u32[]{:S(2)}) collective-permute-start(bf16[64,3200]{1,0:T(8,128)(2,1)S(1)} %bitcast.109), channel_id=1, source_target_pairs={{0,64},{64,0},{1,65},{65,1},{2,66},{66,2},{3,67},{67,3},{4,68},{68... | collective-permute-start | bytes 1228808 | tf_op jit(solution)/shard_map/ppermute | solution.py:37
  37.0 2.5 %convolution_dynamic-update-slice_fusion.15 = f32[512,512]{1,0:T(8,128)S(1)} fusion(bf16[3072,512]{1,0:T(8,128)(2,1)} %get-tuple-element.9, bf16[64,3200]{1,0:T(8,128)(2,1)S(1)} %bitcast.110), kind=kOutput, calls=%fused_computation.45 | convolution fusion | flops 201326592 | bytes 3670016 | tf_op jit(solution)/shard_map/dot_general | solution.py:146
  39.6 0.6 convolution_dynamic-update-slice_fusion.14
  40.3 0.6 convolution_dynamic-update-slice_fusion.13
  41.0 1.8 %collective-permute-start.11 = (bf16[64,3200]{1,0:T(8,128)(2,1)S(1)}, bf16[64,3200]{1,0:T(8,128)(2,1)S(1)}, u32[]{:S(2)}, u32[]{:S(2)}) collective-permute-start(bf16[64,3200]{1,0:T(8,128)(2,1)S(1)} %bitcast.128), channel_id=1, source_target_pairs={{0,64},{64,0},{1,65},{65,1},{2,66},{66,2},{3,67},{67,3},{4,68},{68... | collective-permute-start | bytes 1228808 | tf_op jit(solution)/shard_map/ppermute | solution.py:37
  42.8 0.6 convolution_dynamic-update-slice_fusion.12
  43.6 0.6 convolution_dynamic-update-slice_fusion.11
  44.3 1.8 %collective-permute-start.13 = (bf16[64,3200]{1,0:T(8,128)(2,1)S(1)}, bf16[64,3200]{1,0:T(8,128)(2,1)S(1)}, u32[]{:S(2)}, u32[]{:S(2)}) collective-permute-start(bf16[64,3200]{1,0:T(8,128)(2,1)S(1)} %bitcast.122), channel_id=1, source_target_pairs={{0,64},{64,0},{1,65},{65,1},{2,66},{66,2},{3,67},{67,3},{4,68},{68... | collective-permute-start | bytes 1228808 | tf_op jit(solution)/shard_map/ppermute | solution.py:37
  46.1 0.6 convolution_dynamic-update-slice_fusion.10
  46.9 0.6 convolution_dynamic-update-slice_fusion.7
  47.6 3.6 %collective-permute-start.8 = (bf16[2,32,3200]{2,1,0:T(8,128)(2,1)S(1)}, bf16[2,32,3200]{2,1,0:T(8,128)(2,1)S(1)}, u32[]{:S(2)}, u32[]{:S(2)}) collective-permute-start(bf16[2,32,3200]{2,1,0:T(8,128)(2,1)S(1)} %collective-permute-done.4), channel_id=1, source_target_pairs={{0,48},{1,49},{2,50},{3,51},{4,52},{5,53},{6,54},{7,55},{16,0},{17... | collective-permute-start | bytes 1228808 | tf_op jit(solution)/shard_map/ppermute | solution.py:33
  51.2 0.6 convolution_dynamic-update-slice_fusion.6
  51.9 3.8 %collective-permute-done.7 = bf16[2,32,3200]{2,1,0:T(8,128)(2,1)S(1)} collective-permute-done((bf16[2,32,3200]{2,1,0:T(8,128)(2,1)S(1)}, bf16[2,32,3200]{2,1,0:T(8,128)(2,1)S(1)}, u32[]{:S(2)}, u32[]{:S(2)}) %collective-permute-start.7) | collective-permute-done | bytes 409632 | tf_op jit(solution)/shard_map/ppermute | solution.py:33
  56.0 0.6 convolution_dynamic-update-slice_fusion.9
  56.9 0.6 convolution_dynamic-update-slice_fusion.8
  57.6 0.5 collective-permute-start.16
  58.1 0.6 convolution_dynamic-update-slice_fusion.5
  58.7 0.6 convolution_dynamic-update-slice_fusion.4
  59.4 0.6 convolution_dynamic-update-slice_fusion.3
  60.1 0.6 convolution_dynamic-update-slice_fusion.2
  60.8 0.6 convolution_dynamic-update-slice_fusion.1
  61.5 0.6 convolution_dynamic-update-slice_fusion
  63.8 0.5 collective-permute-start.17
  65.3 0.5 collective-permute-start.19
  66.3 3.5 %collective-permute-start.23 = (bf16[2,32,3072]{2,1,0:T(8,128)(2,1)S(1)}, bf16[2,32,3072]{2,1,0:T(8,128)(2,1)S(1)}, u32[]{:S(2)}, u32[]{:S(2)}) collective-permute-start(bf16[2,32,3072]{2,1,0:T(8,128)(2,1)S(1)} %bitcast.139), channel_id=1, source_target_pairs={{0,48},{1,49},{2,50},{3,51},{4,52},{5,53},{6,54},{7,55},{16,0},{17... | collective-permute-start | bytes 1179656 | tf_op jit(solution)/shard_map/ppermute | solution.py:33
  70.3 2.9 %collective-permute-start.26 = (bf16[2,32,3072]{2,1,0:T(8,128)(2,1)S(1)}, bf16[2,32,3072]{2,1,0:T(8,128)(2,1)S(1)}, u32[]{:S(2)}, u32[]{:S(2)}) collective-permute-start(bf16[2,32,3072]{2,1,0:T(8,128)(2,1)S(1)} %bitcast.142), channel_id=1, source_target_pairs={{0,48},{1,49},{2,50},{3,51},{4,52},{5,53},{6,54},{7,55},{16,0},{17... | collective-permute-start | bytes 1179656 | tf_op jit(solution)/shard_map/ppermute | solution.py:33
  73.9 0.4 add_convert_fusion.3
  74.4 4.3 %collective-permute-done.26 = bf16[2,32,3072]{2,1,0:T(8,128)(2,1)S(1)} collective-permute-done((bf16[2,32,3072]{2,1,0:T(8,128)(2,1)S(1)}, bf16[2,32,3072]{2,1,0:T(8,128)(2,1)S(1)}, u32[]{:S(2)}, u32[]{:S(2)}) %collective-permute-start.26) | collective-permute-done | bytes 393248 | tf_op jit(solution)/shard_map/ppermute | solution.py:33
  78.8 3.5 %collective-permute-start.27 = (bf16[2,32,3072]{2,1,0:T(8,128)(2,1)S(1)}, bf16[2,32,3072]{2,1,0:T(8,128)(2,1)S(1)}, u32[]{:S(2)}, u32[]{:S(2)}) collective-permute-start(bf16[2,32,3072]{2,1,0:T(8,128)(2,1)S(1)} %fusion.30), channel_id=1, source_target_pairs={{0,48},{1,49},{2,50},{3,51},{4,52},{5,53},{6,54},{7,55},{16,0},{17... | collective-permute-start | bytes 1179656 | tf_op jit(solution)/shard_map/ppermute | solution.py:33
  82.7 4.3 %collective-permute-done.27 = bf16[2,32,3072]{2,1,0:T(8,128)(2,1)S(1)} collective-permute-done((bf16[2,32,3072]{2,1,0:T(8,128)(2,1)S(1)}, bf16[2,32,3072]{2,1,0:T(8,128)(2,1)S(1)}, u32[]{:S(2)}, u32[]{:S(2)}) %collective-permute-start.27) | collective-permute-done | bytes 393248 | tf_op jit(solution)/shard_map/ppermute | solution.py:33
  87.2 2.7 %collective-permute-start.29 = (bf16[32,3072]{1,0:T(8,128)(2,1)S(1)}, bf16[32,3072]{1,0:T(8,128)(2,1)S(1)}, u32[]{:S(2)}, u32[]{:S(2)}) collective-permute-start(bf16[32,3072]{1,0:T(8,128)(2,1)S(1)} %get-tuple-element.24), channel_id=1, source_target_pairs={{0,136},{1,137},{2,138},{3,139},{4,140},{5,141},{6,142},{7,143},{1... | collective-permute-start | bytes 589832 | tf_op jit(solution)/shard_map/ppermute | solution.py:33
  89.9 0.7 collective-permute-done.21
  90.9 3.8 %collective-permute-done.29 = bf16[32,3072]{1,0:T(8,128)(2,1)S(1)} collective-permute-done((bf16[32,3072]{1,0:T(8,128)(2,1)S(1)}, bf16[32,3072]{1,0:T(8,128)(2,1)S(1)}, u32[]{:S(2)}, u32[]{:S(2)}) %collective-permute-start.29) | collective-permute-done | bytes 196640 | tf_op jit(solution)/shard_map/ppermute | solution.py:33
  94.6 1.4 %collective-permute-done.28 = bf16[32,3072]{1,0:T(8,128)(2,1)S(1)} collective-permute-done((bf16[32,3072]{1,0:T(8,128)(2,1)S(1)}, bf16[32,3072]{1,0:T(8,128)(2,1)S(1)}, u32[]{:S(2)}, u32[]{:S(2)}) %collective-permute-start.28) | collective-permute-done | bytes 196640 | tf_op jit(solution)/shard_map/ppermute | solution.py:33
  96.0 2.3 %collective-permute-done.24 = bf16[32,3072]{1,0:T(8,128)(2,1)S(1)} collective-permute-done((bf16[32,3072]{1,0:T(8,128)(2,1)S(1)}, bf16[32,3072]{1,0:T(8,128)(2,1)S(1)}, u32[]{:S(2)}, u32[]{:S(2)}) %collective-permute-start.24) | collective-permute-done | bytes 196640 | tf_op jit(solution)/shard_map/ppermute | solution.py:33
  98.5 15.3 %all_to_all.10 = bf16[16,2,3072]{2,1,0:T(2,128)(2,1)S(1)} all-to-all(bf16[16,2,3072]{2,1,0:T(2,128)(2,1)S(1)} %reshape.113), channel_id=1, replica_groups=mesh['xl'=2,'c'=2,'y'=4,'xh'=2,'z'=8] {'c','z'}, dimensions={0} | all-to-all | bytes 393216 | tf_op jit(solution)/shard_map/all_to_all | solution.py:176
  114.1 0.6 pad_maximum_fusion.2
  (89 shorter events, 6.8 us)
Async XLA Ops:
  0.0 62.9 %copy-start = (bf16[1,256,6144]{2,1,0:T(8,128)(2,1)S(1)}, bf16[1,256,6144]{2,1,0:T(8,128)(2,1)}, u32[]{:S(2)}) copy-start(bf16[1,256,6144]{2,1,0:T(8,128)(2,1)} %param.11) | copy-start | bytes 9437188
  1.6 18.4 %all-to-all-start = ((bf16[16,2,3200]{2,1,0:T(2,128)(2,1)}), bf16[16,2,3200]{2,1,0:T(2,128)(2,1)S(1)}, u32[]{:S(2)}, u32[]{:S(2)}) async-start(bf16[16,2,3200]{2,1,0:T(2,128)(2,1)} %prepare.1), calls=%async_computation | async-start | bytes 409600 | tf_op jit(solution)/shard_map/all_to_all | solution.py:114
  20.1 7.7 %collective-permute-start = (bf16[32,3200]{1,0:T(8,128)(2,1)S(1)}, bf16[32,3200]{1,0:T(8,128)(2,1)S(1)}, u32[]{:S(2)}, u32[]{:S(2)}) collective-permute-start(bf16[32,3200]{1,0:T(8,128)(2,1)S(1)} %reshape.101), channel_id=1, source_target_pairs={{0,136},{1,137},{2,138},{3,139},{4,140},{5,141},{6,142},{7,143},{1... | collective-permute-start | bytes 614408 | tf_op jit(solution)/shard_map/ppermute | solution.py:33
  22.9 16.6 %copy-start.2 = (bf16[3072,512]{1,0:T(8,128)(2,1)S(1)}, bf16[3072,512]{1,0:T(8,128)(2,1)}, u32[]{:S(2)}) copy-start(bf16[3072,512]{1,0:T(8,128)(2,1)} %get-tuple-element.9) | copy-start | bytes 9437188
  22.9 7.5 %collective-permute-start.2 = (bf16[32,3200]{1,0:T(8,128)(2,1)S(1)}, bf16[32,3200]{1,0:T(8,128)(2,1)S(1)}, u32[]{:S(2)}, u32[]{:S(2)}) collective-permute-start(bf16[32,3200]{1,0:T(8,128)(2,1)S(1)} %reshape.101), channel_id=1, source_target_pairs={{0,8},{1,9},{2,10},{3,11},{4,12},{5,13},{6,14},{7,15},{16,24},{17,... | collective-permute-start | bytes 614408 | tf_op jit(solution)/shard_map/ppermute | solution.py:33
  23.3 8.3 %collective-permute-start.1 = (bf16[32,3200]{1,0:T(8,128)(2,1)S(1)}, bf16[32,3200]{1,0:T(8,128)(2,1)S(1)}, u32[]{:S(2)}, u32[]{:S(2)}) collective-permute-start(bf16[32,3200]{1,0:T(8,128)(2,1)S(1)} %reshape.101), channel_id=1, source_target_pairs={{0,128},{1,129},{2,130},{3,131},{4,132},{5,133},{6,134},{7,135},{1... | collective-permute-start | bytes 614408 | tf_op jit(solution)/shard_map/ppermute | solution.py:33
  27.9 12.4 %collective-permute-start.3 = (bf16[2,32,3200]{2,1,0:T(8,128)(2,1)S(1)}, bf16[2,32,3200]{2,1,0:T(8,128)(2,1)S(1)}, u32[]{:S(2)}, u32[]{:S(2)}) collective-permute-start(bf16[2,32,3200]{2,1,0:T(8,128)(2,1)S(1)} %pad_maximum_fusion), channel_id=1, source_target_pairs={{0,48},{1,49},{2,50},{3,51},{4,52},{5,53},{6,54},{7,55},{16,0},{17... | collective-permute-start | bytes 1228808 | tf_op jit(solution)/shard_map/ppermute | solution.py:33
  30.4 13.1 %collective-permute-start.5 = (bf16[2,32,3200]{2,1,0:T(8,128)(2,1)S(1)}, bf16[2,32,3200]{2,1,0:T(8,128)(2,1)S(1)}, u32[]{:S(2)}, u32[]{:S(2)}) collective-permute-start(bf16[2,32,3200]{2,1,0:T(8,128)(2,1)S(1)} %pad_maximum_fusion), channel_id=1, source_target_pairs={{0,16},{1,17},{2,18},{3,19},{4,20},{5,21},{6,22},{7,23},{16,32},{1... | collective-permute-start | bytes 1228808 | tf_op jit(solution)/shard_map/ppermute | solution.py:33
  31.7 9.4 %collective-permute-start.4 = (bf16[2,32,3200]{2,1,0:T(8,128)(2,1)S(1)}, bf16[2,32,3200]{2,1,0:T(8,128)(2,1)S(1)}, u32[]{:S(2)}, u32[]{:S(2)}) collective-permute-start(bf16[2,32,3200]{2,1,0:T(8,128)(2,1)S(1)} %pad_maximum_fusion.1), channel_id=1, source_target_pairs={{0,48},{1,49},{2,50},{3,51},{4,52},{5,53},{6,54},{7,55},{16,0},{17... | collective-permute-start | bytes 1228808 | tf_op jit(solution)/shard_map/ppermute | solution.py:33
  33.9 10.4 %collective-permute-start.6 = (bf16[2,32,3200]{2,1,0:T(8,128)(2,1)S(1)}, bf16[2,32,3200]{2,1,0:T(8,128)(2,1)S(1)}, u32[]{:S(2)}, u32[]{:S(2)}) collective-permute-start(bf16[2,32,3200]{2,1,0:T(8,128)(2,1)S(1)} %pad_maximum_fusion.1), channel_id=1, source_target_pairs={{0,16},{1,17},{2,18},{3,19},{4,20},{5,21},{6,22},{7,23},{16,32},{1... | collective-permute-start | bytes 1228808 | tf_op jit(solution)/shard_map/ppermute | solution.py:33
  33.9 12.9 %collective-permute-start.9 = (bf16[64,3200]{1,0:T(8,128)(2,1)S(1)}, bf16[64,3200]{1,0:T(8,128)(2,1)S(1)}, u32[]{:S(2)}, u32[]{:S(2)}) collective-permute-start(bf16[64,3200]{1,0:T(8,128)(2,1)S(1)} %bitcast.109), channel_id=1, source_target_pairs={{0,64},{64,0},{1,65},{65,1},{2,66},{66,2},{3,67},{67,3},{4,68},{68... | collective-permute-start | bytes 1228808 | tf_op jit(solution)/shard_map/ppermute | solution.py:37
  40.2 7.3 %collective-permute-start.10 = (bf16[64,3200]{1,0:T(8,128)(2,1)S(1)}, bf16[64,3200]{1,0:T(8,128)(2,1)S(1)}, u32[]{:S(2)}, u32[]{:S(2)}) collective-permute-start(bf16[64,3200]{1,0:T(8,128)(2,1)S(1)} %bitcast.114), channel_id=1, source_target_pairs={{0,64},{64,0},{1,65},{65,1},{2,66},{66,2},{3,67},{67,3},{4,68},{68... | collective-permute-start | bytes 1228808 | tf_op jit(solution)/shard_map/ppermute | solution.py:37
  41.0 16.6 %collective-permute-start.11 = (bf16[64,3200]{1,0:T(8,128)(2,1)S(1)}, bf16[64,3200]{1,0:T(8,128)(2,1)S(1)}, u32[]{:S(2)}, u32[]{:S(2)}) collective-permute-start(bf16[64,3200]{1,0:T(8,128)(2,1)S(1)} %bitcast.128), channel_id=1, source_target_pairs={{0,64},{64,0},{1,65},{65,1},{2,66},{66,2},{3,67},{67,3},{4,68},{68... | collective-permute-start | bytes 1228808 | tf_op jit(solution)/shard_map/ppermute | solution.py:37
  43.5 15.2 %collective-permute-start.12 = (bf16[64,3200]{1,0:T(8,128)(2,1)S(1)}, bf16[64,3200]{1,0:T(8,128)(2,1)S(1)}, u32[]{:S(2)}, u32[]{:S(2)}) collective-permute-start(bf16[64,3200]{1,0:T(8,128)(2,1)S(1)} %bitcast.132), channel_id=1, source_target_pairs={{0,64},{64,0},{1,65},{65,1},{2,66},{66,2},{3,67},{67,3},{4,68},{68... | collective-permute-start | bytes 1228808 | tf_op jit(solution)/shard_map/ppermute | solution.py:37
  43.6 3.3 %copy-start.1 = (bf16[3072,512]{1,0:T(8,128)(2,1)S(1)}, bf16[3072,512]{1,0:T(8,128)(2,1)}, u32[]{:S(2)}) copy-start(bf16[3072,512]{1,0:T(8,128)(2,1)} %get-tuple-element.10) | copy-start | bytes 9437188
  44.3 15.1 %collective-permute-start.13 = (bf16[64,3200]{1,0:T(8,128)(2,1)S(1)}, bf16[64,3200]{1,0:T(8,128)(2,1)S(1)}, u32[]{:S(2)}, u32[]{:S(2)}) collective-permute-start(bf16[64,3200]{1,0:T(8,128)(2,1)S(1)} %bitcast.122), channel_id=1, source_target_pairs={{0,64},{64,0},{1,65},{65,1},{2,66},{66,2},{3,67},{67,3},{4,68},{68... | collective-permute-start | bytes 1228808 | tf_op jit(solution)/shard_map/ppermute | solution.py:37
  46.8 8.8 %collective-permute-start.7 = (bf16[2,32,3200]{2,1,0:T(8,128)(2,1)S(1)}, bf16[2,32,3200]{2,1,0:T(8,128)(2,1)S(1)}, u32[]{:S(2)}, u32[]{:S(2)}) collective-permute-start(bf16[2,32,3200]{2,1,0:T(8,128)(2,1)S(1)} %collective-permute-done.5), channel_id=1, source_target_pairs={{0,16},{1,17},{2,18},{3,19},{4,20},{5,21},{6,22},{7,23},{16,32},{1... | collective-permute-start | bytes 1228808 | tf_op jit(solution)/shard_map/ppermute | solution.py:33
  47.6 9.1 %collective-permute-start.8 = (bf16[2,32,3200]{2,1,0:T(8,128)(2,1)S(1)}, bf16[2,32,3200]{2,1,0:T(8,128)(2,1)S(1)}, u32[]{:S(2)}, u32[]{:S(2)}) collective-permute-start(bf16[2,32,3200]{2,1,0:T(8,128)(2,1)S(1)} %collective-permute-done.4), channel_id=1, source_target_pairs={{0,48},{1,49},{2,50},{3,51},{4,52},{5,53},{6,54},{7,55},{16,0},{17... | collective-permute-start | bytes 1228808 | tf_op jit(solution)/shard_map/ppermute | solution.py:33
  55.6 4.4 %collective-permute-start.14 = (bf16[64,3200]{1,0:T(8,128)(2,1)S(1)}, bf16[64,3200]{1,0:T(8,128)(2,1)S(1)}, u32[]{:S(2)}, u32[]{:S(2)}) collective-permute-start(bf16[64,3200]{1,0:T(8,128)(2,1)S(1)} %bitcast.126), channel_id=1, source_target_pairs={{0,64},{64,0},{1,65},{65,1},{2,66},{66,2},{3,67},{67,3},{4,68},{68... | collective-permute-start | bytes 1228808 | tf_op jit(solution)/shard_map/ppermute | solution.py:37
  56.7 4.1 %collective-permute-start.15 = (bf16[64,3200]{1,0:T(8,128)(2,1)S(1)}, bf16[64,3200]{1,0:T(8,128)(2,1)S(1)}, u32[]{:S(2)}, u32[]{:S(2)}) collective-permute-start(bf16[64,3200]{1,0:T(8,128)(2,1)S(1)} %bitcast.134), channel_id=1, source_target_pairs={{0,64},{64,0},{1,65},{65,1},{2,66},{66,2},{3,67},{67,3},{4,68},{68... | collective-permute-start | bytes 1228808 | tf_op jit(solution)/shard_map/ppermute | solution.py:37
  57.6 3.9 %collective-permute-start.16 = (bf16[64,3200]{1,0:T(8,128)(2,1)S(1)}, bf16[64,3200]{1,0:T(8,128)(2,1)S(1)}, u32[]{:S(2)}, u32[]{:S(2)}) collective-permute-start(bf16[64,3200]{1,0:T(8,128)(2,1)S(1)} %bitcast.138), channel_id=1, source_target_pairs={{0,64},{64,0},{1,65},{65,1},{2,66},{66,2},{3,67},{67,3},{4,68},{68... | collective-permute-start | bytes 1228808 | tf_op jit(solution)/shard_map/ppermute | solution.py:37
  63.3 2.6 %collective-permute-start.22 = (bf16[128,3072]{1,0:T(8,128)(2,1)S(1)}, bf16[128,3072]{1,0:T(8,128)(2,1)S(1)}, u32[]{:S(2)}, u32[]{:S(2)}) collective-permute-start(bf16[128,3072]{1,0:T(8,128)(2,1)S(1)} %fusion.3), channel_id=1, source_target_pairs={{0,64},{64,0},{1,65},{65,1},{2,66},{66,2},{3,67},{67,3},{4,68},{68... | collective-permute-start | bytes 2359304 | tf_op jit(solution)/shard_map/ppermute | solution.py:37
  63.8 10.0 %collective-permute-start.17 = (bf16[128,3072]{1,0:T(8,128)(2,1)S(1)}, bf16[128,3072]{1,0:T(8,128)(2,1)S(1)}, u32[]{:S(2)}, u32[]{:S(2)}) collective-permute-start(bf16[128,3072]{1,0:T(8,128)(2,1)S(1)} %fusion), channel_id=1, source_target_pairs={{0,64},{64,0},{1,65},{65,1},{2,66},{66,2},{3,67},{67,3},{4,68},{68... | collective-permute-start | bytes 2359304 | tf_op jit(solution)/shard_map/ppermute | solution.py:37
  64.7 8.5 %collective-permute-start.18 = (bf16[128,3072]{1,0:T(8,128)(2,1)S(1)}, bf16[128,3072]{1,0:T(8,128)(2,1)S(1)}, u32[]{:S(2)}, u32[]{:S(2)}) collective-permute-start(bf16[128,3072]{1,0:T(8,128)(2,1)S(1)} %fusion.1), channel_id=1, source_target_pairs={{0,64},{64,0},{1,65},{65,1},{2,66},{66,2},{3,67},{67,3},{4,68},{68... | collective-permute-start | bytes 2359304 | tf_op jit(solution)/shard_map/ppermute | solution.py:37
  65.3 4.4 %collective-permute-start.19 = (bf16[128,3072]{1,0:T(8,128)(2,1)S(1)}, bf16[128,3072]{1,0:T(8,128)(2,1)S(1)}, u32[]{:S(2)}, u32[]{:S(2)}) collective-permute-start(bf16[128,3072]{1,0:T(8,128)(2,1)S(1)} %fusion.2), channel_id=1, source_target_pairs={{0,64},{64,0},{1,65},{65,1},{2,66},{66,2},{3,67},{67,3},{4,68},{68... | collective-permute-start | bytes 2359304 | tf_op jit(solution)/shard_map/ppermute | solution.py:37
  66.3 23.6 %collective-permute-start.23 = (bf16[2,32,3072]{2,1,0:T(8,128)(2,1)S(1)}, bf16[2,32,3072]{2,1,0:T(8,128)(2,1)S(1)}, u32[]{:S(2)}, u32[]{:S(2)}) collective-permute-start(bf16[2,32,3072]{2,1,0:T(8,128)(2,1)S(1)} %bitcast.139), channel_id=1, source_target_pairs={{0,48},{1,49},{2,50},{3,51},{4,52},{5,53},{6,54},{7,55},{16,0},{17... | collective-permute-start | bytes 1179656 | tf_op jit(solution)/shard_map/ppermute | solution.py:33
  70.3 12.0 %collective-permute-start.20 = (bf16[2,32,3072]{2,1,0:T(8,128)(2,1)S(1)}, bf16[2,32,3072]{2,1,0:T(8,128)(2,1)S(1)}, u32[]{:S(2)}, u32[]{:S(2)}) collective-permute-start(bf16[2,32,3072]{2,1,0:T(8,128)(2,1)S(1)} %bitcast.140), channel_id=1, source_target_pairs={{0,16},{1,17},{2,18},{3,19},{4,20},{5,21},{6,22},{7,23},{16,32},{1... | collective-permute-start | bytes 1179656 | tf_op jit(solution)/shard_map/ppermute | solution.py:33
  70.3 8.3 %collective-permute-start.26 = (bf16[2,32,3072]{2,1,0:T(8,128)(2,1)S(1)}, bf16[2,32,3072]{2,1,0:T(8,128)(2,1)S(1)}, u32[]{:S(2)}, u32[]{:S(2)}) collective-permute-start(bf16[2,32,3072]{2,1,0:T(8,128)(2,1)S(1)} %bitcast.142), channel_id=1, source_target_pairs={{0,48},{1,49},{2,50},{3,51},{4,52},{5,53},{6,54},{7,55},{16,0},{17... | collective-permute-start | bytes 1179656 | tf_op jit(solution)/shard_map/ppermute | solution.py:33
  73.7 8.9 %collective-permute-start.25 = (bf16[2,32,3072]{2,1,0:T(8,128)(2,1)S(1)}, bf16[2,32,3072]{2,1,0:T(8,128)(2,1)S(1)}, u32[]{:S(2)}, u32[]{:S(2)}) collective-permute-start(bf16[2,32,3072]{2,1,0:T(8,128)(2,1)S(1)} %bitcast.141), channel_id=1, source_target_pairs={{0,16},{1,17},{2,18},{3,19},{4,20},{5,21},{6,22},{7,23},{16,32},{1... | collective-permute-start | bytes 1179656 | tf_op jit(solution)/shard_map/ppermute | solution.py:33
  78.8 8.2 %collective-permute-start.27 = (bf16[2,32,3072]{2,1,0:T(8,128)(2,1)S(1)}, bf16[2,32,3072]{2,1,0:T(8,128)(2,1)S(1)}, u32[]{:S(2)}, u32[]{:S(2)}) collective-permute-start(bf16[2,32,3072]{2,1,0:T(8,128)(2,1)S(1)} %fusion.30), channel_id=1, source_target_pairs={{0,48},{1,49},{2,50},{3,51},{4,52},{5,53},{6,54},{7,55},{16,0},{17... | collective-permute-start | bytes 1179656 | tf_op jit(solution)/shard_map/ppermute | solution.py:33
  82.4 8.2 %collective-permute-start.21 = (bf16[2,32,3072]{2,1,0:T(8,128)(2,1)S(1)}, bf16[2,32,3072]{2,1,0:T(8,128)(2,1)S(1)}, u32[]{:S(2)}, u32[]{:S(2)}) collective-permute-start(bf16[2,32,3072]{2,1,0:T(8,128)(2,1)S(1)} %fusion.33), channel_id=1, source_target_pairs={{0,16},{1,17},{2,18},{3,19},{4,20},{5,21},{6,22},{7,23},{16,32},{1... | collective-permute-start | bytes 1179656 | tf_op jit(solution)/shard_map/ppermute | solution.py:33
  87.2 7.5 %collective-permute-start.29 = (bf16[32,3072]{1,0:T(8,128)(2,1)S(1)}, bf16[32,3072]{1,0:T(8,128)(2,1)S(1)}, u32[]{:S(2)}, u32[]{:S(2)}) collective-permute-start(bf16[32,3072]{1,0:T(8,128)(2,1)S(1)} %get-tuple-element.24), channel_id=1, source_target_pairs={{0,136},{1,137},{2,138},{3,139},{4,140},{5,141},{6,142},{7,143},{1... | collective-permute-start | bytes 589832 | tf_op jit(solution)/shard_map/ppermute | solution.py:33
  89.9 6.1 %collective-permute-start.28 = (bf16[32,3072]{1,0:T(8,128)(2,1)S(1)}, bf16[32,3072]{1,0:T(8,128)(2,1)S(1)}, u32[]{:S(2)}, u32[]{:S(2)}) collective-permute-start(bf16[32,3072]{1,0:T(8,128)(2,1)S(1)} %get-tuple-element.23), channel_id=1, source_target_pairs={{0,8},{1,9},{2,10},{3,11},{4,12},{5,13},{6,14},{7,15},{16,24},{17,... | collective-permute-start | bytes 589832 | tf_op jit(solution)/shard_map/ppermute | solution.py:33
  90.8 7.6 %collective-permute-start.24 = (bf16[32,3072]{1,0:T(8,128)(2,1)S(1)}, bf16[32,3072]{1,0:T(8,128)(2,1)S(1)}, u32[]{:S(2)}, u32[]{:S(2)}) collective-permute-start(bf16[32,3072]{1,0:T(8,128)(2,1)S(1)} %fusion.56), channel_id=1, source_target_pairs={{0,128},{1,129},{2,130},{3,131},{4,132},{5,133},{6,134},{7,135},{1... | collective-permute-start | bytes 589832 | tf_op jit(solution)/shard_map/ppermute | solution.py:33

commit v5 on v4

--- a/solution.py
+++ b/solution.py
@@ -40,11 +40,15 @@
 def ring_gather(one, two, first):
     from_left_one = move(one, first, 1)
     from_right_two = move(two, first, -1)
+    from_right_one = move(one, first, -1)
     from_left_two = move(two, first, 1)
-    from_right_one = move(one, first, -1)
     far_one = move(from_left_one, first, 1)
     far_two = move(from_right_two, first, -1)
-    return [one, two, from_right_one, from_right_two, from_left_one, from_left_two, far_one, far_two]
+    pairs = (one, two), (from_right_one, from_right_two), (from_left_one, from_left_two), (far_one, far_two)
+    joined = []
+    for pair in pairs:
+        joined.append(jnp.concatenate(pair, axis=0))
+    return joined
 
 
 def add(*terms):
@@ -129,7 +133,7 @@
         tiles.append(move(tile, True, step))
     one = jnp.stack(tiles[:2], axis=0)
     two = jnp.stack(tiles[2:], axis=0)
-    mine = [v.reshape(2 * rows, half + PAD) for v in ring_gather(one, two, False)]
+    mine = [v.reshape(RING * rows, half + PAD) for v in ring_gather(one, two, False)]
     other = []
     for v in mine:
         other.append(swap(v))

time: 116 us -> 109 us (0.940); the launches traced: 115 us -> 109 us
  matrix products: 15.5 us -> 7.8 us
  other arithmetic: 6.83 us -> 9.11 us
  waiting for transfers between devices: 29.4 us -> 31 us
  starting transfers between devices: 44.7 us -> 43.3 us
    dot_general x16 -> x8, matrix products: 12.2 us -> 4.56 us  [product(): parts.append(jnp.dot(v[:, :half], w, preferred_element_type=jnp.float32))]
    ppermute x18, starting transfers between devices: 25.4 us -> 21.6 us  [move(): return lax.ppermute(v, AXES, ring_perm(first, step))]
    ppermute x12 -> x8, starting transfers between devices: 9.35 us -> 11.7 us  [swap(): return lax.ppermute(v, 'c', [(0, 1), (1, 0)])]
    concatenate x0 -> x5, other arithmetic: none -> 1.39 us  [the longest x4 1.31 us: ring_gather(): joined.append(jnp.concatenate(pair, axis=0))]
  transfers between devices with their start and end apart: 31 -> 27, of which waited for: 11 -> 10; matrix products, arithmetic and copies ran while one was open for 18% -> 13% of each run, Pallas kernels for 0% -> 0%
where the time goes in v5:
time: 109 us
  starting transfers between devices  43.3 us (40%)
  waiting for transfers between devices  31 us (28%)
  blocking collectives  14.9 us (14%)
  other arithmetic  9.11 us (8%)
  matrix products  7.8 us (7%)
  Pallas kernels  1.6 us (1%)
    ppermute x18, waiting for transfers between devices, move(): return lax.ppermute(v, AXES, ring_perm(first, step))  26.5 us
    ppermute x18, starting transfers between devices, move(): return lax.ppermute(v, AXES, ring_perm(first, step))  21.6 us
    all_to_all x1, blocking collectives, shards(): lax.all_to_all(last.reshape(16, tok_rows, half), ('c', 'z'), split_axis=0...  14.9 us
    ppermute x8, starting transfers between devices, swap(): return lax.ppermute(v, 'c', [(0, 1), (1, 0)])  11.7 us
    all_to_all x1, starting transfers between devices, shards(): lax.all_to_all(outgoing, ('c', 'z'), split_axis=0, concat_axis=0, tiled=T...  9.97 us
    concatenate x1, other arithmetic, shards(): w_in = jnp.concatenate([gate_weight[0], up_weight[0]], axis=1)  4.75 us
    dot_general x8, matrix products, product(): parts.append(jnp.dot(v[:, :half], w, preferred_element_type=jnp.float32))  4.56 us
    all_to_all x1, waiting for transfers between devices, shards(): lax.all_to_all(outgoing, ('c', 'z'), split_axis=0, concat_axis=0, tiled=T...  3.67 us
  transfers between devices with their start and end apart: 27, of which 10 were waited for; matrix products, arithmetic and copies ran while one was open for 13% of the time, Pallas kernels for 0%

profile of v5, /device:TPU:1, one launch (start us, length us, event | category | flops | bytes accessed | tf_op | source)
XLA Modules:
  0.0 109.0 jit_solution(16314191125269183263)
XLA Ops:
  0.0 1.6 %prepare.1 = bf16[16,2,3200]{2,1,0:T(2,128)(2,1)} custom-call(s32[2,2]{1,0:T(2,128)} %routing.1, f32[2,2]{1,0:T(2,128)} %weights.1, bf16[2,6144]{1,0:T(2,128)(2,1)} %tokens.1), custom_call_target="tpu_custom_call" | custom-call | tf_op jit(solution)/shard_map/prepare/pallas_call | solution.py:99
  1.6 10.0 %all-to-all-start = ((bf16[16,2,3200]{2,1,0:T(2,128)(2,1)}), bf16[16,2,3200]{2,1,0:T(2,128)(2,1)S(1)}, u32[]{:S(2)}, u32[]{:S(2)}) async-start(bf16[16,2,3200]{2,1,0:T(2,128)(2,1)} %prepare.1), calls=%async_computation | async-start | bytes 409600 | tf_op jit(solution)/shard_map/all_to_all | solution.py:118
  11.6 4.7 %fusion.4 = (bf16[3072,512]{1,0:T(8,128)(2,1)}, bf16[3072,512]{1,0:T(8,128)(2,1)}) fusion(s32[]{:T(128)S(6)} %select_n.27, bf16[6144,256]{1,0:T(8,128)(2,1)} %bitcast.107, bf16[6144,256]{1,0:T(8,128)(2,1)} %bitcast.108, s32[]{:T(128)S(6)} %select_n.26), kind=kLoop, calls=%fused_computation.16 | loop fusion | flops 12582912 | bytes 12582920 | tf_op jit(solution)/shard_map/concatenate | solution.py:127
  16.3 3.7 %all-to-all-done = bf16[16,2,3200]{2,1,0:T(2,128)(2,1)S(1)} async-done(((bf16[16,2,3200]{2,1,0:T(2,128)(2,1)}), bf16[16,2,3200]{2,1,0:T(2,128)(2,1)S(1)}, u32[]{:S(2)}, u32[]{:S(2)}) %all-to-all-start) | async-done | bytes 204832 | tf_op jit(solution)/shard_map/all_to_all | solution.py:118
  20.1 3.0 %collective-permute-start.2 = (bf16[32,3200]{1,0:T(8,128)(2,1)S(1)}, bf16[32,3200]{1,0:T(8,128)(2,1)S(1)}, u32[]{:S(2)}, u32[]{:S(2)}) collective-permute-start(bf16[32,3200]{1,0:T(8,128)(2,1)S(1)} %reshape.89), channel_id=1, source_target_pairs={{0,8},{1,9},{2,10},{3,11},{4,12},{5,13},{6,14},{7,15},{16,24},{17,... | collective-permute-start | bytes 614408 | tf_op jit(solution)/shard_map/ppermute | solution.py:33
  23.5 2.4 %collective-permute-start = (bf16[32,3200]{1,0:T(8,128)(2,1)S(1)}, bf16[32,3200]{1,0:T(8,128)(2,1)S(1)}, u32[]{:S(2)}, u32[]{:S(2)}) collective-permute-start(bf16[32,3200]{1,0:T(8,128)(2,1)S(1)} %reshape.89), channel_id=1, source_target_pairs={{0,136},{1,137},{2,138},{3,139},{4,140},{5,141},{6,142},{7,143},{1... | collective-permute-start | bytes 614408 | tf_op jit(solution)/shard_map/ppermute | solution.py:33
  25.8 0.7 collective-permute-done.2
  26.6 2.7 %collective-permute-done.1 = bf16[32,3200]{1,0:T(8,128)(2,1)} collective-permute-done((bf16[32,3200]{1,0:T(8,128)(2,1)S(1)}, bf16[32,3200]{1,0:T(8,128)(2,1)}, u32[]{:S(2)}, u32[]{:S(2)}) %collective-permute-start.1) | collective-permute-done | bytes 204832 | tf_op jit(solution)/shard_map/ppermute | solution.py:33
  29.3 1.0 pad_maximum_fusion.6
  30.3 1.0 collective-permute-start.6
  31.3 1.8 %collective-permute-start.4 = (bf16[2,32,3200]{2,1,0:T(8,128)(2,1)S(1)}, bf16[2,32,3200]{2,1,0:T(8,128)(2,1)S(1)}, u32[]{:S(2)}, u32[]{:S(2)}) collective-permute-start(bf16[2,32,3200]{2,1,0:T(8,128)(2,1)S(1)} %pad_maximum_fusion.6), channel_id=1, source_target_pairs={{0,48},{1,49},{2,50},{3,51},{4,52},{5,53},{6,54},{7,55},{16,0},{17... | collective-permute-start | bytes 1228808 | tf_op jit(solution)/shard_map/ppermute | solution.py:33
  33.2 1.1 pad_maximum_fusion.1
  34.2 2.7 %collective-permute-start.3 = (bf16[2,32,3200]{2,1,0:T(8,128)(2,1)S(1)}, bf16[2,32,3200]{2,1,0:T(8,128)(2,1)S(1)}, u32[]{:S(2)}, u32[]{:S(2)}) collective-permute-start(bf16[2,32,3200]{2,1,0:T(8,128)(2,1)S(1)} %pad_maximum_fusion.5), channel_id=1, source_target_pairs={{0,48},{1,49},{2,50},{3,51},{4,52},{5,53},{6,54},{7,55},{16,0},{17... | collective-permute-start | bytes 1228808 | tf_op jit(solution)/shard_map/ppermute | solution.py:33
  37.0 3.1 %collective-permute-start.9 = (bf16[128,3200]{1,0:T(8,128)(2,1)S(1)}, bf16[128,3200]{1,0:T(8,128)(2,1)S(1)}, u32[]{:S(2)}, u32[]{:S(2)}) collective-permute-start(bf16[128,3200]{1,0:T(8,128)(2,1)S(1)} %bitcast.96), channel_id=1, source_target_pairs={{0,64},{64,0},{1,65},{65,1},{2,66},{66,2},{3,67},{67,3},{4,68},{68... | collective-permute-start | bytes 2457608 | tf_op jit(solution)/shard_map/ppermute | solution.py:37
  40.0 0.6 fusion.44
  40.6 0.7 collective-permute-start.8
  41.3 1.7 %collective-permute-done.5 = bf16[2,32,3200]{2,1,0:T(8,128)(2,1)S(1)} collective-permute-done((bf16[2,32,3200]{2,1,0:T(8,128)(2,1)S(1)}, bf16[2,32,3200]{2,1,0:T(8,128)(2,1)S(1)}, u32[]{:S(2)}, u32[]{:S(2)}) %collective-permute-start.5) | collective-permute-done | bytes 409632 | tf_op jit(solution)/shard_map/ppermute | solution.py:33
  43.2 0.6 fusion.40
  43.8 0.6 fusion.42
  44.4 3.2 %collective-permute-start.10 = (bf16[128,3200]{1,0:T(8,128)(2,1)S(1)}, bf16[128,3200]{1,0:T(8,128)(2,1)S(1)}, u32[]{:S(2)}, u32[]{:S(2)}) collective-permute-start(bf16[128,3200]{1,0:T(8,128)(2,1)S(1)} %bitcast.103), channel_id=1, source_target_pairs={{0,64},{64,0},{1,65},{65,1},{2,66},{66,2},{3,67},{67,3},{4,68},{68... | collective-permute-start | bytes 2457608 | tf_op jit(solution)/shard_map/ppermute | solution.py:37
  47.8 3.6 %collective-permute-done.7 = bf16[2,32,3200]{2,1,0:T(8,128)(2,1)S(1)} collective-permute-done((bf16[2,32,3200]{2,1,0:T(8,128)(2,1)S(1)}, bf16[2,32,3200]{2,1,0:T(8,128)(2,1)S(1)}, u32[]{:S(2)}, u32[]{:S(2)}) %collective-permute-start.7) | collective-permute-done | bytes 409632 | tf_op jit(solution)/shard_map/ppermute | solution.py:33
  51.4 3.9 %collective-permute-start.12 = (bf16[128,3200]{1,0:T(8,128)(2,1)S(1)}, bf16[128,3200]{1,0:T(8,128)(2,1)S(1)}, u32[]{:S(2)}, u32[]{:S(2)}) collective-permute-start(bf16[128,3200]{1,0:T(8,128)(2,1)S(1)} %bitcast.104), channel_id=1, source_target_pairs={{0,64},{64,0},{1,65},{65,1},{2,66},{66,2},{3,67},{67,3},{4,68},{68... | collective-permute-start | bytes 2457608 | tf_op jit(solution)/shard_map/ppermute | solution.py:37
  55.4 0.6 fusion.38
  56.0 0.6 fusion.36
  56.6 0.6 fusion.34
  57.2 0.6 fusion.32
  57.8 0.6 fusion.30
  59.4 0.4 fusion.1
  60.3 0.6 collective-permute-start.13
  61.4 0.4 fusion.3
  61.8 0.6 collective-permute-start.18
  62.4 0.4 add_convert_fusion.2
  62.9 0.8 collective-permute-start.21
  63.7 0.7 collective-permute-done.15
  64.5 0.4 add_convert_fusion.1
  65.0 0.8 collective-permute-start.16
  65.8 1.9 %collective-permute-start.22 = (bf16[2,32,3072]{2,1,0:T(8,128)(2,1)S(1)}, bf16[2,32,3072]{2,1,0:T(8,128)(2,1)S(1)}, u32[]{:S(2)}, u32[]{:S(2)}) collective-permute-start(bf16[2,32,3072]{2,1,0:T(8,128)(2,1)S(1)} %bitcast.121), channel_id=1, source_target_pairs={{0,48},{1,49},{2,50},{3,51},{4,52},{5,53},{6,54},{7,55},{16,0},{17... | collective-permute-start | bytes 1179656 | tf_op jit(solution)/shard_map/ppermute | solution.py:33
  67.7 0.4 add_convert_fusion
  68.3 0.4 add_convert_fusion.3
  68.8 6.5 %collective-permute-done.16 = bf16[2,32,3072]{2,1,0:T(8,128)(2,1)S(1)} collective-permute-done((bf16[2,32,3072]{2,1,0:T(8,128)(2,1)S(1)}, bf16[2,32,3072]{2,1,0:T(8,128)(2,1)S(1)}, u32[]{:S(2)}, u32[]{:S(2)}) %collective-permute-start.16) | collective-permute-done | bytes 393248 | tf_op jit(solution)/shard_map/ppermute | solution.py:33
  75.8 2.7 %collective-permute-start.23 = (bf16[2,32,3072]{2,1,0:T(8,128)(2,1)S(1)}, bf16[2,32,3072]{2,1,0:T(8,128)(2,1)S(1)}, u32[]{:S(2)}, u32[]{:S(2)}) collective-permute-start(bf16[2,32,3072]{2,1,0:T(8,128)(2,1)S(1)} %fusion.46), channel_id=1, source_target_pairs={{0,48},{1,49},{2,50},{3,51},{4,52},{5,53},{6,54},{7,55},{16,0},{17... | collective-permute-start | bytes 1179656 | tf_op jit(solution)/shard_map/ppermute | solution.py:33
  78.6 5.3 %collective-permute-done.17 = bf16[2,32,3072]{2,1,0:T(8,128)(2,1)S(1)} collective-permute-done((bf16[2,32,3072]{2,1,0:T(8,128)(2,1)S(1)}, bf16[2,32,3072]{2,1,0:T(8,128)(2,1)S(1)}, u32[]{:S(2)}, u32[]{:S(2)}) %collective-permute-start.17) | collective-permute-done | bytes 393248 | tf_op jit(solution)/shard_map/ppermute | solution.py:33
  84.3 1.6 %collective-permute-start.24 = (bf16[32,3072]{1,0:T(8,128)(2,1)S(1)}, bf16[32,3072]{1,0:T(8,128)(2,1)S(1)}, u32[]{:S(2)}, u32[]{:S(2)}) collective-permute-start(bf16[32,3072]{1,0:T(8,128)(2,1)S(1)} %get-tuple-element.23), channel_id=1, source_target_pairs={{0,8},{1,9},{2,10},{3,11},{4,12},{5,13},{6,14},{7,15},{16,24},{17,... | collective-permute-start | bytes 589832 | tf_op jit(solution)/shard_map/ppermute | solution.py:33
  85.9 1.3 %collective-permute-start.25 = (bf16[32,3072]{1,0:T(8,128)(2,1)S(1)}, bf16[32,3072]{1,0:T(8,128)(2,1)S(1)}, u32[]{:S(2)}, u32[]{:S(2)}) collective-permute-start(bf16[32,3072]{1,0:T(8,128)(2,1)S(1)} %get-tuple-element.24), channel_id=1, source_target_pairs={{0,136},{1,137},{2,138},{3,139},{4,140},{5,141},{6,142},{7,143},{1... | collective-permute-start | bytes 589832 | tf_op jit(solution)/shard_map/ppermute | solution.py:33
  87.1 5.1 %collective-permute-done.20 = bf16[32,3072]{1,0:T(8,128)(2,1)S(1)} collective-permute-done((bf16[32,3072]{1,0:T(8,128)(2,1)S(1)}, bf16[32,3072]{1,0:T(8,128)(2,1)S(1)}, u32[]{:S(2)}, u32[]{:S(2)}) %collective-permute-start.20) | collective-permute-done | bytes 196640 | tf_op jit(solution)/shard_map/ppermute | solution.py:33
  92.2 0.9 collective-permute-done.25
  93.3 14.9 %all_to_all.10 = bf16[16,2,3072]{2,1,0:T(2,128)(2,1)S(1)} all-to-all(bf16[16,2,3072]{2,1,0:T(2,128)(2,1)S(1)} %reshape.97), channel_id=1, replica_groups=mesh['xl'=2,'c'=2,'y'=4,'xh'=2,'z'=8] {'c','z'}, dimensions={0} | all-to-all | bytes 393216 | tf_op jit(solution)/shard_map/all_to_all | solution.py:180
  108.4 0.6 pad_maximum_fusion.7
  (79 shorter events, 4.6 us)
Async XLA Ops:
  0.0 59.4 %copy-start = (bf16[1,256,6144]{2,1,0:T(8,128)(2,1)S(1)}, bf16[1,256,6144]{2,1,0:T(8,128)(2,1)}, u32[]{:S(2)}) copy-start(bf16[1,256,6144]{2,1,0:T(8,128)(2,1)} %param.11) | copy-start | bytes 9437188
  1.6 18.4 %all-to-all-start = ((bf16[16,2,3200]{2,1,0:T(2,128)(2,1)}), bf16[16,2,3200]{2,1,0:T(2,128)(2,1)S(1)}, u32[]{:S(2)}, u32[]{:S(2)}) async-start(bf16[16,2,3200]{2,1,0:T(2,128)(2,1)} %prepare.1), calls=%async_computation | async-start | bytes 409600 | tf_op jit(solution)/shard_map/all_to_all | solution.py:118
  20.1 6.5 %collective-permute-start.2 = (bf16[32,3200]{1,0:T(8,128)(2,1)S(1)}, bf16[32,3200]{1,0:T(8,128)(2,1)S(1)}, u32[]{:S(2)}, u32[]{:S(2)}) collective-permute-start(bf16[32,3200]{1,0:T(8,128)(2,1)S(1)} %reshape.89), channel_id=1, source_target_pairs={{0,8},{1,9},{2,10},{3,11},{4,12},{5,13},{6,14},{7,15},{16,24},{17,... | collective-permute-start | bytes 614408 | tf_op jit(solution)/shard_map/ppermute | solution.py:33
  23.1 6.2 %collective-permute-start.1 = (bf16[32,3200]{1,0:T(8,128)(2,1)S(1)}, bf16[32,3200]{1,0:T(8,128)(2,1)}, u32[]{:S(2)}, u32[]{:S(2)}) collective-permute-start(bf16[32,3200]{1,0:T(8,128)(2,1)S(1)} %reshape.89), channel_id=1, source_target_pairs={{0,128},{1,129},{2,130},{3,131},{4,132},{5,133},{6,134},{7,135},{1... | collective-permute-start | bytes 614408 | tf_op jit(solution)/shard_map/ppermute | solution.py:33
  23.5 16.6 %copy-start.2 = (bf16[3072,512]{1,0:T(8,128)(2,1)S(1)}, bf16[3072,512]{1,0:T(8,128)(2,1)}, u32[]{:S(2)}) copy-start(bf16[3072,512]{1,0:T(8,128)(2,1)} %get-tuple-element.9) | copy-start | bytes 9437188
  23.5 9.5 %collective-permute-start = (bf16[32,3200]{1,0:T(8,128)(2,1)S(1)}, bf16[32,3200]{1,0:T(8,128)(2,1)S(1)}, u32[]{:S(2)}, u32[]{:S(2)}) collective-permute-start(bf16[32,3200]{1,0:T(8,128)(2,1)S(1)} %reshape.89), channel_id=1, source_target_pairs={{0,136},{1,137},{2,138},{3,139},{4,140},{5,141},{6,142},{7,143},{1... | collective-permute-start | bytes 614408 | tf_op jit(solution)/shard_map/ppermute | solution.py:33
  30.3 12.8 %collective-permute-start.6 = (bf16[2,32,3200]{2,1,0:T(8,128)(2,1)S(1)}, bf16[2,32,3200]{2,1,0:T(8,128)(2,1)S(1)}, u32[]{:S(2)}, u32[]{:S(2)}) collective-permute-start(bf16[2,32,3200]{2,1,0:T(8,128)(2,1)S(1)} %pad_maximum_fusion.6), channel_id=1, source_target_pairs={{0,16},{1,17},{2,18},{3,19},{4,20},{5,21},{6,22},{7,23},{16,32},{1... | collective-permute-start | bytes 1228808 | tf_op jit(solution)/shard_map/ppermute | solution.py:33
  31.3 9.3 %collective-permute-start.4 = (bf16[2,32,3200]{2,1,0:T(8,128)(2,1)S(1)}, bf16[2,32,3200]{2,1,0:T(8,128)(2,1)S(1)}, u32[]{:S(2)}, u32[]{:S(2)}) collective-permute-start(bf16[2,32,3200]{2,1,0:T(8,128)(2,1)S(1)} %pad_maximum_fusion.6), channel_id=1, source_target_pairs={{0,48},{1,49},{2,50},{3,51},{4,52},{5,53},{6,54},{7,55},{16,0},{17... | collective-permute-start | bytes 1228808 | tf_op jit(solution)/shard_map/ppermute | solution.py:33
  33.1 10.0 %collective-permute-start.5 = (bf16[2,32,3200]{2,1,0:T(8,128)(2,1)S(1)}, bf16[2,32,3200]{2,1,0:T(8,128)(2,1)S(1)}, u32[]{:S(2)}, u32[]{:S(2)}) collective-permute-start(bf16[2,32,3200]{2,1,0:T(8,128)(2,1)S(1)} %pad_maximum_fusion.5), channel_id=1, source_target_pairs={{0,16},{1,17},{2,18},{3,19},{4,20},{5,21},{6,22},{7,23},{16,32},{1... | collective-permute-start | bytes 1228808 | tf_op jit(solution)/shard_map/ppermute | solution.py:33
  34.2 8.9 %collective-permute-start.3 = (bf16[2,32,3200]{2,1,0:T(8,128)(2,1)S(1)}, bf16[2,32,3200]{2,1,0:T(8,128)(2,1)S(1)}, u32[]{:S(2)}, u32[]{:S(2)}) collective-permute-start(bf16[2,32,3200]{2,1,0:T(8,128)(2,1)S(1)} %pad_maximum_fusion.5), channel_id=1, source_target_pairs={{0,48},{1,49},{2,50},{3,51},{4,52},{5,53},{6,54},{7,55},{16,0},{17... | collective-permute-start | bytes 1228808 | tf_op jit(solution)/shard_map/ppermute | solution.py:33
  37.0 19.0 %collective-permute-start.9 = (bf16[128,3200]{1,0:T(8,128)(2,1)S(1)}, bf16[128,3200]{1,0:T(8,128)(2,1)S(1)}, u32[]{:S(2)}, u32[]{:S(2)}) collective-permute-start(bf16[128,3200]{1,0:T(8,128)(2,1)S(1)} %bitcast.96), channel_id=1, source_target_pairs={{0,64},{64,0},{1,65},{65,1},{2,66},{66,2},{3,67},{67,3},{4,68},{68... | collective-permute-start | bytes 2457608 | tf_op jit(solution)/shard_map/ppermute | solution.py:37
  40.6 7.2 %collective-permute-start.8 = (bf16[2,32,3200]{2,1,0:T(8,128)(2,1)S(1)}, bf16[2,32,3200]{2,1,0:T(8,128)(2,1)S(1)}, u32[]{:S(2)}, u32[]{:S(2)}) collective-permute-start(bf16[2,32,3200]{2,1,0:T(8,128)(2,1)S(1)} %collective-permute-done.4), channel_id=1, source_target_pairs={{0,48},{1,49},{2,50},{3,51},{4,52},{5,53},{6,54},{7,55},{16,0},{17... | collective-permute-start | bytes 1228808 | tf_op jit(solution)/shard_map/ppermute | solution.py:33
  43.0 8.3 %collective-permute-start.7 = (bf16[2,32,3200]{2,1,0:T(8,128)(2,1)S(1)}, bf16[2,32,3200]{2,1,0:T(8,128)(2,1)S(1)}, u32[]{:S(2)}, u32[]{:S(2)}) collective-permute-start(bf16[2,32,3200]{2,1,0:T(8,128)(2,1)S(1)} %collective-permute-done.5), channel_id=1, source_target_pairs={{0,16},{1,17},{2,18},{3,19},{4,20},{5,21},{6,22},{7,23},{16,32},{1... | collective-permute-start | bytes 1228808 | tf_op jit(solution)/shard_map/ppermute | solution.py:33
  44.4 11.5 %copy-start.1 = (bf16[3072,512]{1,0:T(8,128)(2,1)S(1)}, bf16[3072,512]{1,0:T(8,128)(2,1)}, u32[]{:S(2)}) copy-start(bf16[3072,512]{1,0:T(8,128)(2,1)} %get-tuple-element.10) | copy-start | bytes 9437188
  44.4 12.1 %collective-permute-start.10 = (bf16[128,3200]{1,0:T(8,128)(2,1)S(1)}, bf16[128,3200]{1,0:T(8,128)(2,1)S(1)}, u32[]{:S(2)}, u32[]{:S(2)}) collective-permute-start(bf16[128,3200]{1,0:T(8,128)(2,1)S(1)} %bitcast.103), channel_id=1, source_target_pairs={{0,64},{64,0},{1,65},{65,1},{2,66},{66,2},{3,67},{67,3},{4,68},{68... | collective-permute-start | bytes 2457608 | tf_op jit(solution)/shard_map/ppermute | solution.py:37
  47.7 8.9 %collective-permute-start.11 = (bf16[128,3200]{1,0:T(8,128)(2,1)S(1)}, bf16[128,3200]{1,0:T(8,128)(2,1)S(1)}, u32[]{:S(2)}, u32[]{:S(2)}) collective-permute-start(bf16[128,3200]{1,0:T(8,128)(2,1)S(1)} %bitcast.100), channel_id=1, source_target_pairs={{0,64},{64,0},{1,65},{65,1},{2,66},{66,2},{3,67},{67,3},{4,68},{68... | collective-permute-start | bytes 2457608 | tf_op jit(solution)/shard_map/ppermute | solution.py:37
  51.4 6.3 %collective-permute-start.12 = (bf16[128,3200]{1,0:T(8,128)(2,1)S(1)}, bf16[128,3200]{1,0:T(8,128)(2,1)S(1)}, u32[]{:S(2)}, u32[]{:S(2)}) collective-permute-start(bf16[128,3200]{1,0:T(8,128)(2,1)S(1)} %bitcast.104), channel_id=1, source_target_pairs={{0,64},{64,0},{1,65},{65,1},{2,66},{66,2},{3,67},{67,3},{4,68},{68... | collective-permute-start | bytes 2457608 | tf_op jit(solution)/shard_map/ppermute | solution.py:37
  56.0 1.2 %copy-start.3 = (bf16[128,3200]{1,0:T(8,128)(2,1)}, bf16[128,3200]{1,0:T(8,128)(2,1)S(1)}, u32[]{:S(2)}) copy-start(bf16[128,3200]{1,0:T(8,128)(2,1)S(1)} %collective-permute-done.9) | copy-start | bytes 2457604
  56.6 1.2 %copy-start.4 = (bf16[128,3200]{1,0:T(8,128)(2,1)}, bf16[128,3200]{1,0:T(8,128)(2,1)S(1)}, u32[]{:S(2)}) copy-start(bf16[128,3200]{1,0:T(8,128)(2,1)S(1)} %collective-permute-done.10) | copy-start | bytes 2457604
  56.6 1.2 %copy-start.5 = (bf16[128,3200]{1,0:T(8,128)(2,1)}, bf16[128,3200]{1,0:T(8,128)(2,1)S(1)}, u32[]{:S(2)}) copy-start(bf16[128,3200]{1,0:T(8,128)(2,1)S(1)} %collective-permute-done.11) | copy-start | bytes 2457604
  58.4 0.8 slice-start
  58.5 0.8 slice-start.1
  58.5 0.8 slice-start.2
  59.9 2.6 %collective-permute-start.14 = (bf16[128,3072]{1,0:T(8,128)(2,1)S(1)}, bf16[128,3072]{1,0:T(8,128)(2,1)S(1)}, u32[]{:S(2)}, u32[]{:S(2)}) collective-permute-start(bf16[128,3072]{1,0:T(8,128)(2,1)S(1)} %fusion.1), channel_id=1, source_target_pairs={{0,64},{64,0},{1,65},{65,1},{2,66},{66,2},{3,67},{67,3},{4,68},{68... | collective-permute-start | bytes 2359304 | tf_op jit(solution)/shard_map/ppermute | solution.py:37
  60.3 7.9 %collective-permute-start.13 = (bf16[128,3072]{1,0:T(8,128)(2,1)S(1)}, bf16[128,3072]{1,0:T(8,128)(2,1)S(1)}, u32[]{:S(2)}, u32[]{:S(2)}) collective-permute-start(bf16[128,3072]{1,0:T(8,128)(2,1)S(1)} %fusion), channel_id=1, source_target_pairs={{0,64},{64,0},{1,65},{65,1},{2,66},{66,2},{3,67},{67,3},{4,68},{68... | collective-permute-start | bytes 2359304 | tf_op jit(solution)/shard_map/ppermute | solution.py:37
  61.3 3.2 %collective-permute-start.15 = (bf16[128,3072]{1,0:T(8,128)(2,1)S(1)}, bf16[128,3072]{1,0:T(8,128)(2,1)S(1)}, u32[]{:S(2)}, u32[]{:S(2)}) collective-permute-start(bf16[128,3072]{1,0:T(8,128)(2,1)S(1)} %fusion.2), channel_id=1, source_target_pairs={{0,64},{64,0},{1,65},{65,1},{2,66},{66,2},{3,67},{67,3},{4,68},{68... | collective-permute-start | bytes 2359304 | tf_op jit(solution)/shard_map/ppermute | solution.py:37
  61.8 5.9 %collective-permute-start.18 = (bf16[128,3072]{1,0:T(8,128)(2,1)S(1)}, bf16[128,3072]{1,0:T(8,128)(2,1)S(1)}, u32[]{:S(2)}, u32[]{:S(2)}) collective-permute-start(bf16[128,3072]{1,0:T(8,128)(2,1)S(1)} %fusion.3), channel_id=1, source_target_pairs={{0,64},{64,0},{1,65},{65,1},{2,66},{66,2},{3,67},{67,3},{4,68},{68... | collective-permute-start | bytes 2359304 | tf_op jit(solution)/shard_map/ppermute | solution.py:37
  62.9 21.2 %collective-permute-start.21 = (bf16[2,32,3072]{2,1,0:T(8,128)(2,1)S(1)}, bf16[2,32,3072]{2,1,0:T(8,128)(2,1)S(1)}, u32[]{:S(2)}, u32[]{:S(2)}) collective-permute-start(bf16[2,32,3072]{2,1,0:T(8,128)(2,1)S(1)} %bitcast.120), channel_id=1, source_target_pairs={{0,16},{1,17},{2,18},{3,19},{4,20},{5,21},{6,22},{7,23},{16,32},{1... | collective-permute-start | bytes 1179656 | tf_op jit(solution)/shard_map/ppermute | solution.py:33
  65.0 10.4 %collective-permute-start.16 = (bf16[2,32,3072]{2,1,0:T(8,128)(2,1)S(1)}, bf16[2,32,3072]{2,1,0:T(8,128)(2,1)S(1)}, u32[]{:S(2)}, u32[]{:S(2)}) collective-permute-start(bf16[2,32,3072]{2,1,0:T(8,128)(2,1)S(1)} %bitcast.123), channel_id=1, source_target_pairs={{0,16},{1,17},{2,18},{3,19},{4,20},{5,21},{6,22},{7,23},{16,32},{1... | collective-permute-start | bytes 1179656 | tf_op jit(solution)/shard_map/ppermute | solution.py:33
  65.8 9.9 %collective-permute-start.22 = (bf16[2,32,3072]{2,1,0:T(8,128)(2,1)S(1)}, bf16[2,32,3072]{2,1,0:T(8,128)(2,1)S(1)}, u32[]{:S(2)}, u32[]{:S(2)}) collective-permute-start(bf16[2,32,3072]{2,1,0:T(8,128)(2,1)S(1)} %bitcast.121), channel_id=1, source_target_pairs={{0,48},{1,49},{2,50},{3,51},{4,52},{5,53},{6,54},{7,55},{16,0},{17... | collective-permute-start | bytes 1179656 | tf_op jit(solution)/shard_map/ppermute | solution.py:33
  68.2 10.4 %collective-permute-start.19 = (bf16[2,32,3072]{2,1,0:T(8,128)(2,1)S(1)}, bf16[2,32,3072]{2,1,0:T(8,128)(2,1)S(1)}, u32[]{:S(2)}, u32[]{:S(2)}) collective-permute-start(bf16[2,32,3072]{2,1,0:T(8,128)(2,1)S(1)} %bitcast.122), channel_id=1, source_target_pairs={{0,48},{1,49},{2,50},{3,51},{4,52},{5,53},{6,54},{7,55},{16,0},{17... | collective-permute-start | bytes 1179656 | tf_op jit(solution)/shard_map/ppermute | solution.py:33
  75.4 8.4 %collective-permute-start.17 = (bf16[2,32,3072]{2,1,0:T(8,128)(2,1)S(1)}, bf16[2,32,3072]{2,1,0:T(8,128)(2,1)S(1)}, u32[]{:S(2)}, u32[]{:S(2)}) collective-permute-start(bf16[2,32,3072]{2,1,0:T(8,128)(2,1)S(1)} %fusion.49), channel_id=1, source_target_pairs={{0,16},{1,17},{2,18},{3,19},{4,20},{5,21},{6,22},{7,23},{16,32},{1... | collective-permute-start | bytes 1179656 | tf_op jit(solution)/shard_map/ppermute | solution.py:33
  75.8 8.3 %collective-permute-start.23 = (bf16[2,32,3072]{2,1,0:T(8,128)(2,1)S(1)}, bf16[2,32,3072]{2,1,0:T(8,128)(2,1)S(1)}, u32[]{:S(2)}, u32[]{:S(2)}) collective-permute-start(bf16[2,32,3072]{2,1,0:T(8,128)(2,1)S(1)} %fusion.46), channel_id=1, source_target_pairs={{0,48},{1,49},{2,50},{3,51},{4,52},{5,53},{6,54},{7,55},{16,0},{17... | collective-permute-start | bytes 1179656 | tf_op jit(solution)/shard_map/ppermute | solution.py:33
  84.0 8.2 %collective-permute-start.20 = (bf16[32,3072]{1,0:T(8,128)(2,1)S(1)}, bf16[32,3072]{1,0:T(8,128)(2,1)S(1)}, u32[]{:S(2)}, u32[]{:S(2)}) collective-permute-start(bf16[32,3072]{1,0:T(8,128)(2,1)S(1)} %fusion.56), channel_id=1, source_target_pairs={{0,128},{1,129},{2,130},{3,131},{4,132},{5,133},{6,134},{7,135},{1... | collective-permute-start | bytes 589832 | tf_op jit(solution)/shard_map/ppermute | solution.py:33
  84.3 7.9 %collective-permute-start.24 = (bf16[32,3072]{1,0:T(8,128)(2,1)S(1)}, bf16[32,3072]{1,0:T(8,128)(2,1)S(1)}, u32[]{:S(2)}, u32[]{:S(2)}) collective-permute-start(bf16[32,3072]{1,0:T(8,128)(2,1)S(1)} %get-tuple-element.23), channel_id=1, source_target_pairs={{0,8},{1,9},{2,10},{3,11},{4,12},{5,13},{6,14},{7,15},{16,24},{17,... | collective-permute-start | bytes 589832 | tf_op jit(solution)/shard_map/ppermute | solution.py:33
  85.9 7.3 %collective-permute-start.25 = (bf16[32,3072]{1,0:T(8,128)(2,1)S(1)}, bf16[32,3072]{1,0:T(8,128)(2,1)S(1)}, u32[]{:S(2)}, u32[]{:S(2)}) collective-permute-start(bf16[32,3072]{1,0:T(8,128)(2,1)S(1)} %get-tuple-element.24), channel_id=1, source_target_pairs={{0,136},{1,137},{2,138},{3,139},{4,140},{5,141},{6,142},{7,143},{1... | collective-permute-start | bytes 589832 | tf_op jit(solution)/shard_map/ppermute | solution.py:33
